TPU v7x, 32 devices: a whole 2x2x4 slice. The times are simulated.
32 devices in a mesh: groups: 2 (over x), frame: 16 (over z, y, core).
Axes of the slice: x: 2, y: 2, z: 4, core: 2. Of those that a mesh axis runs over, the one named last changes fastest.
Arguments:
- query_rows: bfloat16 [8192, 2560], P(('groups', 'frame')), parts along dimension 0, may hold values from -60 to 60
- key_rows: bfloat16 [8192, 2560], P(('groups', 'frame')), parts along dimension 0, may hold values from -4 to 4
- value_rows: bfloat16 [8192, 2560], P(('groups', 'frame')), parts along dimension 0, may hold values from -6 to 6
- tile_mask: int32 [128, 27], P(('groups', 'frame')), parts along dimension 0, may hold values from 0 to 1, as said below
- head_weight: bfloat16 [2560, 64], replicated, may hold values from -0.125 to 0.125
- latent: float32 [8192, 64], P(('groups', 'frame')), parts along dimension 0, may hold values from -6 to 6
- step_index: int32 [2], P('groups'), parts along dimension 0, may hold values from 0 to 24
Outputs:
- guided: float32 [8192, 64], P(('groups', 'frame')), parts along dimension 0
- clean: float32 [8192, 64], P(('groups', 'frame')), parts along dimension 0
- latent_next: float32 [8192, 64], P(('groups', 'frame')), parts along dimension 0
There are 2 independent parts, one for each index of `groups`. A program takes and returns all parts, laid end to end along the dimension named above; an argument that names none is the same for every part. Nothing has to cross between parts.
Inputs may be any that keep to these rules, and one draw needn't show every extreme that they name: `tile_mask`: entries are 0 or 1; entry 13 (the query tile itself) is always 1.
All inputs are finite; a program needn't handle non-finite values.
Results may differ from a plain program's by a relative error of at most 0.0041.
Values may be sent and summed in bfloat16 or wider, within the bound.
No kernel may reach another device: no remote copies, remote signals or barrier semaphores. Data moves between devices by JAX's collectives and lax.ppermute only.
A program may use at most 128 MiB of HBM per device.

v0:
```python
import math

import jax
import jax.numpy as jnp
from jax import lax
from jax.sharding import PartitionSpec as P

HEADS = 20
HD = 128
SH = 4
SW = 8
SAMPLE_STEPS = 50


GUIDANCE = 5.0
FLOW_SHIFT = 5.0


def passed_along(value, axis, steps):
    count = lax.axis_size(axis)
    pairs = [(source, (source + steps) % count) for source in range(count)]
    return lax.ppermute(value, axis, pairs)


def flow_sigma(moment):
    remain = 1.0 - moment / SAMPLE_STEPS
    return FLOW_SHIFT * remain / (1.0 + (FLOW_SHIFT - 1.0) * remain)


def edge_range(offset):
    if offset < 0:
        return (1, 2)
    if offset > 0:
        return (0, 1)
    return (0, 2)


def direct_window(stacked, block_count, block_cols):
    received_parts = {}
    for frame_step in (1, 0, -1):
        for row_step in (1, 0, -1):
            for col_step in (1, 0, -1):
                distance = frame_step * block_count + row_step * block_cols + col_step
                row_start, row_stop = edge_range(row_step)
                col_start, col_stop = edge_range(col_step)
                outgoing = stacked[row_start:row_stop, col_start:col_stop]
                if frame_step == 0 and row_step == 0 and (col_step == 0):
                    received = outgoing
                elif row_step == 0 and col_step == 0:
                    received = passed_along(outgoing, "frame", -distance)
                elif row_step != 0 and col_step != 0:
                    received = passed_along(outgoing, "frame", -distance)
                else:
                    received = passed_along(outgoing, "frame", -distance)
                received_parts[frame_step, row_step, col_step] = received
    planes = []
    for frame_step in (-1, 0, 1):
        row_parts = []
        for row_step in (-1, 0, 1):
            col_parts = [received_parts[frame_step, row_step, col_step] for col_step in (-1, 0, 1)]
            row_parts.append(jnp.concatenate(col_parts, axis=1))
        planes.append(jnp.concatenate(row_parts, axis=0))
    return planes


def window_allowed(tile_mask, frame_tile, block_row, block_col, tile_frames):
    offsets = jnp.arange(27, dtype=jnp.int32)
    frame_step = offsets // 9 - 1
    row_step = offsets // 3 % 3 - 1
    col_step = offsets % 3 - 1
    local_tile = jnp.arange(4, dtype=jnp.int32)
    tile_row = 2 * block_row + local_tile // 2
    tile_col = 2 * block_col + local_tile % 2
    frame_there = frame_tile + frame_step
    row_there = tile_row[:, None] + row_step[None, :]
    col_there = tile_col[:, None] + col_step[None, :]
    usable = ((frame_there >= 0) & (frame_there < tile_frames))[None, :]
    usable = usable & (row_there >= 0) & (row_there < SH) & (col_there >= 0) & (col_there < SW)
    return usable & (tile_mask > 0)


def attend_window(query_rows, planes, allowed):
    tok_rows, inner_width = query_rows.shape
    tile_tok = tok_rows // 4
    query_tiles = query_rows.reshape(4, tile_tok, inner_width)
    mask_full = allowed[:, None, :, None]

    def one_head(head_number, result_rows):
        key_planes = [lax.dynamic_slice_in_dim(plane, head_number * HD, HD, 3) for plane in planes]
        value_planes = [
            lax.dynamic_slice_in_dim(plane, inner_width + head_number * HD, HD, 3)
            for plane in planes
        ]
        key_list = []
        value_list = []
        for row_local in range(2):
            for col_local in range(2):
                key_list.append(
                    jnp.stack(
                        [
                            part[row_local : row_local + 3, col_local : col_local + 3]
                            for part in key_planes
                        ]
                    ).reshape(27 * tile_tok, HD)
                )
                value_list.append(
                    jnp.stack(
                        [
                            part[row_local : row_local + 3, col_local : col_local + 3]
                            for part in value_planes
                        ]
                    ).reshape(27 * tile_tok, HD)
                )
        key_tiles = jnp.stack(key_list)
        value_tiles = jnp.stack(value_list)
        head_query = lax.dynamic_slice_in_dim(query_tiles, head_number * HD, HD, 2)
        scores = jnp.einsum(
            "qtd,qkd->qtk", head_query, key_tiles, preferred_element_type=jnp.float32
        ) / math.sqrt(HD)
        scores = scores.reshape(4, tile_tok, 27, tile_tok)
        scores = jnp.where(mask_full, scores, -1e30)
        row_max = jnp.max(scores, axis=(2, 3), keepdims=True)
        shifted = jnp.where(mask_full, jnp.exp(scores - row_max), 0.0)
        weights = (shifted / jnp.sum(shifted, axis=(2, 3), keepdims=True)).astype(jnp.bfloat16)
        weights = weights.reshape(4, tile_tok, 27 * tile_tok)
        head_out = jnp.einsum(
            "qtk,qkd->qtd", weights, value_tiles, preferred_element_type=jnp.float32
        ).astype(jnp.bfloat16)
        return lax.dynamic_update_slice_in_dim(result_rows, head_out, head_number * HD, 2)

    result_rows = lax.fori_loop(
        0, HEADS, one_head, jnp.zeros((4, tile_tok, inner_width), jnp.bfloat16)
    )
    return result_rows.reshape(tok_rows, inner_width)


def per_device(query_rows, key_rows, value_rows, tile_mask, head_weight, latent, step_index):
    frame_count = lax.axis_size("frame")
    frame_index = lax.axis_index("frame")
    half_size = frame_count // 2
    block_cols = SW // 2
    block_count = SH // 2 * block_cols
    tile_frames = frame_count // (2 * block_count)
    frame_tile = frame_index // block_count % tile_frames
    block_spot = frame_index % block_count
    block_row = block_spot // block_cols
    block_col = block_spot % block_cols
    tok_rows, inner_width = query_rows.shape
    tile_tok = tok_rows // 4
    stacked = jnp.concatenate([key_rows, value_rows], axis=1).reshape(
        2, 2, tile_tok, 2 * inner_width
    )
    planes = direct_window(stacked, block_count, block_cols)
    allowed = window_allowed(tile_mask, frame_tile, block_row, block_col, tile_frames)
    attention = attend_window(query_rows, planes, allowed)
    velocity = jnp.dot(attention, head_weight, preferred_element_type=jnp.float32)
    partner_rows = passed_along(velocity, "frame", half_size)
    is_cond = frame_index < half_size
    cond_rows = jnp.where(is_cond, velocity, partner_rows)
    uncond_rows = jnp.where(is_cond, partner_rows, velocity)
    guided = uncond_rows + GUIDANCE * (cond_rows - uncond_rows)
    moment = step_index[0].astype(jnp.float32)
    sigma_now = flow_sigma(moment)
    step_size = flow_sigma(moment + 1.0) - sigma_now
    clean = latent - sigma_now * guided
    latent_next = latent + step_size * guided
    return (guided, clean, latent_next)


def solution(mesh):
    placed = (
        P(("groups", "frame"), None),
        P(("groups", "frame"), None),
        P(("groups", "frame"), None),
        P(("groups", "frame"), None),
        P(),
        P(("groups", "frame"), None),
        P("groups"),
    )
    return jax.shard_map(
        per_device,
        mesh=mesh,
        in_specs=placed,
        out_specs=(
            P(("groups", "frame"), None),
            P(("groups", "frame"), None),
            P(("groups", "frame"), None),
        ),
        check_vma=False,
    )
```

profile of v0, /device:TPU:0, one launch (start us, length us, event | category | flops | bytes accessed | tf_op | source)
XLA Modules:
  0.0 654.4 jit_solution(14808526750160094436)
XLA Ops:
  6.1 3.5 collective-permute-start
  9.9 3.2 collective-permute-start.14
  14.9 38.2 %collective-permute-done.11 = bf16[1,1,64,5120]{3,2,1,0:T(8,128)(2,1)S(1)} collective-permute-done((bf16[1,1,64,5120]{3,2,1,0:T(8,128)(2,1)S(1)}, bf16[1,1,64,5120]{3,2,1,0:T(8,128)(2,1)S(1)}, u32[]{:S(2)}, u32[]{:S(2)}) %collective-permute-start.11) | collective-permute-done | bytes 655392 | tf_op jit(solution)/shard_map/ppermute | solution.py:22
  53.0 26.6 %collective-permute-start.6 = (bf16[1,1,64,5120]{3,2,1,0:T(8,128)(2,1)S(1)}, bf16[1,1,64,5120]{3,2,1,0:T(8,128)(2,1)}, u32[]{:S(2)}, u32[]{:S(2)}) collective-permute-start(bf16[1,1,64,5120]{3,2,1,0:T(8,128)(2,1)S(1)} %get-tuple-element.228), channel_id=1, source_target_pairs={{0,5},{1,6},{2,7},{3,8},{4,9},{5,10},{6,11},{7,12},{8,13},{9,14},{... | collective-permute-start | bytes 1966088 | tf_op jit(solution)/shard_map/ppermute | solution.py:22
  81.4 24.6 %collective-permute-done.16 = bf16[1,1,64,5120]{3,2,1,0:T(8,128)(2,1)S(1)} collective-permute-done((bf16[1,1,64,5120]{3,2,1,0:T(8,128)(2,1)}, bf16[1,1,64,5120]{3,2,1,0:T(8,128)(2,1)S(1)}, u32[]{:S(2)}, u32[]{:S(2)}) %collective-permute-start.16) | collective-permute-done | bytes 655392 | tf_op jit(solution)/shard_map/ppermute | solution.py:22
  106.8 3.2 collective-permute-start.12
  110.0 8.1 %collective-permute-start.13 = (bf16[2,1,64,5120]{3,2,1,0:T(8,128)(2,1)}, bf16[2,1,64,5120]{3,2,1,0:T(8,128)(2,1)}, u32[]{:S(2)}, u32[]{:S(2)}) collective-permute-start(bf16[2,1,64,5120]{3,2,1,0:T(8,128)(2,1)} %get-tuple-element.233), channel_id=1, source_target_pairs={{0,15},{1,0},{2,1},{3,2},{4,3},{5,4},{6,5},{7,6},{8,7},{9,8},{10,9... | collective-permute-start | bytes 3932168 | tf_op jit(solution)/shard_map/ppermute | solution.py:22
  123.5 61.3 %collective-permute-done.8 = bf16[1,1,64,5120]{3,2,1,0:T(8,128)(2,1)} collective-permute-done((bf16[1,1,64,5120]{3,2,1,0:T(8,128)(2,1)}, bf16[1,1,64,5120]{3,2,1,0:T(8,128)(2,1)}, u32[]{:S(2)}, u32[]{:S(2)}) %collective-permute-start.8) | collective-permute-done | bytes 655392 | tf_op jit(solution)/shard_map/ppermute | solution.py:22
  184.8 5.8 collective-permute-start.4
  190.8 7.0 %collective-permute-start.3 = (bf16[2,1,64,5120]{3,2,1,0:T(8,128)(2,1)}, bf16[2,1,64,5120]{3,2,1,0:T(8,128)(2,1)S(1)}, u32[]{:S(2)}, u32[]{:S(2)}) collective-permute-start(bf16[2,1,64,5120]{3,2,1,0:T(8,128)(2,1)} %get-tuple-element.232), channel_id=1, source_target_pairs={{0,9},{1,10},{2,11},{3,12},{4,13},{5,14},{6,15},{7,0},{8,1},{9,2},... | collective-permute-start | bytes 3932168 | tf_op jit(solution)/shard_map/ppermute | solution.py:22
  197.7 6.1 collective-permute-start.5
  203.9 4.4 collective-permute-start.1
  208.3 98.6 %collective-permute-start.7 = (bf16[1,2,64,5120]{3,2,1,0:T(8,128)(2,1)}, bf16[1,2,64,5120]{3,2,1,0:T(8,128)(2,1)S(1)}, u32[]{:S(2)}, u32[]{:S(2)}) collective-permute-start(bf16[1,2,64,5120]{3,2,1,0:T(8,128)(2,1)} %bitcast.29), channel_id=1, source_target_pairs={{0,4},{1,5},{2,6},{3,7},{4,8},{5,9},{6,10},{7,11},{8,12},{9,13},{1... | collective-permute-start | bytes 3932168 | tf_op jit(solution)/shard_map/ppermute | solution.py:22
  306.9 8.8 %maximum_maximum_fusion.1 = bf16[4,4,64,5120]{3,2,1,0:T(8,128)(2,1)} fusion(bf16[1,1,64,5120]{3,2,1,0:T(8,128)(2,1)} %copy-done.4, bf16[1,2,64,5120]{3,2,1,0:T(8,128)(2,1)} %collective-permute-done.15, bf16[1,1,64,5120]{3,2,1,0:T(8,128)(2,1)} %copy-done.3, bf16[2,1,64,5120]{3,2,1,0:T(8,128)(2,1)} %collective-permute-done.13, ...), kind=kLoop, calls=%fused_computation.53 | loop fusion | flops 41943040 | bytes 20971520 | tf_op jit(solution)/shard_map/concatenate | solution.py:62
  315.8 132.1 %collective-permute-done.5 = bf16[2,1,64,5120]{3,2,1,0:T(8,128)(2,1)S(1)} collective-permute-done((bf16[2,1,64,5120]{3,2,1,0:T(8,128)(2,1)}, bf16[2,1,64,5120]{3,2,1,0:T(8,128)(2,1)S(1)}, u32[]{:S(2)}, u32[]{:S(2)}) %collective-permute-start.5) | collective-permute-done | bytes 1310752 | tf_op jit(solution)/shard_map/ppermute | solution.py:22
  447.9 7.9 %maximum_maximum_fusion = bf16[4,4,64,5120]{3,2,1,0:T(8,128)(2,1)} fusion(bf16[1,1,64,5120]{3,2,1,0:T(8,128)(2,1)} %collective-permute-done.8, bf16[1,2,64,5120]{3,2,1,0:T(8,128)(2,1)S(1)} %collective-permute-done.7, bf16[1,1,64,5120]{3,2,1,0:T(8,128)(2,1)} %collective-permute-done.6, bf16[2,1,64,5120]{3,2,1,0:T(8,128)(2,1)S(1)} %collective-permute-done.5, ...), kind=kLoop, calls=%fused_computation.52 | loop fusion | flops 41943040 | bytes 20971520 | tf_op jit(solution)/shard_map/concatenate | solution.py:62
  456.9 172.1 %while.15 = (s32[]{:T(128)}, bf16[4,64,2560]{2,1,0:T(8,128)(2,1)}, pred[4,1,27,1]{2,0,3,1:T(4,128)(4,1)S(1)}, bf16[4,64,2560]{2,1,0:T(8,128)(2,1)}, bf16[4,4,64,...) while((s32[]{:T(128)}, bf16[4,64,2560]{2,1,0:T(8,128)(2,1)}, ...), condition=%wide.region_3.4_spmd, body=%wide.region_0.3_spmd.sunk | while | flops 238470848 | bytes 24941196 | solution.py:131
  459.7 3.1 fusion.61
  468.2 3.1 fusion.61
  485.5 3.1 fusion.61
  494.0 3.1 fusion.61
  511.4 3.1 fusion.61
  519.9 3.1 fusion.61
  528.5 3.1 fusion.61
  537.0 3.1 fusion.61
  545.7 3.1 fusion.61
  554.2 3.1 fusion.61
  571.6 3.1 fusion.61
  580.4 3.1 fusion.61
  588.9 3.1 fusion.61
  597.4 3.1 fusion.61
  630.8 18.5 %collective-permute-start.17 = (f32[256,64]{0,1:T(8,128)S(1)}, f32[256,64]{0,1:T(8,128)S(1)}, u32[]{:S(2)}, u32[]{:S(2)}) collective-permute-start(f32[256,64]{0,1:T(8,128)S(1)} %fusion.50), channel_id=1, source_target_pairs={{0,8},{1,9},{2,10},{3,11},{4,12},{5,13},{6,14},{7,15},{8,0},{9,1},... | collective-permute-start | bytes 196616 | tf_op jit(solution)/shard_map/ppermute | solution.py:22
  (336 shorter events, 149.7 us)
Async XLA Ops:
  0.6 628.4 %copy-start = (bf16[2560,64]{0,1:T(8,128)(2,1)S(1)}, bf16[2560,64]{0,1:T(8,128)(2,1)}, u32[]{:S(2)}) copy-start(bf16[2560,64]{0,1:T(8,128)(2,1)} %param.13) | copy-start | bytes 983044
  0.6 1.8 copy-start.1
  3.6 106.4 %collective-permute-start.9 = (bf16[1,1,64,5120]{3,2,1,0:T(8,128)(2,1)S(1)}, bf16[1,1,64,5120]{3,2,1,0:T(8,128)(2,1)}, u32[]{:S(2)}, u32[]{:S(2)}) collective-permute-start(bf16[1,1,64,5120]{3,2,1,0:T(8,128)(2,1)S(1)} %get-tuple-element.226), channel_id=1, source_target_pairs={{0,5},{1,6},{2,7},{3,8},{4,9},{5,10},{6,11},{7,12},{8,13},{9,14},{... | collective-permute-start | bytes 1966088 | tf_op jit(solution)/shard_map/ppermute | solution.py:22
  6.1 112.1 %collective-permute-start = (bf16[1,1,64,5120]{3,2,1,0:T(8,128)(2,1)S(1)}, bf16[1,1,64,5120]{3,2,1,0:T(8,128)(2,1)}, u32[]{:S(2)}, u32[]{:S(2)}) collective-permute-start(bf16[1,1,64,5120]{3,2,1,0:T(8,128)(2,1)S(1)} %get-tuple-element.226), channel_id=1, source_target_pairs={{0,13},{1,14},{2,15},{3,0},{4,1},{5,2},{6,3},{7,4},{8,5},{9,6},{10... | collective-permute-start | bytes 1966088 | tf_op jit(solution)/shard_map/ppermute | solution.py:22
  9.6 43.5 %collective-permute-start.11 = (bf16[1,1,64,5120]{3,2,1,0:T(8,128)(2,1)S(1)}, bf16[1,1,64,5120]{3,2,1,0:T(8,128)(2,1)S(1)}, u32[]{:S(2)}, u32[]{:S(2)}) collective-permute-start(bf16[1,1,64,5120]{3,2,1,0:T(8,128)(2,1)S(1)} %get-tuple-element.229), channel_id=1, source_target_pairs={{0,3},{1,4},{2,5},{3,6},{4,7},{5,8},{6,9},{7,10},{8,11},{9,12},{10... | collective-permute-start | bytes 1966088 | tf_op jit(solution)/shard_map/ppermute | solution.py:22
  9.6 111.5 %collective-permute-start.2 = (bf16[1,1,64,5120]{3,2,1,0:T(8,128)(2,1)S(1)}, bf16[1,1,64,5120]{3,2,1,0:T(8,128)(2,1)}, u32[]{:S(2)}, u32[]{:S(2)}) collective-permute-start(bf16[1,1,64,5120]{3,2,1,0:T(8,128)(2,1)S(1)} %get-tuple-element.229), channel_id=1, source_target_pairs={{0,11},{1,12},{2,13},{3,14},{4,15},{5,0},{6,1},{7,2},{8,3},{9,4},{... | collective-permute-start | bytes 1966088 | tf_op jit(solution)/shard_map/ppermute | solution.py:22
  9.9 69.7 %collective-permute-start.14 = (bf16[1,1,64,5120]{3,2,1,0:T(8,128)(2,1)S(1)}, bf16[1,1,64,5120]{3,2,1,0:T(8,128)(2,1)S(1)}, u32[]{:S(2)}, u32[]{:S(2)}) collective-permute-start(bf16[1,1,64,5120]{3,2,1,0:T(8,128)(2,1)S(1)} %get-tuple-element.228), channel_id=1, source_target_pairs={{0,13},{1,14},{2,15},{3,0},{4,1},{5,2},{6,3},{7,4},{8,5},{9,6},{10... | collective-permute-start | bytes 1966088 | tf_op jit(solution)/shard_map/ppermute | solution.py:22
  53.0 28.3 %copy-start.2 = (bf16[1,1,64,5120]{3,2,1,0:T(8,128)(2,1)}, bf16[1,1,64,5120]{3,2,1,0:T(8,128)(2,1)S(1)}, u32[]{:S(2)}) copy-start(bf16[1,1,64,5120]{3,2,1,0:T(8,128)(2,1)S(1)} %collective-permute-done.11) | copy-start | bytes 1966084
  53.0 69.0 %collective-permute-start.6 = (bf16[1,1,64,5120]{3,2,1,0:T(8,128)(2,1)S(1)}, bf16[1,1,64,5120]{3,2,1,0:T(8,128)(2,1)}, u32[]{:S(2)}, u32[]{:S(2)}) collective-permute-start(bf16[1,1,64,5120]{3,2,1,0:T(8,128)(2,1)S(1)} %get-tuple-element.228), channel_id=1, source_target_pairs={{0,5},{1,6},{2,7},{3,8},{4,9},{5,10},{6,11},{7,12},{8,13},{9,14},{... | collective-permute-start | bytes 1966088 | tf_op jit(solution)/shard_map/ppermute | solution.py:22
  79.6 1.7 copy-start.3
  79.6 111.0 %copy-start.7 = (s32[4,27]{1,0:T(4,128)S(1)}, s32[4,27]{1,0:T(4,128)}, u32[]{:S(2)}) copy-start(s32[4,27]{1,0:T(4,128)} %param.12) | copy-start | bytes 1300
  79.6 26.3 %collective-permute-start.16 = (bf16[1,1,64,5120]{3,2,1,0:T(8,128)(2,1)}, bf16[1,1,64,5120]{3,2,1,0:T(8,128)(2,1)S(1)}, u32[]{:S(2)}, u32[]{:S(2)}) collective-permute-start(bf16[1,1,64,5120]{3,2,1,0:T(8,128)(2,1)} %get-tuple-element.227), channel_id=1, source_target_pairs={{0,11},{1,12},{2,13},{3,14},{4,15},{5,0},{6,1},{7,2},{8,3},{9,4},{... | collective-permute-start | bytes 1966088 | tf_op jit(solution)/shard_map/ppermute | solution.py:22
  106.8 83.9 %collective-permute-start.12 = (bf16[2,1,64,5120]{3,2,1,0:T(8,128)(2,1)}, bf16[2,1,64,5120]{3,2,1,0:T(8,128)(2,1)}, u32[]{:S(2)}, u32[]{:S(2)}) collective-permute-start(bf16[2,1,64,5120]{3,2,1,0:T(8,128)(2,1)} %get-tuple-element.232), channel_id=1, source_target_pairs={{0,1},{1,2},{2,3},{3,4},{4,5},{5,6},{6,7},{7,8},{8,9},{9,10},{10,1... | collective-permute-start | bytes 3932168 | tf_op jit(solution)/shard_map/ppermute | solution.py:22
  110.0 87.7 %collective-permute-start.13 = (bf16[2,1,64,5120]{3,2,1,0:T(8,128)(2,1)}, bf16[2,1,64,5120]{3,2,1,0:T(8,128)(2,1)}, u32[]{:S(2)}, u32[]{:S(2)}) collective-permute-start(bf16[2,1,64,5120]{3,2,1,0:T(8,128)(2,1)} %get-tuple-element.233), channel_id=1, source_target_pairs={{0,15},{1,0},{2,1},{3,2},{4,3},{5,4},{6,5},{7,6},{8,7},{9,8},{10,9... | collective-permute-start | bytes 3932168 | tf_op jit(solution)/shard_map/ppermute | solution.py:22
  118.2 85.7 %collective-permute-start.10 = (bf16[1,2,64,5120]{3,2,1,0:T(8,128)(2,1)}, bf16[1,2,64,5120]{3,2,1,0:T(8,128)(2,1)}, u32[]{:S(2)}, u32[]{:S(2)}) collective-permute-start(bf16[1,2,64,5120]{3,2,1,0:T(8,128)(2,1)} %bitcast.28), channel_id=1, source_target_pairs={{0,4},{1,5},{2,6},{3,7},{4,8},{5,9},{6,10},{7,11},{8,12},{9,13},{1... | collective-permute-start | bytes 3932168 | tf_op jit(solution)/shard_map/ppermute | solution.py:22
  121.1 87.2 %collective-permute-start.15 = (bf16[1,2,64,5120]{3,2,1,0:T(8,128)(2,1)}, bf16[1,2,64,5120]{3,2,1,0:T(8,128)(2,1)}, u32[]{:S(2)}, u32[]{:S(2)}) collective-permute-start(bf16[1,2,64,5120]{3,2,1,0:T(8,128)(2,1)} %bitcast.29), channel_id=1, source_target_pairs={{0,12},{1,13},{2,14},{3,15},{4,0},{5,1},{6,2},{7,3},{8,4},{9,5},{1... | collective-permute-start | bytes 3932168 | tf_op jit(solution)/shard_map/ppermute | solution.py:22
  122.0 62.8 %collective-permute-start.8 = (bf16[1,1,64,5120]{3,2,1,0:T(8,128)(2,1)}, bf16[1,1,64,5120]{3,2,1,0:T(8,128)(2,1)}, u32[]{:S(2)}, u32[]{:S(2)}) collective-permute-start(bf16[1,1,64,5120]{3,2,1,0:T(8,128)(2,1)} %get-tuple-element.227), channel_id=1, source_target_pairs={{0,3},{1,4},{2,5},{3,6},{4,7},{5,8},{6,9},{7,10},{8,11},{9,12},{10... | collective-permute-start | bytes 1966088 | tf_op jit(solution)/shard_map/ppermute | solution.py:22
  184.8 263.0 %collective-permute-start.4 = (bf16[2,2,64,5120]{3,2,1,0:T(8,128)(2,1)S(1)}, bf16[2,2,64,5120]{3,2,1,0:T(8,128)(2,1)S(1)}, u32[]{:S(2)}, u32[]{:S(2)}) collective-permute-start(bf16[2,2,64,5120]{3,2,1,0:T(8,128)(2,1)S(1)} %bitcast.74), channel_id=1, source_target_pairs={{0,8},{1,9},{2,10},{3,11},{4,12},{5,13},{6,14},{7,15},{8,0},{9,1},... | collective-permute-start | bytes 7864328 | tf_op jit(solution)/shard_map/ppermute | solution.py:22
  190.8 125.0 %collective-permute-start.3 = (bf16[2,1,64,5120]{3,2,1,0:T(8,128)(2,1)}, bf16[2,1,64,5120]{3,2,1,0:T(8,128)(2,1)S(1)}, u32[]{:S(2)}, u32[]{:S(2)}) collective-permute-start(bf16[2,1,64,5120]{3,2,1,0:T(8,128)(2,1)} %get-tuple-element.232), channel_id=1, source_target_pairs={{0,9},{1,10},{2,11},{3,12},{4,13},{5,14},{6,15},{7,0},{8,1},{9,2},... | collective-permute-start | bytes 3932168 | tf_op jit(solution)/shard_map/ppermute | solution.py:22
  197.7 250.1 %collective-permute-start.5 = (bf16[2,1,64,5120]{3,2,1,0:T(8,128)(2,1)}, bf16[2,1,64,5120]{3,2,1,0:T(8,128)(2,1)S(1)}, u32[]{:S(2)}, u32[]{:S(2)}) collective-permute-start(bf16[2,1,64,5120]{3,2,1,0:T(8,128)(2,1)} %get-tuple-element.233), channel_id=1, source_target_pairs={{0,7},{1,8},{2,9},{3,10},{4,11},{5,12},{6,13},{7,14},{8,15},{9,0},... | collective-permute-start | bytes 3932168 | tf_op jit(solution)/shard_map/ppermute | solution.py:22
  203.9 244.0 %collective-permute-start.1 = (bf16[1,2,64,5120]{3,2,1,0:T(8,128)(2,1)}, bf16[1,2,64,5120]{3,2,1,0:T(8,128)(2,1)S(1)}, u32[]{:S(2)}, u32[]{:S(2)}) collective-permute-start(bf16[1,2,64,5120]{3,2,1,0:T(8,128)(2,1)} %bitcast.28), channel_id=1, source_target_pairs={{0,12},{1,13},{2,14},{3,15},{4,0},{5,1},{6,2},{7,3},{8,4},{9,5},{1... | collective-permute-start | bytes 3932168 | tf_op jit(solution)/shard_map/ppermute | solution.py:22
  208.3 239.5 %collective-permute-start.7 = (bf16[1,2,64,5120]{3,2,1,0:T(8,128)(2,1)}, bf16[1,2,64,5120]{3,2,1,0:T(8,128)(2,1)S(1)}, u32[]{:S(2)}, u32[]{:S(2)}) collective-permute-start(bf16[1,2,64,5120]{3,2,1,0:T(8,128)(2,1)} %bitcast.29), channel_id=1, source_target_pairs={{0,4},{1,5},{2,6},{3,7},{4,8},{5,9},{6,10},{7,11},{8,12},{9,13},{1... | collective-permute-start | bytes 3932168 | tf_op jit(solution)/shard_map/ppermute | solution.py:22
  456.9 196.2 %copy-start.5 = (f32[256,64]{0,1:T(8,128)S(1)}, f32[256,64]{0,1:T(8,128)}, u32[]{:S(2)}) copy-start(f32[256,64]{0,1:T(8,128)} %param.14) | copy-start | bytes 196612
  471.4 1.5 copy-start.8
  480.1 1.5 copy-start.8
  497.1 1.5 copy-start.8
  505.8 1.5 copy-start.8
  514.5 1.5 copy-start.8
  531.6 1.5 copy-start.8
  540.1 1.5 copy-start.8
  557.3 1.5 copy-start.8
  630.8 22.2 %collective-permute-start.17 = (f32[256,64]{0,1:T(8,128)S(1)}, f32[256,64]{0,1:T(8,128)S(1)}, u32[]{:S(2)}, u32[]{:S(2)}) collective-permute-start(f32[256,64]{0,1:T(8,128)S(1)} %fusion.50), channel_id=1, source_target_pairs={{0,8},{1,9},{2,10},{3,11},{4,12},{5,13},{6,14},{7,15},{8,0},{9,1},... | collective-permute-start | bytes 196616 | tf_op jit(solution)/shard_map/ppermute | solution.py:22
  (14 other events, 19.5 us)
where the time goes:
time: 662 us; the launch traced here: 654 us
  waiting for transfers between devices  259 us (39%)
  starting transfers between devices  193 us (29%)
  matrix products  87.9 us (13%)
  local copies, waits for them, and re-layouts  85.6 us (13%)
  other arithmetic  25.3 us (4%)
    ppermute x18, waiting for transfers between devices, passed_along(): return lax.ppermute(value, axis, pairs)  259 us
    ppermute x18, starting transfers between devices, passed_along(): return lax.ppermute(value, axis, pairs)  193 us
    sub x20, matrix products, one_head(): shifted = jnp.where(mask_full, jnp.exp(scores - row_max), 0.0)  62.3 us
    another operation x20, local copies, waits for them, and re-layouts, one_head(): jnp.stack([part[row_local:row_local + 3, col_local:col_local + 3] for par...  47.8 us
    while x40, local copies, waits for them, and re-layouts  25.9 us
    dot_general x20, matrix products, one_head(): jnp.einsum('qtk,qkd->qtd', weights, value_tiles, preferred_element_type=j...  23.7 us
    concatenate x2, other arithmetic, direct_window(): planes.append(jnp.concatenate(row_parts, axis=0))  16.7 us
  transfers between devices with their start and end apart: 18, of which 5 were waited for; matrix products, arithmetic and copies ran while one was open for 2% of the time, Pallas kernels for 0%

commit v1 on v0

--- a/solution.py
+++ b/solution.py
@@ -1,8 +1,11 @@
+import functools
 import math
 
 import jax
 import jax.numpy as jnp
 from jax import lax
+from jax.experimental import pallas as pl
+from jax.experimental.pallas import tpu as pltpu
 from jax.sharding import PartitionSpec as P
 
 HEADS = 20
@@ -134,7 +137,7 @@
     return result_rows.reshape(tok_rows, inner_width)
 
 
-def per_device(query_rows, key_rows, value_rows, tile_mask, head_weight, latent, step_index):
+def per_device_frames(query_rows, key_rows, value_rows, tile_mask, head_weight, latent, step_index):
     frame_count = lax.axis_size("frame")
     frame_index = lax.axis_index("frame")
     half_size = frame_count // 2
@@ -167,6 +170,369 @@
     return (guided, clean, latent_next)
 
 
+NEG = -1e30
+EXP_SCALE = math.log2(math.e) / math.sqrt(HD)
+GROUP = 4
+
+
+def contract_last(left, right):
+    return lax.dot_general(
+        left, right, (((1,), (1,)), ((), ())), preferred_element_type=jnp.float32
+    )
+
+
+def contract(left, right):
+    return jnp.dot(left, right, preferred_element_type=jnp.float32)
+
+
+def spread(flags, tile_tok):
+    lanes = len(flags) * tile_tok
+    lane = lax.broadcasted_iota(jnp.int32, (1, lanes), 1)
+    row = jnp.zeros((1, lanes), jnp.float32)
+    for number, flag in enumerate(flags):
+        bias = jnp.where(flag, jnp.float32(0.0), jnp.float32(NEG))
+        inside = (lane >= number * tile_tok) & (lane < (number + 1) * tile_tok)
+        row = jnp.where(inside, bias, row)
+    return row
+
+
+def biased(scores, rows, tile_tok):
+    return jnp.concatenate(
+        [scores[t * tile_tok : (t + 1) * tile_tok] + row for t, row in enumerate(rows)],
+        axis=0,
+    )
+
+
+def folded_values(weight_t, values):
+    exact = contract_last(weight_t, values)
+    high = exact.astype(jnp.bfloat16)
+    low = (exact - high.astype(jnp.float32)).astype(jnp.bfloat16)
+    return jnp.concatenate([high, low], axis=0)
+
+
+def weighted(pair, weights):
+    both = contract(pair, weights)
+    half = both.shape[0] // 2
+    return both[:half] + both[half:]
+
+
+def spot_of(index_ref, block_count, block_cols):
+    spot = index_ref[0] % block_count
+    block_row = spot // block_cols
+    block_col = spot % block_cols
+    return block_row, block_col, block_col % 2
+
+
+def per_head(step):
+    def run(group, carry):
+        for inner in range(GROUP):
+            step(group * GROUP + inner)
+        return carry
+
+    lax.fori_loop(0, HEADS // GROUP, run, 0)
+
+
+def head_lanes(head):
+    return pl.ds(pl.multiple_of(head * HD, HD), HD)
+
+
+def own_kernel(
+    block_count, block_cols, tile_tok,
+    index_ref, mask_ref, query_ref, key_ref, value_ref, inner_ref, weight_ref,
+    out_ref, top_ref, sum_ref,
+):
+    _, _, odd = spot_of(index_ref, block_count, block_cols)
+    side = 1 - 2 * odd
+    rows = []
+    for key_tile in range(4):
+        flags = []
+        for tile in range(4):
+            row_step = key_tile // 2 - tile // 2
+            col_step = key_tile % 2 - tile % 2
+            flags.append(mask_ref[tile, 9 + 3 * (row_step + 1) + col_step + 1] > 0)
+        rows.append(spread(flags, tile_tok))
+    for key_row in range(2):
+        flags = []
+        for tile in range(4):
+            row_step = key_row - tile // 2
+            entry = mask_ref[tile, 9 + 3 * (row_step + 1) + side + 1] > 0
+            flags.append(entry & (tile % 2 == 1 - odd))
+        rows.append(spread(flags, tile_tok))
+
+    def step(head):
+        lanes = head_lanes(head)
+        query = query_ref[:, lanes]
+        weight_t = weight_ref[:, lanes]
+        scores = jnp.concatenate(
+            [
+                contract_last(key_ref[:, lanes], query),
+                contract_last(inner_ref[0, :, lanes], query),
+            ],
+            axis=0,
+        )
+        scores = biased(scores, rows, tile_tok)
+        top = jnp.max(scores, axis=0, keepdims=True)
+        weights = jnp.exp2((scores - top) * EXP_SCALE)
+        top_ref[pl.ds(head, 1), :] = top
+        sum_ref[pl.ds(head, 1), :] = jnp.sum(weights, axis=0, keepdims=True)
+        pair = jnp.concatenate(
+            [
+                folded_values(weight_t, value_ref[:, lanes]),
+                folded_values(weight_t, inner_ref[1, :, lanes]),
+            ],
+            axis=1,
+        )
+        out_ref[head] = weighted(pair, weights.astype(jnp.bfloat16))
+
+    per_head(step)
+
+
+def edge_kernel(
+    block_count, block_cols, tile_tok,
+    index_ref, mask_ref, guest_mask_ref,
+    query_ref, key_ref, value_ref, inner_ref, outer_ref, guest_ref, weight_ref,
+    old_out_ref, old_top_ref, old_sum_ref,
+    out_ref, guest_out_ref, top_ref, sum_ref, send_ref,
+):
+    block_row, block_col, odd = spot_of(index_ref, block_count, block_cols)
+    side = 2 * odd - 1
+    there = (block_col + side >= 0) & (block_col + side < block_cols)
+    edge_row = 1 - block_row
+    edge_rows = pl.ds(pl.multiple_of(edge_row * 2 * tile_tok, 2 * tile_tok), 2 * tile_tok)
+    halo_rows = pl.ds(pl.multiple_of(edge_row * tile_tok, tile_tok), tile_tok)
+    guest_step = 2 * block_row - 1
+    rows = []
+    for key_row in range(2):
+        flags = []
+        for tile in range(4):
+            row_step = key_row - tile // 2
+            entry = mask_ref[tile, 9 + 3 * (row_step + 1) + side + 1] > 0
+            flags.append(entry & (tile % 2 == odd) & there)
+        rows.append(spread(flags, tile_tok))
+    guest_rows = []
+    base = 9 + 3 * (guest_step + 1) + 1
+    for key_col in range(2):
+        guest_rows.append(
+            spread(
+                [guest_mask_ref[col, base + key_col - col] > 0.5 for col in range(2)],
+                tile_tok,
+            )
+        )
+    guest_rows.append(
+        spread(
+            [
+                (guest_mask_ref[col, base - side] > 0.5) & (col == 1 - odd)
+                for col in range(2)
+            ],
+            tile_tok,
+        )
+    )
+    guest_rows.append(
+        spread(
+            [
+                (guest_mask_ref[col, base + side] > 0.5) & (col == odd) & there
+                for col in range(2)
+            ],
+            tile_tok,
+        )
+    )
+
+    def step(head):
+        lanes = head_lanes(head)
+        weight_t = weight_ref[:, lanes]
+        outer_pair = folded_values(weight_t, outer_ref[1, :, lanes])
+        scores = biased(
+            contract_last(outer_ref[0, :, lanes], query_ref[:, lanes]), rows, tile_tok
+        )
+        old_top = old_top_ref[pl.ds(head, 1), :]
+        top = jnp.maximum(old_top, jnp.max(scores, axis=0, keepdims=True))
+        shrink = jnp.exp2((old_top - top) * EXP_SCALE)
+        weights = jnp.exp2((scores - top) * EXP_SCALE)
+        top_ref[pl.ds(head, 1), :] = top
+        sum_ref[pl.ds(head, 1), :] = shrink * old_sum_ref[pl.ds(head, 1), :] + jnp.sum(
+            weights, axis=0, keepdims=True
+        )
+        out_ref[head] = shrink * old_out_ref[head] + weighted(
+            outer_pair, weights.astype(jnp.bfloat16)
+        )
+        guest_keys = jnp.concatenate(
+            [
+                key_ref[edge_rows, lanes],
+                inner_ref[0, halo_rows, lanes],
+                outer_ref[0, halo_rows, lanes],
+            ],
+            axis=0,
+        )
+        guest_values = jnp.concatenate(
+            [
+                value_ref[edge_rows, lanes],
+                inner_ref[1, halo_rows, lanes],
+                outer_ref[1, halo_rows, lanes],
+            ],
+            axis=0,
+        )
+        guest_scores = biased(
+            contract_last(guest_keys, guest_ref[:, lanes]), guest_rows, tile_tok
+        )
+        guest_top = jnp.max(guest_scores, axis=0, keepdims=True)
+        guest_weights = jnp.exp2((guest_scores - guest_top) * EXP_SCALE)
+        send_ref[2, pl.ds(head, 1), :] = guest_top
+        send_ref[3, pl.ds(head, 1), :] = jnp.sum(guest_weights, axis=0, keepdims=True)
+        guest_out_ref[head] = weighted(
+            folded_values(weight_t, guest_values), guest_weights.astype(jnp.bfloat16)
+        )
+
+    per_head(step)
+    send_ref[0] = top_ref[:, edge_rows]
+    send_ref[1] = sum_ref[:, edge_rows]
+
+
+def blend_kernel(
+    block_count, block_cols, tile_tok,
+    index_ref, out_ref, guest_out_ref, top_ref, sum_ref, sent_ref, got_ref,
+    velocity_ref, guest_velocity_ref, far_top, far_sum,
+):
+    block_row, _, _ = spot_of(index_ref, block_count, block_cols)
+    edge_lanes = pl.ds(
+        pl.multiple_of((1 - block_row) * 2 * tile_tok, 2 * tile_tok), 2 * tile_tok
+    )
+    far_top[...] = jnp.full_like(far_top, NEG)
+    far_sum[...] = jnp.zeros_like(far_sum)
+    far_top[:, edge_lanes] = got_ref[2]
+    far_sum[:, edge_lanes] = got_ref[3]
+
+    def share(near_top, near_sum, away_top, away_sum):
+        top = jnp.maximum(near_top, away_top)
+        near = jnp.exp2((near_top - top) * EXP_SCALE)
+        away = jnp.exp2((away_top - top) * EXP_SCALE)
+        return near / (near * near_sum + away * away_sum)
+
+    own_share = share(top_ref[...], sum_ref[...], far_top[...], far_sum[...])
+    guest_share = share(sent_ref[2], sent_ref[3], got_ref[0], got_ref[1])
+    velocity = jnp.zeros(velocity_ref.shape, jnp.float32)
+    guest_velocity = jnp.zeros(guest_velocity_ref.shape, jnp.float32)
+    for head in range(HEADS):
+        velocity = velocity + own_share[head : head + 1] * out_ref[head]
+        guest_velocity = guest_velocity + guest_share[head : head + 1] * guest_out_ref[head]
+    velocity_ref[...] = velocity
+    guest_velocity_ref[...] = guest_velocity
+
+
+def kernel_call(body, args, outs, smem, scratch=()):
+    specs = [
+        pl.BlockSpec(memory_space=pltpu.SMEM if number < smem else pltpu.VMEM)
+        for number in range(len(args))
+    ]
+    return pl.pallas_call(
+        body,
+        out_shape=[jax.ShapeDtypeStruct(shape, jnp.float32) for shape in outs],
+        in_specs=specs,
+        out_specs=[pl.BlockSpec(memory_space=pltpu.VMEM) for _ in outs],
+        scratch_shapes=list(scratch),
+    )(*args)
+
+
+def per_device(query_rows, key_rows, value_rows, tile_mask, head_weight, latent, step_index):
+    frame_count = lax.axis_size("frame")
+    half_size = frame_count // 2
+    block_cols = SW // 2
+    block_rows = SH // 2
+    block_count = block_rows * block_cols
+    if half_size != block_count or block_rows != 2 or block_cols % 2:
+        return per_device_frames(
+            query_rows, key_rows, value_rows, tile_mask, head_weight, latent, step_index
+        )
+    frame_index = lax.axis_index("frame")
+    spot = frame_index % block_count
+    edge_row = 1 - spot // block_cols
+    odd = spot % 2
+    tok_rows, width = query_rows.shape
+    tile_tok = tok_rows // 4
+    channels = head_weight.shape[1]
+    places = range(frame_count)
+    row_pairs = [
+        (f, f + block_cols if f % block_count < block_cols else f - block_cols)
+        for f in places
+    ]
+    mate_pairs = [(f, f + 1 - 2 * (f % 2)) for f in places]
+    side_pairs = []
+    for f in places:
+        step = 2 * (f % 2) - 1
+        if 0 <= f % block_cols + step < block_cols:
+            side_pairs.append((f, f + step))
+    branch_pairs = [(f, (f + half_size) % frame_count) for f in places]
+
+    guest_query = lax.ppermute(
+        lax.dynamic_slice_in_dim(query_rows, edge_row * 2 * tile_tok, 2 * tile_tok, 0),
+        "frame",
+        row_pairs,
+    )
+    grid = (2, 2, tile_tok, width)
+
+    def column(number):
+        parts = [
+            lax.dynamic_index_in_dim(rows.reshape(grid), number, 1, keepdims=False)
+            for rows in (key_rows, value_rows)
+        ]
+        return jnp.stack(parts).reshape(2, 2 * tile_tok, width)
+
+    outer = lax.ppermute(column(odd), "frame", side_pairs)
+    inner = lax.ppermute(column(1 - odd), "frame", mate_pairs)
+    guest_mask = lax.ppermute(
+        lax.dynamic_slice_in_dim(tile_mask, edge_row * 2, 2, 0).astype(jnp.float32),
+        "frame",
+        row_pairs,
+    )
+    index = frame_index.astype(jnp.int32).reshape(1)
+    weight_t = head_weight.T
+    sizes = (block_count, block_cols, tile_tok)
+    stats = (HEADS, tok_rows)
+    own_out = (HEADS, channels, tok_rows)
+    own, top, total = kernel_call(
+        functools.partial(own_kernel, *sizes),
+        (index, tile_mask, query_rows, key_rows, value_rows, inner, weight_t),
+        (own_out, stats, stats),
+        2,
+    )
+    own, guest_out, top, total, sent = kernel_call(
+        functools.partial(edge_kernel, *sizes),
+        (
+            index, tile_mask, guest_mask, query_rows, key_rows, value_rows, inner, outer,
+            guest_query, weight_t, own, top, total,
+        ),
+        (
+            own_out,
+            (HEADS, channels, 2 * tile_tok),
+            stats,
+            stats,
+            (4, HEADS, 2 * tile_tok),
+        ),
+        3,
+    )
+    got = lax.ppermute(sent, "frame", row_pairs)
+    velocity, guest_velocity = kernel_call(
+        functools.partial(blend_kernel, *sizes),
+        (index, own, guest_out, top, total, sent, got),
+        ((channels, tok_rows), (channels, 2 * tile_tok)),
+        1,
+        (pltpu.VMEM(stats, jnp.float32), pltpu.VMEM(stats, jnp.float32)),
+    )
+    back = lax.ppermute(guest_velocity, "frame", row_pairs)
+    lane = jnp.arange(tok_rows)[None, :] // (2 * tile_tok)
+    velocity = velocity + jnp.where(lane == edge_row, jnp.tile(back, (1, 2)), 0.0)
+    partner = lax.ppermute(velocity, "frame", branch_pairs)
+    is_cond = frame_index < half_size
+    cond = jnp.where(is_cond, velocity, partner).T
+    uncond = jnp.where(is_cond, partner, velocity).T
+    guided = uncond + GUIDANCE * (cond - uncond)
+    moment = step_index[0].astype(jnp.float32)
+    sigma_now = flow_sigma(moment)
+    step_size = flow_sigma(moment + 1.0) - sigma_now
+    clean = latent - sigma_now * guided
+    latent_next = latent + step_size * guided
+    return (guided, clean, latent_next)
+
+
 def solution(mesh):
     placed = (
         P(("groups", "frame"), None),

time: 662 us -> 59.7 us (0.09); the launches traced: 654 us -> 59.4 us
  waiting for transfers between devices: 259 us -> 9.05 us
  starting transfers between devices: 193 us -> 12.2 us
  matrix products: 87.9 us -> 0 us
  local copies, waits for them, and re-layouts: 85.6 us -> 4.57 us
  Pallas kernels: 0 us -> 27.6 us
  other arithmetic: 25.3 us -> 4.52 us
    ppermute x18 -> x7, waiting for transfers between devices: 259 us -> 9.05 us  [the longest x1 2.8 us: per_device(): got = lax.ppermute(sent, 'frame', row_pairs)]
    ppermute x18 -> x7, starting transfers between devices: 193 us -> 12.2 us  [the longest x1 2.84 us: per_device(): partner = lax.ppermute(velocity, 'frame', branch_pairs)]
    sub x20 -> x0, matrix products: 62.3 us -> none  [one_head(): shifted = jnp.where(mask_full, jnp.exp(scores - row_max), 0.0)]
    another operation x20 -> x1, local copies, waits for them, and re-layouts: 47.8 us -> 0.02 us  [per_device(): jnp.tile(back, (1, 2))]
    pallas_call x0 -> x3, Pallas kernels: none -> 27.6 us  [kernel_call(): pl.pallas_call(body, out_shape=[jax.ShapeDtypeStruct(shape, jnp.float32)...]
    while x40 -> x0, local copies, waits for them, and re-layouts: 25.9 us -> none
    dot_general x21 -> x0, matrix products: 25.6 us -> none  [the longest x20 23.7 us: one_head(): jnp.einsum('qtk,qkd->qtd', weights, value_tiles, preferred_element_type=j...]
    concatenate x2 -> x0, other arithmetic: 16.7 us -> none  [direct_window(): planes.append(jnp.concatenate(row_parts, axis=0))]
  transfers between devices with their start and end apart: 18 -> 7, of which waited for: 5 -> 4; matrix products, arithmetic and copies ran while one was open for 2% -> 2% of each run, Pallas kernels for 0% -> 18%
where the time goes in v1:
time: 59.7 us; the launch traced here: 59.4 us
  Pallas kernels  27.6 us (46%)
  starting transfers between devices  12.2 us (20%)
  waiting for transfers between devices  9.05 us (15%)
  local copies, waits for them, and re-layouts  4.57 us (8%)
  other arithmetic  4.52 us (8%)
  between operations  1.46 us (2%)
    pallas_call x3, Pallas kernels, kernel_call(): pl.pallas_call(body, out_shape=[jax.ShapeDtypeStruct(shape, jnp.float32)...  27.6 us
    ppermute x1, starting transfers between devices, per_device(): partner = lax.ppermute(velocity, 'frame', branch_pairs)  2.84 us
    ppermute x1, waiting for transfers between devices, per_device(): got = lax.ppermute(sent, 'frame', row_pairs)  2.8 us
    ppermute x1, starting transfers between devices, per_device(): lax.ppermute(lax.dynamic_slice_in_dim(query_rows, edge_row * 2 * tile_tok...  2.63 us
    unnamed x16, local copies, waits for them, and re-layouts  2.55 us
    ppermute x1, starting transfers between devices, per_device(): got = lax.ppermute(sent, 'frame', row_pairs)  2.53 us
    ppermute x1, waiting for transfers between devices, per_device(): back = lax.ppermute(guest_velocity, 'frame', row_pairs)  2.36 us
    another operation x2, other arithmetic, column(): return jnp.stack(parts).reshape(2, 2 * tile_tok, width)  2.35 us
  transfers between devices with their start and end apart: 7, of which 4 were waited for; matrix products, arithmetic and copies ran while one was open for 2% of the time, Pallas kernels for 18%

profile of v1, /device:TPU:0, one launch (start us, length us, event | category | flops | bytes accessed | tf_op | source)
XLA Modules:
  0.0 59.4 jit_solution(9115379519638829678)
XLA Ops:
  0.7 1.9 %constant_dynamic-slice_fusion.1 = (bf16[2,1,64,2560]{3,2,1,0:T(8,128)(2,1)S(1)}, bf16[2,1,64,2560]{3,2,1,0:T(8,128)(2,1)S(1)}, bf16[2,1,64,2560]{3,2,1,0:T(8,128)(2,1)S(1)}, bf16[2,1,64,2560]{3,2,1,0:T(8,128)(2,1)S(1)}) fusion(bf16[2,2,64,2560]{3,2,1,0:T(8,128)(2,1)} %bitcast.34, s32[]{:T(128)S(6)} %select_n.62, s32[]{:T(128)S(6)} %select_n.61, ...), kind=kLoop, calls=%fused_computation.14 | loop fusion | bytes 5242888 | tf_op jit(solution)/shard_map/jit(dynamic_index_in_dim)/dynamic_slice | solution.py:474
  2.6 1.2 %pad_maximum_fusion = bf16[2,128,2560]{2,1,0:T(8,128)(2,1)} fusion(bf16[1,128,2560]{2,1,0:T(8,128)(2,1)S(1)} %bitcast.37, bf16[1,128,2560]{2,1,0:T(8,128)(2,1)S(1)} %bitcast.38), kind=kLoop, calls=%fused_computation | loop fusion | flops 655360 | bytes 2621440 | tf_op jit(solution)/shard_map/stack | solution.py:477
  3.8 0.5 collective-permute-start.1
  4.3 0.0 copy-start
  4.3 1.2 %pad_maximum_fusion.1 = bf16[2,128,2560]{2,1,0:T(8,128)(2,1)} fusion(bf16[1,128,2560]{2,1,0:T(8,128)(2,1)S(1)} %bitcast.35, bf16[1,128,2560]{2,1,0:T(8,128)(2,1)S(1)} %bitcast.36), kind=kLoop, calls=%fused_computation.1 | loop fusion | flops 655360 | bytes 2621440 | tf_op jit(solution)/shard_map/stack | solution.py:477
  5.5 1.9 %collective-permute-start.2 = (bf16[2,128,2560]{2,1,0:T(8,128)(2,1)}, bf16[2,128,2560]{2,1,0:T(8,128)(2,1)}, u32[]{:S(2)}, u32[]{:S(2)}) collective-permute-start(bf16[2,128,2560]{2,1,0:T(8,128)(2,1)} %pad_maximum_fusion.1), channel_id=1, source_target_pairs={{1,2},{2,1},{5,6},{6,5},{9,10},{10,9},{13,14},{14,13},{17,18},{18,... | collective-permute-start | bytes 3932168 | tf_op jit(solution)/shard_map/ppermute | solution.py:479
  7.4 0.0 copy-done
  7.4 2.6 %collective-permute-start.3 = (bf16[128,2560]{1,0:T(8,128)(2,1)S(1)}, bf16[128,2560]{1,0:T(8,128)(2,1)S(1)}, u32[]{:S(2)}, u32[]{:S(2)}) collective-permute-start(bf16[128,2560]{1,0:T(8,128)(2,1)S(1)} %constant_dynamic-slice_fusion), channel_id=1, source_target_pairs={{0,4},{1,5},{2,6},{3,7},{4,0},{5,1},{6,2},{7,3},{8,12},{9,13},{10,... | collective-permute-start | bytes 1966088 | tf_op jit(solution)/shard_map/ppermute | solution.py:465
  10.0 0.0 copy-done.6
  10.0 0.1 collective-permute-start
  10.1 0.0 collective-permute-done.1.inner_ref
  10.1 1.1 %copy-done.1 = bf16[2,128,2560]{2,1,0:T(8,128)(2,1)} copy-done((bf16[2,128,2560]{2,1,0:T(8,128)(2,1)}, bf16[2,128,2560]{2,1,0:T(8,128)(2,1)S(1)}, u32[]{:S(2)}) %copy-start.1) | copy-done | bytes 1310744
  11.2 10.9 %shard_map.94 = (f32[20,64,256]{2,1,0:T(8,128)}, f32[20,256]{1,0:T(8,128)}, f32[20,256]{1,0:T(8,128)}) custom-call(s32[1]{0:T(128)} %bitcast.index_ref, s32[4,27]{1,0:T(4,128)} %mask_ref.3, bf16[256,2560]{1,0:T(8,128)(2,1)} %query_ref.3, bf16[256,2560]{1,0:T(8,128)(2,1)} %key_ref.3, bf16[256,2560]{1,0:T(8,128)(2,1)} %value_ref.3, ...), custom_call_target="tpu_custom_call" | custom-call | tf_op jit(solution)/shard_map/pallas_call | solution.py:426
  22.1 2.2 %collective-permute-done.guest_mask_ref = f32[2,27]{1,0:T(2,128)S(1)} collective-permute-done((f32[2,27]{1,0:T(2,128)S(1)}, f32[2,27]{1,0:T(2,128)S(1)}, u32[]{:S(2)}, u32[]{:S(2)}) %collective-permute-start) | collective-permute-done | bytes 248 | tf_op jit(solution)/shard_map/ppermute | solution.py:481
  24.4 0.0 collective-permute-done.3.guest_ref
  24.4 0.0 collective-permute-done.2.outer_ref
  24.4 0.5 copy-done.7
  24.9 0.3 copy-done.2
  25.2 14.3 %shard_map.95 = (f32[20,64,256]{2,1,0:T(8,128)}, f32[20,64,128]{2,1,0:T(8,128)}, f32[20,256]{1,0:T(8,128)}, f32[20,256]{1,0:T(8,128)}, f32[4,20,128]{2,1,0:T(8,128)}) custom-call(s32[1]{0:T(128)} %bitcast.index_ref, s32[4,27]{1,0:T(4,128)} %mask_ref.3, f32[2,27]{1,0:T(2,128)} %copy-done.7, bf16[256,2560]{1,0:T(8,128)(2,1)} %query_ref.3, ...), custom_call_target="tpu_custom_call" | custom-call | tf_op jit(solution)/shard_map/pallas_call | solution.py:426
  39.6 2.5 %collective-permute-start.4 = (f32[4,20,128]{2,1,0:T(8,128)}, f32[4,20,128]{2,1,0:T(8,128)S(1)}, u32[]{:S(2)}, u32[]{:S(2)}) collective-permute-start(f32[4,20,128]{2,1,0:T(8,128)} %get-tuple-element.20.sent_ref), channel_id=1, source_target_pairs={{0,4},{1,5},{2,6},{3,7},{4,0},{5,1},{6,2},{7,3},{8,12},{9,13},{10,... | collective-permute-start | bytes 122888 | tf_op jit(solution)/shard_map/ppermute | solution.py:512
  42.1 2.8 %collective-permute-done.4.got_ref = f32[4,20,128]{2,1,0:T(8,128)S(1)} collective-permute-done((f32[4,20,128]{2,1,0:T(8,128)}, f32[4,20,128]{2,1,0:T(8,128)S(1)}, u32[]{:S(2)}, u32[]{:S(2)}) %collective-permute-start.4) | collective-permute-done | bytes 40992 | tf_op jit(solution)/shard_map/ppermute | solution.py:512
  44.9 0.6 %copy-done.5 = f32[4,20,128]{2,1,0:T(8,128)} copy-done((f32[4,20,128]{2,1,0:T(8,128)}, f32[4,20,128]{2,1,0:T(8,128)S(1)}, u32[]{:S(2)}) %copy-start.5) | copy-done | bytes 40984
  45.5 2.3 %shard_map.96 = (f32[64,256]{1,0:T(8,128)}, f32[64,128]{1,0:T(8,128)}) custom-call(s32[1]{0:T(128)} %bitcast.index_ref, f32[20,64,256]{2,1,0:T(8,128)} %get-tuple-element.16.out_ref, f32[20,64,128]{2,1,0:T(8,128)} %get-tuple-element.17.guest_out_ref, f32[20,256]{1,0:T(8,128)} %get-tuple-element.18.top_ref, f32[20,256]{1,0:T(8,128)} %get-tuple-element.19.sum_ref, ...), custom_call_target="tpu_custom_call" | custom-call | tf_op jit(solution)/shard_map/pallas_call | solution.py:426
  47.9 1.8 %collective-permute-start.5 = (f32[64,128]{1,0:T(8,128)}, f32[64,128]{1,0:T(8,128)S(1)}, u32[]{:S(2)}, u32[]{:S(2)}) collective-permute-start(f32[64,128]{1,0:T(8,128)} %get-tuple-element.22), channel_id=1, source_target_pairs={{0,4},{1,5},{2,6},{3,7},{4,0},{5,1},{6,2},{7,3},{8,12},{9,13},{10,... | collective-permute-start | bytes 98312 | tf_op jit(solution)/shard_map/ppermute | solution.py:520
  49.6 2.4 %collective-permute-done.5 = f32[64,128]{1,0:T(8,128)S(1)} collective-permute-done((f32[64,128]{1,0:T(8,128)}, f32[64,128]{1,0:T(8,128)S(1)}, u32[]{:S(2)}, u32[]{:S(2)}) %collective-permute-start.5) | collective-permute-done | bytes 32800 | tf_op jit(solution)/shard_map/ppermute | solution.py:520
  52.0 0.9 %fusion = f32[64,256]{1,0:T(8,128)S(1)} fusion(f32[64,256]{1,0:T(8,128)} %get-tuple-element.21, f32[8,8,2,128]{3,2,1,0:T(2,128)S(1)} %bitcast.41, pred[256]{0:T(512)(128)(4,1)S(1)} %fusion.4), kind=kLoop, calls=%fused_computation.3 | loop fusion | flops 32768 | bytes 196864 | tf_op jit(solution)/shard_map/add | solution.py:522
  52.9 2.8 %collective-permute-start.6 = (f32[64,256]{1,0:T(8,128)S(1)}, f32[64,256]{1,0:T(8,128)S(1)}, u32[]{:S(2)}, u32[]{:S(2)}) collective-permute-start(f32[64,256]{1,0:T(8,128)S(1)} %fusion), channel_id=1, source_target_pairs={{0,8},{1,9},{2,10},{3,11},{4,12},{5,13},{6,14},{7,15},{8,0},{9,1},... | collective-permute-start | bytes 196616 | tf_op jit(solution)/shard_map/ppermute | solution.py:523
  56.5 1.6 %collective-permute-done.6 = f32[64,256]{1,0:T(8,128)S(1)} collective-permute-done((f32[64,256]{1,0:T(8,128)S(1)}, f32[64,256]{1,0:T(8,128)S(1)}, u32[]{:S(2)}, u32[]{:S(2)}) %collective-permute-start.6) | collective-permute-done | bytes 65568 | tf_op jit(solution)/shard_map/ppermute | solution.py:523
  58.1 0.0 copy-done.3
  58.1 0.7 %multiply_add_fusion = (f32[256,64]{0,1:T(8,128)}, f32[256,64]{0,1:T(8,128)S(1)}) fusion(f32[256,64]{0,1:T(8,128)S(1)} %copy-done.3, f32[]{:T(128)S(6)} %sub.44, f32[64,256]{1,0:T(8,128)S(1)} %fusion, f32[64,256]{1,0:T(8,128)S(1)} %collective-permute-done.6, pred[]{:T(512)S(6)} %lt.28), kind=kLoop, calls=%fused_computation.7 | loop fusion | flops 114688 | bytes 327685 | tf_op jit(solution)/shard_map/add | solution.py:532
  58.8 0.6 %multiply_subtract_fusion = f32[256,64]{0,1:T(8,128)} fusion(f32[256,64]{0,1:T(8,128)S(1)} %copy-done.3, f32[256,64]{0,1:T(8,128)S(1)} %get-tuple-element.24, f32[]{:T(128)} %bitcast.10), kind=kLoop, calls=%fused_computation.8 | loop fusion | flops 32768 | bytes 196612 | tf_op jit(solution)/shard_map/sub | solution.py:531
  59.4 0.0 copy-done.4
  (11 shorter events, 0.1 us)
Async XLA Ops:
  3.8 6.3 %collective-permute-start.1 = (bf16[2,128,2560]{2,1,0:T(8,128)(2,1)}, bf16[2,128,2560]{2,1,0:T(8,128)(2,1)S(1)}, u32[]{:S(2)}, u32[]{:S(2)}) collective-permute-start(bf16[2,128,2560]{2,1,0:T(8,128)(2,1)} %pad_maximum_fusion), channel_id=1, source_target_pairs={{0,1},{1,0},{2,3},{3,2},{4,5},{5,4},{6,7},{7,6},{8,9},{9,8},{10,11... | collective-permute-start | bytes 3932168 | tf_op jit(solution)/shard_map/ppermute | solution.py:480
  4.3 3.1 %copy-start = (bf16[256,2560]{1,0:T(8,128)(2,1)S(1)}, bf16[256,2560]{1,0:T(8,128)(2,1)}, u32[]{:S(2)}) copy-start(bf16[256,2560]{1,0:T(8,128)(2,1)} %query_ref.3) | copy-start | bytes 3932164
  5.5 4.6 %copy-start.6 = (s32[4,27]{1,0:T(4,128)S(1)}, s32[4,27]{1,0:T(4,128)}, u32[]{:S(2)}) copy-start(s32[4,27]{1,0:T(4,128)} %mask_ref.3) | copy-start | bytes 1300
  5.5 18.9 %collective-permute-start.2 = (bf16[2,128,2560]{2,1,0:T(8,128)(2,1)}, bf16[2,128,2560]{2,1,0:T(8,128)(2,1)}, u32[]{:S(2)}, u32[]{:S(2)}) collective-permute-start(bf16[2,128,2560]{2,1,0:T(8,128)(2,1)} %pad_maximum_fusion.1), channel_id=1, source_target_pairs={{1,2},{2,1},{5,6},{6,5},{9,10},{10,9},{13,14},{14,13},{17,18},{18,... | collective-permute-start | bytes 3932168 | tf_op jit(solution)/shard_map/ppermute | solution.py:479
  7.4 17.0 %collective-permute-start.3 = (bf16[128,2560]{1,0:T(8,128)(2,1)S(1)}, bf16[128,2560]{1,0:T(8,128)(2,1)S(1)}, u32[]{:S(2)}, u32[]{:S(2)}) collective-permute-start(bf16[128,2560]{1,0:T(8,128)(2,1)S(1)} %constant_dynamic-slice_fusion), channel_id=1, source_target_pairs={{0,4},{1,5},{2,6},{3,7},{4,0},{5,1},{6,2},{7,3},{8,12},{9,13},{10,... | collective-permute-start | bytes 1966088 | tf_op jit(solution)/shard_map/ppermute | solution.py:465
  10.0 14.3 %collective-permute-start = (f32[2,27]{1,0:T(2,128)S(1)}, f32[2,27]{1,0:T(2,128)S(1)}, u32[]{:S(2)}, u32[]{:S(2)}) collective-permute-start(f32[2,27]{1,0:T(2,128)S(1)} %fusion.3), channel_id=1, source_target_pairs={{0,4},{1,5},{2,6},{3,7},{4,0},{5,1},{6,2},{7,3},{8,12},{9,13},{10,... | collective-permute-start | bytes 656 | tf_op jit(solution)/shard_map/ppermute | solution.py:481
  10.1 1.1 %copy-start.1 = (bf16[2,128,2560]{2,1,0:T(8,128)(2,1)}, bf16[2,128,2560]{2,1,0:T(8,128)(2,1)S(1)}, u32[]{:S(2)}) copy-start(bf16[2,128,2560]{2,1,0:T(8,128)(2,1)S(1)} %collective-permute-done.1.inner_ref) | copy-start | bytes 3932164
  24.4 0.5 copy-start.7
  24.4 0.9 %copy-start.2 = (bf16[128,2560]{1,0:T(8,128)(2,1)}, bf16[128,2560]{1,0:T(8,128)(2,1)S(1)}, u32[]{:S(2)}) copy-start(bf16[128,2560]{1,0:T(8,128)(2,1)S(1)} %collective-permute-done.3.guest_ref) | copy-start | bytes 1966084
  39.6 18.5 %copy-start.3 = (f32[256,64]{0,1:T(8,128)S(1)}, f32[256,64]{0,1:T(8,128)}, u32[]{:S(2)}) copy-start(f32[256,64]{0,1:T(8,128)} %param.12) | copy-start | bytes 196612
  39.6 5.3 %collective-permute-start.4 = (f32[4,20,128]{2,1,0:T(8,128)}, f32[4,20,128]{2,1,0:T(8,128)S(1)}, u32[]{:S(2)}, u32[]{:S(2)}) collective-permute-start(f32[4,20,128]{2,1,0:T(8,128)} %get-tuple-element.20.sent_ref), channel_id=1, source_target_pairs={{0,4},{1,5},{2,6},{3,7},{4,0},{5,1},{6,2},{7,3},{8,12},{9,13},{10,... | collective-permute-start | bytes 122888 | tf_op jit(solution)/shard_map/ppermute | solution.py:512
  44.9 0.6 %copy-start.5 = (f32[4,20,128]{2,1,0:T(8,128)}, f32[4,20,128]{2,1,0:T(8,128)S(1)}, u32[]{:S(2)}) copy-start(f32[4,20,128]{2,1,0:T(8,128)S(1)} %collective-permute-done.4.got_ref) | copy-start | bytes 122884
  47.9 4.1 %collective-permute-start.5 = (f32[64,128]{1,0:T(8,128)}, f32[64,128]{1,0:T(8,128)S(1)}, u32[]{:S(2)}, u32[]{:S(2)}) collective-permute-start(f32[64,128]{1,0:T(8,128)} %get-tuple-element.22), channel_id=1, source_target_pairs={{0,4},{1,5},{2,6},{3,7},{4,0},{5,1},{6,2},{7,3},{8,12},{9,13},{10,... | collective-permute-start | bytes 98312 | tf_op jit(solution)/shard_map/ppermute | solution.py:520
  52.9 5.2 %collective-permute-start.6 = (f32[64,256]{1,0:T(8,128)S(1)}, f32[64,256]{1,0:T(8,128)S(1)}, u32[]{:S(2)}, u32[]{:S(2)}) collective-permute-start(f32[64,256]{1,0:T(8,128)S(1)} %fusion), channel_id=1, source_target_pairs={{0,8},{1,9},{2,10},{3,11},{4,12},{5,13},{6,14},{7,15},{8,0},{9,1},... | collective-permute-start | bytes 196616 | tf_op jit(solution)/shard_map/ppermute | solution.py:523
  58.8 0.7 %copy-start.4 = (f32[256,64]{0,1:T(8,128)}, f32[256,64]{0,1:T(8,128)S(1)}, u32[]{:S(2)}) copy-start(f32[256,64]{0,1:T(8,128)S(1)} %get-tuple-element.24) | copy-start | bytes 196612

commit v2 on v0

--- a/solution.py
+++ b/solution.py
@@ -1,9 +1,13 @@
+import functools
 import math
 
 import jax
 import jax.numpy as jnp
 from jax import lax
+from jax.experimental import pallas as pl
+from jax.experimental.pallas import tpu as pltpu
 from jax.sharding import PartitionSpec as P
+
 
 HEADS = 20
 HD = 128
@@ -134,7 +138,7 @@
     return result_rows.reshape(tok_rows, inner_width)
 
 
-def per_device(query_rows, key_rows, value_rows, tile_mask, head_weight, latent, step_index):
+def per_device_frames(query_rows, key_rows, value_rows, tile_mask, head_weight, latent, step_index):
     frame_count = lax.axis_size("frame")
     frame_index = lax.axis_index("frame")
     half_size = frame_count // 2
@@ -167,6 +171,551 @@
     return (guided, clean, latent_next)
 
 
+NEG = -1e30
+VMEM_LIMIT = 16 << 20
+PIECES = 4
+EXP_SCALE = math.log2(math.e) / math.sqrt(HD)
+
+
+def contract_last(left, right):
+    return lax.dot_general(
+        left, right, (((1,), (1,)), ((), ())), preferred_element_type=jnp.float32
+    )
+
+
+def contract(left, right):
+    return jnp.dot(left, right, preferred_element_type=jnp.float32)
+
+
+def head_lanes(head):
+    return slice(head * HD, (head + 1) * HD)
+
+
+class Spot:
+    def __init__(self, index, block_count, block_cols):
+        spot = index % block_count
+        block_row = spot // block_cols
+        block_col = spot % block_cols
+        odd = block_col % 2
+        self.edge = 1 - block_row
+        self.rest = block_row
+        self.near = 1 - odd
+        self.far = odd
+        self.near_step = 1 - 2 * odd
+        self.far_step = 2 * odd - 1
+        side = block_col + self.far_step
+        self.there = (side >= 0) & (side < block_cols)
+        self.guest_step = 2 * block_row - 1
+        self.lane_tiles = (
+            (self.rest, self.near),
+            (self.edge, self.near),
+            (self.edge, self.far),
+            (self.rest, self.far),
+        )
+        self.key_tiles = (
+            (self.edge, self.near),
+            (self.rest, self.near),
+            (self.rest, self.far),
+            (self.edge, self.far),
+        )
+
+
+def tile_rows(tile, tile_tok):
+    row, col = tile
+    return pl.ds(pl.multiple_of((2 * row + col) * tile_tok, tile_tok), tile_tok)
+
+
+def entry(row_step, col_step):
+    return 9 + 3 * (row_step + 1) + col_step + 1
+
+
+def bias_of(flag):
+    return jnp.where(flag, jnp.float32(0.0), jnp.float32(NEG))
+
+
+def key_bias(rows, tile_tok):
+    biases = []
+    for flags in rows:
+        lanes = len(flags) * tile_tok
+        lane = lax.broadcasted_iota(jnp.int32, (1, lanes), 1) // tile_tok
+        bias = jnp.zeros((1, lanes), jnp.float32)
+        for number, flag in enumerate(flags):
+            bias = jnp.where(lane == number, bias_of(flag), bias)
+        biases.append(bias)
+    return biases
+
+
+def biased(scores, biases, tile_tok):
+    return above(
+        *[scores[t * tile_tok : (t + 1) * tile_tok] + row for t, row in enumerate(biases)]
+    )
+
+
+def beside(left, right):
+    return jnp.concatenate([left, right], axis=1)
+
+
+def above(*parts):
+    return jnp.concatenate(parts, axis=0)
+
+
+def largest(scores):
+    return jnp.max(scores, axis=0, keepdims=True)
+
+
+def softened(scores, top):
+    return jnp.exp2((scores - top) * EXP_SCALE).astype(jnp.bfloat16)
+
+
+def with_ones(folded):
+    return above(folded, jnp.ones((16, folded.shape[1]), folded.dtype))
+
+
+def pipelined(*stages):
+    for turn in range(HEADS + len(stages) - 1):
+        for number, stage in enumerate(stages):
+            if 0 <= turn - number < HEADS:
+                stage(turn - number)
+
+
+def folded_at(width, channels, head):
+    row = head % 2 * channels
+    lane = width + head // 2 * 2 * channels
+    return slice(row, row + channels), slice(lane, lane + 2 * channels)
+
+
+def copied(pairs, sems):
+    copies = [
+        pltpu.make_async_copy(source, target, sems.at[number])
+        for number, (source, target) in enumerate(pairs)
+    ]
+    for copy in copies:
+        copy.start()
+    return copies
+
+
+def piece(rows, start, stop):
+    return pl.ds(pl.multiple_of(rows.start + start, stop - start), stop - start)
+
+
+def guest_pack_kernel(block_count, block_cols, tile_tok, index_ref, query_ref, out_ref, sems):
+    spot = Spot(index_ref[0], block_count, block_cols)
+    step = tile_tok // PIECES
+    pairs = []
+    for number, col in enumerate((spot.near, spot.far)):
+        rows = tile_rows((spot.edge, col), tile_tok)
+        for start in range(0, tile_tok, step):
+            source = query_ref.at[piece(rows, start, start + step)]
+            pairs.append((source, out_ref.at[pl.ds(number * tile_tok + start, step)]))
+    for copy in copied(pairs, sems):
+        copy.wait()
+
+
+def column_pack_kernel(
+    block_count, block_cols, tile_tok,
+    index_ref, key_ref, value_ref, weight_ref, near_ref, far_ref, values, weight, sems,
+):
+    spot = Spot(index_ref[0], block_count, block_cols)
+    channels, width = weight_ref.shape
+    half = 2 * tile_tok
+    pairs = [(weight_ref, weight)]
+    for number, tile in enumerate(spot.key_tiles):
+        rows = pl.ds(number * tile_tok, tile_tok)
+        pairs.append((value_ref.at[tile_rows(tile, tile_tok)], values.at[rows]))
+    for number, tile in enumerate(spot.key_tiles):
+        out_ref = (near_ref, far_ref)[number // 2]
+        target = out_ref.at[pl.ds(number % 2 * tile_tok, tile_tok), pl.ds(0, width)]
+        pairs.append((key_ref.at[tile_rows(tile, tile_tok)], target))
+    copies = copied(pairs, sems)
+    for copy in copies[:5]:
+        copy.wait()
+    for head in range(HEADS):
+        lanes = head_lanes(head)
+        folded = contract_last(weight[:, lanes], values[:, lanes]).astype(jnp.bfloat16)
+        where = folded_at(width, channels, head)
+        near_ref[where] = folded[:, :half]
+        far_ref[where] = folded[:, half:]
+    for copy in copies[5:]:
+        copy.wait()
+
+
+def own_kernel(
+    block_count, block_cols, tile_tok,
+    index_ref, mask_ref, query_ref, near_ref, far_ref, inner_ref,
+    out_ref, top_ref, sum_ref,
+    own_scores, halo_scores, own_weights, halo_weights,
+):
+    spot = Spot(index_ref[0], block_count, block_cols)
+    width = query_ref.shape[1]
+    channels = out_ref.shape[1]
+    half = 2 * tile_tok
+
+    def flag(tile, row_step, col_step):
+        return mask_ref[2 * tile[0] + tile[1], entry(row_step, col_step)] > 0
+
+    bias = key_bias(
+        [
+            [flag(t, key[0] - t[0], key[1] - t[1]) for t in spot.lane_tiles]
+            for key in spot.key_tiles
+        ],
+        tile_tok,
+    )
+    halo_bias = key_bias(
+        [
+            [flag(t, row - t[0], spot.near_step) for t in spot.lane_tiles[:2]]
+            for row in (spot.edge, spot.rest)
+        ],
+        tile_tok,
+    )
+    places = [tile_rows(tile, tile_tok) for tile in spot.lane_tiles]
+
+    def score(head):
+        lanes = head_lanes(head)
+        query = above(*[query_ref[place, lanes] for place in places])
+        keys = above(near_ref[:, lanes], far_ref[:, lanes])
+        own = biased(contract_last(keys, query), bias, tile_tok)
+        halo = biased(
+            contract_last(inner_ref[:, lanes], query[:half]), halo_bias, tile_tok
+        )
+        own_scores[head] = own
+        halo_scores[head] = halo
+        top = largest(own)
+        top_ref[head : head + 1, :half] = jnp.maximum(top[:, :half], largest(halo))
+        top_ref[head : head + 1, half:] = top[:, half:]
+
+    def soften(head):
+        top = top_ref[head : head + 1]
+        own_weights[head] = softened(own_scores[head], top)
+        halo_weights[head] = softened(halo_scores[head], top[:, :half])
+
+    def weigh(head):
+        where = folded_at(width, channels, head)
+        folded = with_ones(beside(near_ref[where], far_ref[where]))
+        own = contract(folded, own_weights[head])
+        halo = contract(with_ones(inner_ref[where]), halo_weights[head])
+        left = own[:, :half] + halo
+        out_ref[head, :, :half] = left[:channels]
+        out_ref[head, :, half:] = own[:channels, half:]
+        sum_ref[head : head + 1, :half] = left[channels : channels + 1]
+        sum_ref[head : head + 1, half:] = own[channels : channels + 1, half:]
+
+    pipelined(score, soften, weigh)
+
+
+def edge_kernel(
+    block_count, block_cols, tile_tok,
+    index_ref, mask_ref, guest_mask_ref,
+    query_ref, near_ref, far_ref, inner_ref, outer_ref, guest_ref, own_top_ref, own_sum_ref,
+    out_ref, guest_out_ref, side_top_ref, top_ref, sum_ref, send_ref,
+    side_scores, guest_scores, side_weights, guest_weights,
+):
+    spot = Spot(index_ref[0], block_count, block_cols)
+    width = query_ref.shape[1]
+    channels = out_ref.shape[1]
+    half = 2 * tile_tok
+
+    def flag(tile, row_step, col_step):
+        return mask_ref[2 * tile[0] + tile[1], entry(row_step, col_step)] > 0
+
+    def guest_flag(col, col_step):
+        return guest_mask_ref[col, entry(spot.guest_step, col_step)] > 0.5
+
+    never = spot.near < 0
+    bias = key_bias(
+        [
+            [flag(t, row - t[0], spot.far_step) & spot.there for t in spot.lane_tiles[2:]]
+            for row in (spot.rest, spot.edge)
+        ],
+        tile_tok,
+    )
+    guest_bias = key_bias(
+        [
+            [guest_flag(col, key - col) for col in (spot.near, spot.far)]
+            for key in (spot.near, spot.far)
+        ]
+        + [
+            [guest_flag(spot.near, spot.near_step), never],
+            [never, guest_flag(spot.far, spot.far_step) & spot.there],
+        ],
+        tile_tok,
+    )
+    places = [tile_rows(tile, tile_tok) for tile in spot.lane_tiles[2:]]
+    left = lax.broadcasted_iota(jnp.int32, (channels, half), 1) < tile_tok
+
+    def score(head):
+        lanes = head_lanes(head)
+        query = above(*[query_ref[place, lanes] for place in places])
+        scores = biased(contract_last(outer_ref[:, lanes], query), bias, tile_tok)
+        side_scores[head] = scores
+        side_top_ref[head : head + 1] = largest(scores)
+        keys = above(
+            near_ref[:tile_tok, lanes],
+            far_ref[tile_tok:, lanes],
+            inner_ref[:tile_tok, lanes],
+            outer_ref[tile_tok:, lanes],
+        )
+        scores = biased(contract_last(keys, guest_ref[:, lanes]), guest_bias, tile_tok)
+        guest_scores[head] = scores
+        send_ref[2, head : head + 1] = largest(scores)
+
+    def soften(head):
+        side_weights[head] = softened(side_scores[head], side_top_ref[head : head + 1])
+        guest_weights[head] = softened(guest_scores[head], send_ref[2, head : head + 1])
+
+    def weigh(head):
+        where = folded_at(width, channels, head)
+        side = contract(with_ones(outer_ref[where]), side_weights[head])
+        out_ref[head] = side[:channels]
+        sum_ref[head : head + 1, half:] = side[channels : channels + 1]
+        folded = beside(
+            jnp.where(left, near_ref[where], far_ref[where]),
+            jnp.where(left, inner_ref[where], outer_ref[where]),
+        )
+        guest = contract(with_ones(folded), guest_weights[head])
+        guest_out_ref[head] = guest[:channels]
+        send_ref[3, head : head + 1] = guest[channels : channels + 1]
+
+    pipelined(score, soften, weigh)
+
+    near_top = own_top_ref[:, :half]
+    near_sum = own_sum_ref[:, :half]
+    old_top = own_top_ref[:, half:]
+    side_top = side_top_ref[...]
+    far_top = jnp.maximum(old_top, side_top)
+    far_sum = (
+        jnp.exp2((old_top - far_top) * EXP_SCALE) * own_sum_ref[:, half:]
+        + jnp.exp2((side_top - far_top) * EXP_SCALE) * sum_ref[:, half:]
+    )
+    top_ref[:, :half] = near_top
+    top_ref[:, half:] = far_top
+    sum_ref[:, :half] = near_sum
+    sum_ref[:, half:] = far_sum
+    send_ref[0] = beside(near_top[:, tile_tok:], far_top[:, :tile_tok])
+    send_ref[1] = beside(near_sum[:, tile_tok:], far_sum[:, :tile_tok])
+
+
+def shares(near_top, near_sum, away_top, away_sum):
+    top = jnp.maximum(near_top, away_top)
+    near = jnp.exp2((near_top - top) * EXP_SCALE) * near_sum
+    away = jnp.exp2((away_top - top) * EXP_SCALE) * away_sum
+    return top, near + away
+
+
+def centred(values, fill, tile_tok):
+    side = jnp.full((values.shape[0], tile_tok), fill, values.dtype)
+    return jnp.concatenate([side, values, side], axis=1)
+
+
+def blend_kernel(
+    tile_tok,
+    own_out_ref, side_out_ref, guest_out_ref, own_top_ref, side_top_ref,
+    top_ref, sum_ref, sent_ref, got_ref,
+    velocity_ref, guest_velocity_ref,
+):
+    half = 2 * tile_tok
+    top, total = shares(
+        top_ref[...], sum_ref[...],
+        centred(got_ref[2], NEG, tile_tok), centred(got_ref[3], 0.0, tile_tok),
+    )
+    own_share = jnp.exp2((own_top_ref[...] - top) * EXP_SCALE) / total
+    side_share = jnp.exp2((side_top_ref[...] - top[:, half:]) * EXP_SCALE) / total[:, half:]
+    guest_top, guest_total = shares(sent_ref[2], sent_ref[3], got_ref[0], got_ref[1])
+    guest_share = jnp.exp2((sent_ref[2] - guest_top) * EXP_SCALE) / guest_total
+    guest = jnp.zeros(guest_velocity_ref.shape, jnp.float32)
+    near = jnp.zeros(guest_velocity_ref.shape, jnp.float32)
+    far = jnp.zeros(guest_velocity_ref.shape, jnp.float32)
+    for head in range(HEADS):
+        one = slice(head, head + 1)
+        guest = guest + guest_share[one] * guest_out_ref[head]
+        near = near + own_share[one, :half] * own_out_ref[head, :, :half]
+        far = far + own_share[one, half:] * own_out_ref[head, :, half:]
+        far = far + side_share[one] * side_out_ref[head]
+    guest_velocity_ref[...] = guest
+    velocity_ref[:, :half] = near
+    velocity_ref[:, half:] = far
+
+
+def join_kernel(tile_tok, velocity_ref, back_ref, out_ref):
+    out_ref[...] = velocity_ref[...] + centred(back_ref[...], 0.0, tile_tok)
+
+
+def update_kernel(
+    block_count, block_cols, tile_tok, half_size,
+    index_ref, step_ref, velocity_ref, partner_ref, latent_ref,
+    guided_ref, clean_ref, next_ref,
+):
+    spot = Spot(index_ref[0], block_count, block_cols)
+    half = 2 * tile_tok
+    is_cond = index_ref[0] < half_size
+    own = velocity_ref[...]
+    other = partner_ref[...]
+    cond = jnp.where(is_cond, own, other)
+    uncond = jnp.where(is_cond, other, own)
+    blended = uncond + GUIDANCE * (cond - uncond)
+    edge = blended[:, tile_tok : tile_tok + half]
+    rest = jnp.concatenate([blended[:, :tile_tok], blended[:, tile_tok + half :]], axis=1)
+
+    def natural(pair):
+        swapped = jnp.concatenate([pair[:, tile_tok:], pair[:, :tile_tok]], axis=1)
+        return jnp.where(spot.near == 0, pair, swapped)
+
+    edge = natural(edge)
+    rest = natural(rest)
+    moment = jnp.full((1, half), step_ref[0].astype(jnp.float32))
+    sigma_now = flow_sigma(moment)
+    step_size = flow_sigma(moment + 1.0) - sigma_now
+    for row in range(2):
+        lanes = slice(row * half, (row + 1) * half)
+        guided = jnp.where(spot.edge == row, edge, rest)
+        latent = latent_ref[:, lanes]
+        guided_ref[:, lanes] = guided
+        clean_ref[:, lanes] = latent - sigma_now * guided
+        next_ref[:, lanes] = latent + step_size * guided
+
+
+def kernel_call(body, args, outs, smem=0, scratch=(), far=(), stay=True):
+    spaces = [pltpu.SMEM] * smem + [pltpu.VMEM] * (len(args) - smem)
+    for number in far:
+        spaces[number] = pltpu.HBM
+    args = [
+        arg if space == pltpu.SMEM else pltpu.with_memory_space_constraint(arg, space)
+        for arg, space in zip(args, spaces)
+    ]
+    specs = [pl.BlockSpec(memory_space=space) for space in spaces]
+    return pl.pallas_call(
+        body,
+        out_shape=[
+            pltpu.VMEM(shape, dtype) if stay else jax.ShapeDtypeStruct(shape, dtype)
+            for shape, dtype in outs
+        ],
+        in_specs=specs,
+        out_specs=[pl.BlockSpec(memory_space=pltpu.VMEM) for _ in outs],
+        scratch_shapes=list(scratch),
+        compiler_params=pltpu.CompilerParams(vmem_limit_bytes=VMEM_LIMIT),
+    )(*args)
+
+
+def one_frame_tile(frame_count):
+    return frame_count == SH // 2 * (SW // 2) * 2 and SH == 4 and SW % 4 == 0
+
+
+def per_device_plan(query_rows, key_rows, value_rows, tile_mask, head_weight, latent, step_index):
+    frame_count = lax.axis_size("frame")
+    half_size = frame_count // 2
+    block_cols = SW // 2
+    block_count = SH // 2 * block_cols
+    frame_index = lax.axis_index("frame")
+    tok_rows, width = query_rows.shape
+    tile_tok = tok_rows // 4
+    half = 2 * tile_tok
+    channels = head_weight.shape[1]
+    places = range(frame_count)
+    row_pairs = [
+        (f, f + block_cols if f % block_count < block_cols else f - block_cols)
+        for f in places
+    ]
+    mate_pairs = [(f, f + 1 - 2 * (f % 2)) for f in places]
+    side_pairs = []
+    for f in places:
+        step = 2 * (f % 2) - 1
+        if 0 <= f % block_cols + step < block_cols:
+            side_pairs.append((f, f + step))
+    branch_pairs = [(f, (f + half_size) % frame_count) for f in places]
+    sizes = (block_count, block_cols, tile_tok)
+    index = frame_index.astype(jnp.int32).reshape(1)
+    single = jnp.float32
+    packed_type = query_rows.dtype
+
+    (guest_send,) = kernel_call(
+        functools.partial(guest_pack_kernel, *sizes),
+        (index, query_rows),
+        (((half, width), packed_type),),
+        1,
+        (pltpu.SemaphoreType.DMA((2 * PIECES,)),),
+        far=(1,),
+    )
+    guest_send = pltpu.with_memory_space_constraint(guest_send, pltpu.VMEM)
+    guest = lax.ppermute(guest_send, "frame", row_pairs)
+
+    packed = (half, width + (HEADS + 1) // 2 * 2 * channels)
+    near, far = kernel_call(
+        functools.partial(column_pack_kernel, *sizes),
+        (index, key_rows, value_rows, head_weight.T),
+        ((packed, packed_type), (packed, packed_type)),
+        1,
+        (
+            pltpu.VMEM((tok_rows, width), packed_type),
+            pltpu.VMEM((channels, width), packed_type),
+            pltpu.SemaphoreType.DMA((9,)),
+        ),
+        far=(1, 2, 3),
+    )
+    outer = lax.ppermute(far, "frame", side_pairs)
+    inner = lax.ppermute(near, "frame", mate_pairs)
+    edge_row = 1 - frame_index % block_count // block_cols
+    guest_mask = lax.ppermute(
+        lax.dynamic_slice_in_dim(tile_mask, edge_row * 2, 2, 0).astype(single),
+        "frame",
+        row_pairs,
+    )
+    stats = ((HEADS, tok_rows), single)
+    half_stats = ((HEADS, half), single)
+    own_out, own_top, own_sum = kernel_call(
+        functools.partial(own_kernel, *sizes),
+        (index, tile_mask, query_rows, near, far, inner),
+        (((HEADS, channels, tok_rows), single), stats, stats),
+        2,
+        (
+            pltpu.VMEM((HEADS, tok_rows, tok_rows), single),
+            pltpu.VMEM((HEADS, half, half), single),
+            pltpu.VMEM((HEADS, tok_rows, tok_rows), packed_type),
+            pltpu.VMEM((HEADS, half, half), packed_type),
+        ),
+    )
+    half_out = ((HEADS, channels, half), single)
+    side_out, guest_out, side_top, top, total, sent = kernel_call(
+        functools.partial(edge_kernel, *sizes),
+        (
+            index, tile_mask, guest_mask, query_rows, near, far, inner, outer, guest,
+            own_top, own_sum,
+        ),
+        (half_out, half_out, half_stats, stats, stats, ((4, HEADS, half), single)),
+        3,
+        (
+            pltpu.VMEM((HEADS, half, half), single),
+            pltpu.VMEM((HEADS, tok_rows, half), single),
+            pltpu.VMEM((HEADS, half, half), packed_type),
+            pltpu.VMEM((HEADS, tok_rows, half), packed_type),
+        ),
+    )
+    got = lax.ppermute(sent, "frame", row_pairs)
+    velocity, guest_velocity = kernel_call(
+        functools.partial(blend_kernel, tile_tok),
+        (own_out, side_out, guest_out, own_top, side_top, top, total, sent, got),
+        (((channels, tok_rows), single), ((channels, half), single)),
+    )
+    back = lax.ppermute(guest_velocity, "frame", row_pairs)
+    (velocity,) = kernel_call(
+        functools.partial(join_kernel, tile_tok),
+        (velocity, back),
+        (((channels, tok_rows), single),),
+    )
+    partner = lax.ppermute(velocity, "frame", branch_pairs)
+    out = ((channels, tok_rows), single)
+    results = kernel_call(
+        functools.partial(update_kernel, *sizes, half_size),
+        (index, step_index, velocity, partner, latent.T),
+        (out, out, out),
+        2,
+        stay=False,
+    )
+    return tuple(result.T for result in results)
+
+
+def per_device(*args):
+    return per_device_plan(*args)
+
+
 def solution(mesh):
     placed = (
         P(("groups", "frame"), None),
@@ -177,8 +726,9 @@
         P(("groups", "frame"), None),
         P("groups"),
     )
+    fast = one_frame_tile(mesh.shape["frame"])
     return jax.shard_map(
-        per_device,
+        per_device if fast else per_device_frames,
         mesh=mesh,
         in_specs=placed,
         out_specs=(

time: 662 us -> 44 us (0.07); the launches traced: 654 us -> 43.7 us
  waiting for transfers between devices: 259 us -> 16.9 us
  starting transfers between devices: 193 us -> 12.4 us
  matrix products: 87.9 us -> 0 us
  local copies, waits for them, and re-layouts: 85.6 us -> 0.02 us
  other arithmetic: 25.3 us -> 0.01 us
  Pallas kernels: 0 us -> 13 us
    ppermute x18 -> x7, waiting for transfers between devices: 259 us -> 16.9 us  [the longest x1 10.6 us: per_device_plan(): lax.ppermute(lax.dynamic_slice_in_dim(tile_mask, edge_row * 2, 2, 0).asty...]
    ppermute x18 -> x7, starting transfers between devices: 193 us -> 12.4 us  [the longest x1 2.86 us: per_device_plan(): partner = lax.ppermute(velocity, 'frame', branch_pairs)]
    sub x20 -> x0, matrix products: 62.3 us -> none  [one_head(): shifted = jnp.where(mask_full, jnp.exp(scores - row_max), 0.0)]
    another operation x20 -> x0, local copies, waits for them, and re-layouts: 47.8 us -> none  [one_head(): jnp.stack([part[row_local:row_local + 3, col_local:col_local + 3] for par...]
    while x40 -> x0, local copies, waits for them, and re-layouts: 25.9 us -> none
    dot_general x21 -> x0, matrix products: 25.6 us -> none  [the longest x20 23.7 us: one_head(): jnp.einsum('qtk,qkd->qtd', weights, value_tiles, preferred_element_type=j...]
    concatenate x2 -> x0, other arithmetic: 16.7 us -> none  [direct_window(): planes.append(jnp.concatenate(row_parts, axis=0))]
    pallas_call x0 -> x7, Pallas kernels: none -> 13 us  [kernel_call(): pl.pallas_call(body, out_shape=[pltpu.VMEM(shape, dtype) if stay else jax...]
  transfers between devices with their start and end apart: 18 -> 7, of which waited for: 5 -> 4; matrix products, arithmetic and copies ran while one was open for 2% -> 0% of each run, Pallas kernels for 0% -> 13%
where the time goes in v2:
time: 44 us; the launch traced here: 43.7 us
  waiting for transfers between devices  16.9 us (38%)
  Pallas kernels  13 us (30%)
  starting transfers between devices  12.4 us (28%)
  between operations  1.34 us (3%)
    pallas_call x7, Pallas kernels, kernel_call(): pl.pallas_call(body, out_shape=[pltpu.VMEM(shape, dtype) if stay else jax...  13 us
    ppermute x1, waiting for transfers between devices, per_device_plan(): lax.ppermute(lax.dynamic_slice_in_dim(tile_mask, edge_row * 2, 2, 0).asty...  10.6 us
    ppermute x1, starting transfers between devices, per_device_plan(): partner = lax.ppermute(velocity, 'frame', branch_pairs)  2.86 us
    ppermute x1, starting transfers between devices, per_device_plan(): guest = lax.ppermute(guest_send, 'frame', row_pairs)  2.79 us
    ppermute x1, waiting for transfers between devices, per_device_plan(): got = lax.ppermute(sent, 'frame', row_pairs)  2.54 us
    ppermute x1, starting transfers between devices, per_device_plan(): got = lax.ppermute(sent, 'frame', row_pairs)  2.52 us
    ppermute x1, waiting for transfers between devices, per_device_plan(): back = lax.ppermute(guest_velocity, 'frame', row_pairs)  2.07 us
    ppermute x1, starting transfers between devices, per_device_plan(): back = lax.ppermute(guest_velocity, 'frame', row_pairs)  1.91 us
  transfers between devices with their start and end apart: 7, of which 4 were waited for; matrix products, arithmetic and copies ran while one was open for 0% of the time, Pallas kernels for 13%

profile of v2, /device:TPU:0, one launch (start us, length us, event | category | flops | bytes accessed | tf_op | source)
XLA Modules:
  0.0 43.7 jit_solution(8348481622658434116)
XLA Ops:
  0.6 2.0 %shard_map.94 = (bf16[128,3840]{1,0:T(8,128)(2,1)S(1)}, bf16[128,3840]{1,0:T(8,128)(2,1)S(1)}) custom-call(s32[1]{0:T(128)} %bitcast.index_ref, bf16[256,2560]{1,0:T(8,128)(2,1)} %key_ref.1, bf16[256,2560]{1,0:T(8,128)(2,1)} %value_ref.1, bf16[64,2560]{1,0:T(8,128)(2,1)} %bitcast.7), custom_call_target="tpu_custom_call" | custom-call | tf_op jit(solution)/shard_map/pallas_call | solution.py:585
  2.7 0.0 copy-start.2
  2.7 0.0 copy-start
  2.7 0.5 %collective-permute-start = (bf16[128,3840]{1,0:T(8,128)(2,1)S(1)}, bf16[128,3840]{1,0:T(8,128)(2,1)}, u32[]{:S(2)}, u32[]{:S(2)}) collective-permute-start(bf16[128,3840]{1,0:T(8,128)(2,1)S(1)} %get-tuple-element.19.near_ref), channel_id=1, source_target_pairs={{0,1},{1,0},{2,3},{3,2},{4,5},{5,4},{6,7},{7,6},{8,9},{9,8},{10,11... | collective-permute-start | bytes 2949128 | tf_op jit(solution)/shard_map/ppermute | solution.py:654
  3.3 1.7 %collective-permute-start.2 = (bf16[128,3840]{1,0:T(8,128)(2,1)S(1)}, bf16[128,3840]{1,0:T(8,128)(2,1)}, u32[]{:S(2)}, u32[]{:S(2)}) collective-permute-start(bf16[128,3840]{1,0:T(8,128)(2,1)S(1)} %get-tuple-element.20.far_ref), channel_id=1, source_target_pairs={{1,2},{2,1},{5,6},{6,5},{9,10},{10,9},{13,14},{14,13},{17,18},{18,... | collective-permute-start | bytes 2949128 | tf_op jit(solution)/shard_map/ppermute | solution.py:653
  4.9 2.1 %shard_map.96 = bf16[128,2560]{1,0:T(8,128)(2,1)} custom-call(s32[1]{0:T(128)} %bitcast.index_ref, bf16[256,2560]{1,0:T(8,128)(2,1)} %query_ref.5), custom_call_target="tpu_custom_call" | custom-call | tf_op jit(solution)/shard_map/pallas_call | solution.py:585
  7.0 2.8 %collective-permute-start.3 = (bf16[128,2560]{1,0:T(8,128)(2,1)}, bf16[128,2560]{1,0:T(8,128)(2,1)}, u32[]{:S(2)}, u32[]{:S(2)}) collective-permute-start(bf16[128,2560]{1,0:T(8,128)(2,1)} %shard_map.96), channel_id=1, source_target_pairs={{0,4},{1,5},{2,6},{3,7},{4,0},{5,1},{6,2},{7,3},{8,12},{9,13},{10,... | collective-permute-start | bytes 1966088 | tf_op jit(solution)/shard_map/ppermute | solution.py:638
  9.8 0.0 copy-done.2
  9.8 0.1 collective-permute-start.1
  10.0 0.0 collective-permute-done.inner_ref
  10.0 0.0 copy-done
  10.0 3.8 %shard_map.95 = (f32[20,64,256]{2,1,0:T(8,128)S(1)}, f32[20,256]{1,0:T(8,128)S(1)}, f32[20,256]{1,0:T(8,128)S(1)}) custom-call(s32[1]{0:T(128)} %bitcast.index_ref, s32[4,27]{1,0:T(4,128)S(1)} %copy-done.2, bf16[256,2560]{1,0:T(8,128)(2,1)S(1)} %copy-done, bf16[128,3840]{1,0:T(8,128)(2,1)S(1)} %get-tuple-element.19.near_ref, ...), custom_call_target="tpu_custom_call" | custom-call | tf_op jit(solution)/shard_map/pallas_call | solution.py:585
  13.7 10.6 %collective-permute-done.1.guest_mask_ref = f32[2,27]{1,0:T(2,128)S(1)} collective-permute-done((f32[2,27]{1,0:T(2,128)S(1)}, f32[2,27]{1,0:T(2,128)S(1)}, u32[]{:S(2)}, u32[]{:S(2)}) %collective-permute-start.1) | collective-permute-done | bytes 248 | tf_op jit(solution)/shard_map/ppermute | solution.py:656
  24.4 0.0 collective-permute-done.3.guest_ref
  24.4 0.0 collective-permute-done.2.outer_ref
  24.4 3.8 %shard_map.97 = (f32[20,64,128]{2,1,0:T(8,128)S(1)}, f32[20,64,128]{2,1,0:T(8,128)S(1)}, f32[20,128]{1,0:T(8,128)S(1)}, f32[20,256]{1,0:T(8,128)S(1)}, f32[20,256]{1,0:T(8,128)S(1)}, /*index=5*/f32[4,20,128]{2,1,0:T(8,128)S(1)}) custom-call(s32[1]{0:T(128)} %bitcast.index_ref, s32[4,27]{1,0:T(4,128)S(1)} %copy-done.2, ...), custom_call_target="tpu_custom_call" | custom-call | tf_op jit(solution)/shard_map/pallas_call | solution.py:585
  28.2 2.5 %collective-permute-start.4 = (f32[4,20,128]{2,1,0:T(8,128)S(1)}, f32[4,20,128]{2,1,0:T(8,128)S(1)}, u32[]{:S(2)}, u32[]{:S(2)}) collective-permute-start(f32[4,20,128]{2,1,0:T(8,128)S(1)} %get-tuple-element.29.sent_ref), channel_id=1, source_target_pairs={{0,4},{1,5},{2,6},{3,7},{4,0},{5,1},{6,2},{7,3},{8,12},{9,13},{10,... | collective-permute-start | bytes 122888 | tf_op jit(solution)/shard_map/ppermute | solution.py:691
  30.7 2.5 %collective-permute-done.4.got_ref = f32[4,20,128]{2,1,0:T(8,128)S(1)} collective-permute-done((f32[4,20,128]{2,1,0:T(8,128)S(1)}, f32[4,20,128]{2,1,0:T(8,128)S(1)}, u32[]{:S(2)}, u32[]{:S(2)}) %collective-permute-start.4) | collective-permute-done | bytes 40992 | tf_op jit(solution)/shard_map/ppermute | solution.py:691
  33.2 0.0 copy-start.1
  33.2 0.3 shard_map.98
  33.5 1.9 %collective-permute-start.5 = (f32[64,128]{1,0:T(8,128)S(1)}, f32[64,128]{1,0:T(8,128)S(1)}, u32[]{:S(2)}, u32[]{:S(2)}) collective-permute-start(f32[64,128]{1,0:T(8,128)S(1)} %get-tuple-element.31), channel_id=1, source_target_pairs={{0,4},{1,5},{2,6},{3,7},{4,0},{5,1},{6,2},{7,3},{8,12},{9,13},{10,... | collective-permute-start | bytes 98312 | tf_op jit(solution)/shard_map/ppermute | solution.py:697
  35.4 2.1 %collective-permute-done.5.back_ref = f32[64,128]{1,0:T(8,128)S(1)} collective-permute-done((f32[64,128]{1,0:T(8,128)S(1)}, f32[64,128]{1,0:T(8,128)S(1)}, u32[]{:S(2)}, u32[]{:S(2)}) %collective-permute-start.5) | collective-permute-done | bytes 32800 | tf_op jit(solution)/shard_map/ppermute | solution.py:697
  37.5 0.1 shard_map.99.velocity_ref
  37.6 2.9 %collective-permute-start.6 = (f32[64,256]{1,0:T(8,128)S(1)}, f32[64,256]{1,0:T(8,128)S(1)}, u32[]{:S(2)}, u32[]{:S(2)}) collective-permute-start(f32[64,256]{1,0:T(8,128)S(1)} %shard_map.99.velocity_ref), channel_id=1, source_target_pairs={{0,8},{1,9},{2,10},{3,11},{4,12},{5,13},{6,14},{7,15},{8,0},{9,1},... | collective-permute-start | bytes 196616 | tf_op jit(solution)/shard_map/ppermute | solution.py:703
  41.1 1.7 %collective-permute-done.6.partner_ref = f32[64,256]{1,0:T(8,128)S(1)} collective-permute-done((f32[64,256]{1,0:T(8,128)S(1)}, f32[64,256]{1,0:T(8,128)S(1)}, u32[]{:S(2)}, u32[]{:S(2)}) %collective-permute-start.6) | collective-permute-done | bytes 65568 | tf_op jit(solution)/shard_map/ppermute | solution.py:703
  42.7 0.0 copy-done.1
  42.7 1.0 %shard_map.100 = (f32[64,256]{1,0:T(8,128)}, f32[64,256]{1,0:T(8,128)}, f32[64,256]{1,0:T(8,128)}) custom-call(s32[1]{0:T(128)} %bitcast.index_ref, s32[1]{0:T(128)S(6)} %copy.10.step_ref, f32[64,256]{1,0:T(8,128)S(1)} %shard_map.99.velocity_ref, f32[64,256]{1,0:T(8,128)S(1)} %collective-permute-done.6.partner_ref, f32[64,256]{1,0:T(8,128)S(1)} %bitcast.6), custom_call_target="tpu_custom_call" | custom-call | tf_op jit(solution)/shard_map/pallas_call | solution.py:585
  (1 shorter events, 0.0 us)
Async XLA Ops:
  2.7 7.1 %copy-start.2 = (s32[4,27]{1,0:T(4,128)S(1)}, s32[4,27]{1,0:T(4,128)}, u32[]{:S(2)}) copy-start(s32[4,27]{1,0:T(4,128)} %mask_ref.3) | copy-start | bytes 1300
  2.7 7.3 %copy-start = (bf16[256,2560]{1,0:T(8,128)(2,1)S(1)}, bf16[256,2560]{1,0:T(8,128)(2,1)}, u32[]{:S(2)}) copy-start(bf16[256,2560]{1,0:T(8,128)(2,1)} %query_ref.5) | copy-start | bytes 3932164
  2.7 7.3 %collective-permute-start = (bf16[128,3840]{1,0:T(8,128)(2,1)S(1)}, bf16[128,3840]{1,0:T(8,128)(2,1)}, u32[]{:S(2)}, u32[]{:S(2)}) collective-permute-start(bf16[128,3840]{1,0:T(8,128)(2,1)S(1)} %get-tuple-element.19.near_ref), channel_id=1, source_target_pairs={{0,1},{1,0},{2,3},{3,2},{4,5},{5,4},{6,7},{7,6},{8,9},{9,8},{10,11... | collective-permute-start | bytes 2949128 | tf_op jit(solution)/shard_map/ppermute | solution.py:654
  3.3 21.1 %collective-permute-start.2 = (bf16[128,3840]{1,0:T(8,128)(2,1)S(1)}, bf16[128,3840]{1,0:T(8,128)(2,1)}, u32[]{:S(2)}, u32[]{:S(2)}) collective-permute-start(bf16[128,3840]{1,0:T(8,128)(2,1)S(1)} %get-tuple-element.20.far_ref), channel_id=1, source_target_pairs={{1,2},{2,1},{5,6},{6,5},{9,10},{10,9},{13,14},{14,13},{17,18},{18,... | collective-permute-start | bytes 2949128 | tf_op jit(solution)/shard_map/ppermute | solution.py:653
  7.0 17.3 %collective-permute-start.3 = (bf16[128,2560]{1,0:T(8,128)(2,1)}, bf16[128,2560]{1,0:T(8,128)(2,1)}, u32[]{:S(2)}, u32[]{:S(2)}) collective-permute-start(bf16[128,2560]{1,0:T(8,128)(2,1)} %shard_map.96), channel_id=1, source_target_pairs={{0,4},{1,5},{2,6},{3,7},{4,0},{5,1},{6,2},{7,3},{8,12},{9,13},{10,... | collective-permute-start | bytes 1966088 | tf_op jit(solution)/shard_map/ppermute | solution.py:638
  9.8 14.5 %collective-permute-start.1 = (f32[2,27]{1,0:T(2,128)S(1)}, f32[2,27]{1,0:T(2,128)S(1)}, u32[]{:S(2)}, u32[]{:S(2)}) collective-permute-start(f32[2,27]{1,0:T(2,128)S(1)} %dynamic-slice_convert_fusion), channel_id=1, source_target_pairs={{0,4},{1,5},{2,6},{3,7},{4,0},{5,1},{6,2},{7,3},{8,12},{9,13},{10,... | collective-permute-start | bytes 656 | tf_op jit(solution)/shard_map/ppermute | solution.py:656
  28.2 5.1 %collective-permute-start.4 = (f32[4,20,128]{2,1,0:T(8,128)S(1)}, f32[4,20,128]{2,1,0:T(8,128)S(1)}, u32[]{:S(2)}, u32[]{:S(2)}) collective-permute-start(f32[4,20,128]{2,1,0:T(8,128)S(1)} %get-tuple-element.29.sent_ref), channel_id=1, source_target_pairs={{0,4},{1,5},{2,6},{3,7},{4,0},{5,1},{6,2},{7,3},{8,12},{9,13},{10,... | collective-permute-start | bytes 122888 | tf_op jit(solution)/shard_map/ppermute | solution.py:691
  33.2 9.5 %copy-start.1 = (f32[256,64]{0,1:T(8,128)S(1)}, f32[256,64]{0,1:T(8,128)}, u32[]{:S(2)}) copy-start(f32[256,64]{0,1:T(8,128)} %param.12) | copy-start | bytes 196612
  33.5 4.0 %collective-permute-start.5 = (f32[64,128]{1,0:T(8,128)S(1)}, f32[64,128]{1,0:T(8,128)S(1)}, u32[]{:S(2)}, u32[]{:S(2)}) collective-permute-start(f32[64,128]{1,0:T(8,128)S(1)} %get-tuple-element.31), channel_id=1, source_target_pairs={{0,4},{1,5},{2,6},{3,7},{4,0},{5,1},{6,2},{7,3},{8,12},{9,13},{10,... | collective-permute-start | bytes 98312 | tf_op jit(solution)/shard_map/ppermute | solution.py:697
  37.6 5.2 %collective-permute-start.6 = (f32[64,256]{1,0:T(8,128)S(1)}, f32[64,256]{1,0:T(8,128)S(1)}, u32[]{:S(2)}, u32[]{:S(2)}) collective-permute-start(f32[64,256]{1,0:T(8,128)S(1)} %shard_map.99.velocity_ref), channel_id=1, source_target_pairs={{0,8},{1,9},{2,10},{3,11},{4,12},{5,13},{6,14},{7,15},{8,0},{9,1},... | collective-permute-start | bytes 196616 | tf_op jit(solution)/shard_map/ppermute | solution.py:703

commit v3 on v2

--- a/solution.py
+++ b/solution.py
@@ -173,7 +173,7 @@
 
 NEG = -1e30
 VMEM_LIMIT = 16 << 20
-PIECES = 4
+FIRST_HEADS = 14
 EXP_SCALE = math.log2(math.e) / math.sqrt(HD)
 
 
@@ -192,8 +192,9 @@
 
 
 class Spot:
-    def __init__(self, index, block_count, block_cols):
-        spot = index % block_count
+    def __init__(self, block_count, block_cols):
+        self.index = lax.axis_index("frame")
+        spot = self.index % block_count
         block_row = spot // block_cols
         block_col = spot % block_cols
         odd = block_col % 2
@@ -271,17 +272,41 @@
     return above(folded, jnp.ones((16, folded.shape[1]), folded.dtype))
 
 
-def pipelined(*stages):
-    for turn in range(HEADS + len(stages) - 1):
+def pipelined(heads, *stages):
+    for turn in range(len(heads) + len(stages) - 1):
         for number, stage in enumerate(stages):
-            if 0 <= turn - number < HEADS:
-                stage(turn - number)
-
-
-def folded_at(width, channels, head):
-    row = head % 2 * channels
-    lane = width + head // 2 * 2 * channels
-    return slice(row, row + channels), slice(lane, lane + 2 * channels)
+            if 0 <= turn - number < len(heads):
+                stage(heads[turn - number])
+
+
+def packed_width(heads, channels):
+    return heads * HD + (heads + 1) // 2 * 2 * channels
+
+
+class Column:
+    def __init__(self, refs, groups, channels):
+        self.refs = refs
+        self.groups = groups
+        self.channels = channels
+
+    def place(self, head):
+        for ref, group in zip(self.refs, self.groups):
+            if head in group:
+                return ref, head - group.start, len(group) * HD
+
+    def keys(self, head):
+        ref, local, _ = self.place(head)
+        return ref[:, head_lanes(local)]
+
+    def folded_at(self, head):
+        ref, local, width = self.place(head)
+        row = local % 2 * self.channels
+        lane = width + local // 2 * 2 * self.channels
+        return ref, (slice(row, row + self.channels), slice(lane, lane + 2 * self.channels))
+
+    def folded(self, head):
+        ref, where = self.folded_at(head)
+        return ref[where]
 
 
 def copied(pairs, sems):
@@ -294,61 +319,82 @@
     return copies
 
 
-def piece(rows, start, stop):
-    return pl.ds(pl.multiple_of(rows.start + start, stop - start), stop - start)
-
-
-def guest_pack_kernel(block_count, block_cols, tile_tok, index_ref, query_ref, out_ref, sems):
-    spot = Spot(index_ref[0], block_count, block_cols)
-    step = tile_tok // PIECES
-    pairs = []
-    for number, col in enumerate((spot.near, spot.far)):
-        rows = tile_rows((spot.edge, col), tile_tok)
-        for start in range(0, tile_tok, step):
-            source = query_ref.at[piece(rows, start, start + step)]
-            pairs.append((source, out_ref.at[pl.ds(number * tile_tok + start, step)]))
+def guest_pack_kernel(
+    block_count, block_cols, tile_tok, groups,
+    query_ref, mask_ref, weight_ref, *refs
+):
+    spot = Spot(block_count, block_cols)
+    *out_refs, bias_ref, near_weight_ref, mask, sems = refs
+    pairs = [(mask_ref, mask), (weight_ref, near_weight_ref)]
+    for out_ref, group in zip(out_refs, groups):
+        lanes = pl.ds(group.start * HD, len(group) * HD)
+        for number, col in enumerate((spot.near, spot.far)):
+            rows = tile_rows((spot.edge, col), tile_tok)
+            target = out_ref.at[pl.ds(number * tile_tok, tile_tok)]
+            pairs.append((query_ref.at[rows, lanes], target))
     for copy in copied(pairs, sems):
         copy.wait()
+    steps = -spot.guest_step
+
+    def flag(col, col_step):
+        return mask[2 * spot.edge + col, entry(steps, col_step)] > 0
+
+    never = spot.near < 0
+    cols = (spot.near, spot.far)
+    rows = [[flag(col, key - col) for col in cols] for key in cols] + [
+        [flag(spot.near, spot.near_step), never],
+        [never, flag(spot.far, spot.far_step) & spot.there],
+    ]
+    for number, row in enumerate(key_bias(rows, tile_tok)):
+        bias_ref[number : number + 1] = row
 
 
 def column_pack_kernel(
-    block_count, block_cols, tile_tok,
-    index_ref, key_ref, value_ref, weight_ref, near_ref, far_ref, values, weight, sems,
+    block_count, block_cols, tile_tok, groups, key_ref, value_ref, weight_ref, *refs
 ):
-    spot = Spot(index_ref[0], block_count, block_cols)
-    channels, width = weight_ref.shape
-    half = 2 * tile_tok
-    pairs = [(weight_ref, weight)]
-    for number, tile in enumerate(spot.key_tiles):
-        rows = pl.ds(number * tile_tok, tile_tok)
-        pairs.append((value_ref.at[tile_rows(tile, tile_tok)], values.at[rows]))
-    for number, tile in enumerate(spot.key_tiles):
-        out_ref = (near_ref, far_ref)[number // 2]
-        target = out_ref.at[pl.ds(number % 2 * tile_tok, tile_tok), pl.ds(0, width)]
-        pairs.append((key_ref.at[tile_rows(tile, tile_tok)], target))
+    spot = Spot(block_count, block_cols)
+    channels = weight_ref.shape[0]
+    *far_refs, near_ref, sems = refs[-2 - len(groups) :]
+    sides = (
+        (spot.key_tiles[2:], far_refs, groups),
+        (spot.key_tiles[:2], [near_ref], (range(HEADS),)),
+    )
+    pairs = []
+    for tiles, out_refs, out_groups in sides:
+        for out_ref, group in zip(out_refs, out_groups):
+            width = len(group) * HD
+            for number, tile in enumerate(tiles):
+                source = key_ref.at[tile_rows(tile, tile_tok), pl.ds(group.start * HD, width)]
+                target = out_ref.at[pl.ds(number * tile_tok, tile_tok), pl.ds(0, width)]
+                pairs.append((source, target))
     copies = copied(pairs, sems)
-    for copy in copies[:5]:
+    for tiles, out_refs, out_groups in sides:
+        column = Column(out_refs, out_groups, channels)
+        places = [tile_rows(tile, tile_tok) for tile in tiles]
+        for head in range(HEADS):
+            lanes = head_lanes(head)
+            values = above(*[value_ref[place, lanes] for place in places])
+            folded = contract_last(weight_ref[:, lanes], values)
+            ref, where = column.folded_at(head)
+            ref[where] = folded.astype(jnp.bfloat16)
+    for copy in copies:
         copy.wait()
-    for head in range(HEADS):
-        lanes = head_lanes(head)
-        folded = contract_last(weight[:, lanes], values[:, lanes]).astype(jnp.bfloat16)
-        where = folded_at(width, channels, head)
-        near_ref[where] = folded[:, :half]
-        far_ref[where] = folded[:, half:]
-    for copy in copies[5:]:
-        copy.wait()
 
 
 def own_kernel(
-    block_count, block_cols, tile_tok,
-    index_ref, mask_ref, query_ref, near_ref, far_ref, inner_ref,
-    out_ref, top_ref, sum_ref,
-    own_scores, halo_scores, own_weights, halo_weights,
+    block_count, block_cols, tile_tok, groups, mask_ref, query_ref, *refs
 ):
-    spot = Spot(index_ref[0], block_count, block_cols)
-    width = query_ref.shape[1]
+    count = len(groups)
+    far_refs = refs[1 : 1 + count]
+    out_ref, top_ref, sum_ref, side_bias_ref = refs[2 + count : 6 + count]
+    own_scores, halo_scores, own_weights, halo_weights = refs[6 + count :]
+    spot = Spot(block_count, block_cols)
     channels = out_ref.shape[1]
     half = 2 * tile_tok
+    every = (range(HEADS),)
+    near_column = Column(refs[:1], every, channels)
+    far_column = Column(far_refs, groups, channels)
+    inner_column = Column(refs[1 + count : 2 + count], every, channels)
 
     def flag(tile, row_step, col_step):
         return mask_ref[2 * tile[0] + tile[1], entry(row_step, col_step)] > 0
@@ -367,15 +413,21 @@
         ],
         tile_tok,
     )
+    side_rows = [
+        [flag(t, row - t[0], spot.far_step) & spot.there for t in spot.lane_tiles[2:]]
+        for row in (spot.rest, spot.edge)
+    ]
+    for number, row in enumerate(key_bias(side_rows, tile_tok)):
+        side_bias_ref[number : number + 1] = row
     places = [tile_rows(tile, tile_tok) for tile in spot.lane_tiles]
 
     def score(head):
         lanes = head_lanes(head)
         query = above(*[query_ref[place, lanes] for place in places])
-        keys = above(near_ref[:, lanes], far_ref[:, lanes])
+        keys = above(near_column.keys(head), far_column.keys(head))
         own = biased(contract_last(keys, query), bias, tile_tok)
         halo = biased(
-            contract_last(inner_ref[:, lanes], query[:half]), halo_bias, tile_tok
+            contract_last(inner_column.keys(head), query[:half]), halo_bias, tile_tok
         )
         own_scores[head] = own
         halo_scores[head] = halo
@@ -389,102 +441,82 @@
         halo_weights[head] = softened(halo_scores[head], top[:, :half])
 
     def weigh(head):
-        where = folded_at(width, channels, head)
-        folded = with_ones(beside(near_ref[where], far_ref[where]))
+        folded = with_ones(beside(near_column.folded(head), far_column.folded(head)))
         own = contract(folded, own_weights[head])
-        halo = contract(with_ones(inner_ref[where]), halo_weights[head])
+        halo = contract(with_ones(inner_column.folded(head)), halo_weights[head])
         left = own[:, :half] + halo
         out_ref[head, :, :half] = left[:channels]
         out_ref[head, :, half:] = own[:channels, half:]
         sum_ref[head : head + 1, :half] = left[channels : channels + 1]
         sum_ref[head : head + 1, half:] = own[channels : channels + 1, half:]
 
-    pipelined(score, soften, weigh)
+    pipelined(range(HEADS), score, soften, weigh)
 
 
 def edge_kernel(
-    block_count, block_cols, tile_tok,
-    index_ref, mask_ref, guest_mask_ref,
+    block_count, block_cols, tile_tok, group,
+    side_bias_ref, guest_bias_ref,
     query_ref, near_ref, far_ref, inner_ref, outer_ref, guest_ref, own_top_ref, own_sum_ref,
     out_ref, guest_out_ref, side_top_ref, top_ref, sum_ref, send_ref,
     side_scores, guest_scores, side_weights, guest_weights,
 ):
-    spot = Spot(index_ref[0], block_count, block_cols)
-    width = query_ref.shape[1]
+    spot = Spot(block_count, block_cols)
     channels = out_ref.shape[1]
     half = 2 * tile_tok
-
-    def flag(tile, row_step, col_step):
-        return mask_ref[2 * tile[0] + tile[1], entry(row_step, col_step)] > 0
-
-    def guest_flag(col, col_step):
-        return guest_mask_ref[col, entry(spot.guest_step, col_step)] > 0.5
-
-    never = spot.near < 0
-    bias = key_bias(
-        [
-            [flag(t, row - t[0], spot.far_step) & spot.there for t in spot.lane_tiles[2:]]
-            for row in (spot.rest, spot.edge)
-        ],
-        tile_tok,
-    )
-    guest_bias = key_bias(
-        [
-            [guest_flag(col, key - col) for col in (spot.near, spot.far)]
-            for key in (spot.near, spot.far)
-        ]
-        + [
-            [guest_flag(spot.near, spot.near_step), never],
-            [never, guest_flag(spot.far, spot.far_step) & spot.there],
-        ],
-        tile_tok,
-    )
+    near_column = Column([near_ref], (range(HEADS),), channels)
+    inner_column = Column([inner_ref], (range(HEADS),), channels)
+    far_column = Column([far_ref], (group,), channels)
+    outer_column = Column([outer_ref], (group,), channels)
+
+    bias = [side_bias_ref[number : number + 1] for number in range(2)]
+    guest_bias = [guest_bias_ref[number : number + 1] for number in range(4)]
     places = [tile_rows(tile, tile_tok) for tile in spot.lane_tiles[2:]]
     left = lax.broadcasted_iota(jnp.int32, (channels, half), 1) < tile_tok
 
     def score(head):
-        lanes = head_lanes(head)
-        query = above(*[query_ref[place, lanes] for place in places])
-        scores = biased(contract_last(outer_ref[:, lanes], query), bias, tile_tok)
-        side_scores[head] = scores
-        side_top_ref[head : head + 1] = largest(scores)
+        row = head - group.start
+        query = above(*[query_ref[place, head_lanes(head)] for place in places])
+        scores = biased(contract_last(outer_column.keys(head), query), bias, tile_tok)
+        side_scores[row] = scores
+        side_top_ref[row : row + 1] = largest(scores)
         keys = above(
-            near_ref[:tile_tok, lanes],
-            far_ref[tile_tok:, lanes],
-            inner_ref[:tile_tok, lanes],
-            outer_ref[tile_tok:, lanes],
+            near_column.keys(head)[:tile_tok],
+            far_column.keys(head)[tile_tok:],
+            inner_column.keys(head)[:tile_tok],
+            outer_column.keys(head)[tile_tok:],
         )
-        scores = biased(contract_last(keys, guest_ref[:, lanes]), guest_bias, tile_tok)
-        guest_scores[head] = scores
-        send_ref[2, head : head + 1] = largest(scores)
+        scores = contract_last(keys, guest_ref[:, head_lanes(row)])
+        scores = biased(scores, guest_bias, tile_tok)
+        guest_scores[row] = scores
+        send_ref[2, row : row + 1] = largest(scores)
 
     def soften(head):
-        side_weights[head] = softened(side_scores[head], side_top_ref[head : head + 1])
-        guest_weights[head] = softened(guest_scores[head], send_ref[2, head : head + 1])
+        row = head - group.start
+        side_weights[row] = softened(side_scores[row], side_top_ref[row : row + 1])
+        guest_weights[row] = softened(guest_scores[row], send_ref[2, row : row + 1])
 
     def weigh(head):
-        where = folded_at(width, channels, head)
-        side = contract(with_ones(outer_ref[where]), side_weights[head])
-        out_ref[head] = side[:channels]
-        sum_ref[head : head + 1, half:] = side[channels : channels + 1]
+        row = head - group.start
+        side = contract(with_ones(outer_column.folded(head)), side_weights[row])
+        out_ref[row] = side[:channels]
+        sum_ref[row : row + 1, half:] = side[channels : channels + 1]
         folded = beside(
-            jnp.where(left, near_ref[where], far_ref[where]),
-            jnp.where(left, inner_ref[where], outer_ref[where]),
+            jnp.where(left, near_column.folded(head), far_column.folded(head)),
+            jnp.where(left, inner_column.folded(head), outer_column.folded(head)),
         )
-        guest = contract(with_ones(folded), guest_weights[head])
-        guest_out_ref[head] = guest[:channels]
-        send_ref[3, head : head + 1] = guest[channels : channels + 1]
-
-    pipelined(score, soften, weigh)
-
-    near_top = own_top_ref[:, :half]
-    near_sum = own_sum_ref[:, :half]
-    old_top = own_top_ref[:, half:]
+        guest = contract(with_ones(folded), guest_weights[row])
+        guest_out_ref[row] = guest[:channels].astype(guest_out_ref.dtype)
+        send_ref[3, row : row + 1] = guest[channels : channels + 1]
+
+    pipelined(group, score, soften, weigh)
+
+    mine = slice(group.start, group.stop)
+    near_top = own_top_ref[mine, :half]
+    near_sum = own_sum_ref[mine, :half]
+    old_top = own_top_ref[mine, half:]
     side_top = side_top_ref[...]
-    far_top = jnp.maximum(old_top, side_top)
-    far_sum = (
-        jnp.exp2((old_top - far_top) * EXP_SCALE) * own_sum_ref[:, half:]
-        + jnp.exp2((side_top - far_top) * EXP_SCALE) * sum_ref[:, half:]
+    far_top, far_sum = shares(
+        old_top, own_sum_ref[mine, half:], side_top, sum_ref[:, half:]
     )
     top_ref[:, :half] = near_top
     top_ref[:, half:] = far_top
@@ -506,47 +538,75 @@
     return jnp.concatenate([side, values, side], axis=1)
 
 
-def blend_kernel(
-    tile_tok,
-    own_out_ref, side_out_ref, guest_out_ref, own_top_ref, side_top_ref,
-    top_ref, sum_ref, sent_ref, got_ref,
-    velocity_ref, guest_velocity_ref,
-):
+def guest_blend_kernel(guest_out_ref, sent_ref, got_ref, late_ref, back_ref):
+    heads, channels, _ = guest_out_ref.shape
+    top, total = shares(sent_ref[2], sent_ref[3], got_ref[0], got_ref[1])
+    share = jnp.exp2((sent_ref[2] - top) * EXP_SCALE) / total
+    velocity = jnp.zeros(guest_out_ref.shape[1:], jnp.float32)
+    for row in range(heads):
+        velocity = velocity + share[row : row + 1] * guest_out_ref[row]
+    back_ref[:channels] = velocity
+    late = late_ref.shape[1]
+    back_ref[channels : channels + late] = late_ref[2]
+    back_ref[channels + late : channels + 2 * late] = late_ref[3]
+
+
+def own_part(tile_tok, group, own_out_ref, side_out_ref, own_top_ref, side_top_ref,
+             top, total, far_top, far_total):
     half = 2 * tile_tok
     top, total = shares(
-        top_ref[...], sum_ref[...],
-        centred(got_ref[2], NEG, tile_tok), centred(got_ref[3], 0.0, tile_tok),
-    )
-    own_share = jnp.exp2((own_top_ref[...] - top) * EXP_SCALE) / total
+        top, total, centred(far_top, NEG, tile_tok), centred(far_total, 0.0, tile_tok)
+    )
+    own_top = own_top_ref[group.start : group.stop]
+    own_share = jnp.exp2((own_top - top) * EXP_SCALE) / total
     side_share = jnp.exp2((side_top_ref[...] - top[:, half:]) * EXP_SCALE) / total[:, half:]
-    guest_top, guest_total = shares(sent_ref[2], sent_ref[3], got_ref[0], got_ref[1])
-    guest_share = jnp.exp2((sent_ref[2] - guest_top) * EXP_SCALE) / guest_total
-    guest = jnp.zeros(guest_velocity_ref.shape, jnp.float32)
-    near = jnp.zeros(guest_velocity_ref.shape, jnp.float32)
-    far = jnp.zeros(guest_velocity_ref.shape, jnp.float32)
-    for head in range(HEADS):
-        one = slice(head, head + 1)
-        guest = guest + guest_share[one] * guest_out_ref[head]
+    near = jnp.zeros((own_out_ref.shape[1], half), jnp.float32)
+    far = jnp.zeros((own_out_ref.shape[1], half), jnp.float32)
+    for row, head in enumerate(group):
+        one = slice(row, row + 1)
         near = near + own_share[one, :half] * own_out_ref[head, :, :half]
         far = far + own_share[one, half:] * own_out_ref[head, :, half:]
-        far = far + side_share[one] * side_out_ref[head]
-    guest_velocity_ref[...] = guest
-    velocity_ref[:, :half] = near
-    velocity_ref[:, half:] = far
-
-
-def join_kernel(tile_tok, velocity_ref, back_ref, out_ref):
-    out_ref[...] = velocity_ref[...] + centred(back_ref[...], 0.0, tile_tok)
+        far = far + side_share[one] * side_out_ref[row]
+    guest_top = beside(top[:, tile_tok:half], top[:, half : half + tile_tok])
+    guest_total = beside(total[:, tile_tok:half], total[:, half : half + tile_tok])
+    return beside(near, far), jnp.exp2((far_top - guest_top) * EXP_SCALE) / guest_total
+
+
+def own_blend_kernel(
+    tile_tok, group, own_out_ref, side_out_ref, own_top_ref, side_top_ref,
+    top_ref, sum_ref, got_ref, velocity_ref,
+):
+    velocity_ref[...], _ = own_part(
+        tile_tok, group, own_out_ref, side_out_ref, own_top_ref, side_top_ref,
+        top_ref[...], sum_ref[...], got_ref[2], got_ref[3],
+    )
+
+
+def join_kernel(
+    tile_tok, group, own_out_ref, side_out_ref, own_top_ref, side_top_ref,
+    top_ref, sum_ref, velocity_ref, back_ref, back_out_ref, out_ref,
+):
+    channels = own_out_ref.shape[1]
+    late = len(group)
+    velocity, share = own_part(
+        tile_tok, group, own_out_ref, side_out_ref, own_top_ref, side_top_ref,
+        top_ref[...], sum_ref[...],
+        back_ref[channels : channels + late], back_ref[channels + late : channels + 2 * late],
+    )
+    guest = back_ref[:channels]
+    for row in range(late):
+        guest = guest + share[row : row + 1] * back_out_ref[row].astype(jnp.float32)
+    out_ref[...] = velocity_ref[...] + velocity + centred(guest, 0.0, tile_tok)
 
 
 def update_kernel(
     block_count, block_cols, tile_tok, half_size,
-    index_ref, step_ref, velocity_ref, partner_ref, latent_ref,
+    step_ref, velocity_ref, partner_ref, latent_ref,
     guided_ref, clean_ref, next_ref,
 ):
-    spot = Spot(index_ref[0], block_count, block_cols)
+    spot = Spot(block_count, block_cols)
     half = 2 * tile_tok
-    is_cond = index_ref[0] < half_size
+    is_cond = spot.index < half_size
     own = velocity_ref[...]
     other = partner_ref[...]
     cond = jnp.where(is_cond, own, other)
@@ -604,8 +664,7 @@
     half_size = frame_count // 2
     block_cols = SW // 2
     block_count = SH // 2 * block_cols
-    frame_index = lax.axis_index("frame")
-    tok_rows, width = query_rows.shape
+    tok_rows, _ = query_rows.shape
     tile_tok = tok_rows // 4
     half = 2 * tile_tok
     channels = head_weight.shape[1]
@@ -616,97 +675,125 @@
     ]
     mate_pairs = [(f, f + 1 - 2 * (f % 2)) for f in places]
     side_pairs = []
+    group_count = lax.axis_size("groups")
     for f in places:
         step = 2 * (f % 2) - 1
-        if 0 <= f % block_cols + step < block_cols:
-            side_pairs.append((f, f + step))
+        inside = 0 <= f % block_cols + step < block_cols
+        for g in range(group_count):
+            if inside:
+                side_pairs.append((g * frame_count + f, g * frame_count + f + step))
+            else:
+                other = (g + 1) % group_count
+                side_pairs.append((g * frame_count + f, other * frame_count + f))
     branch_pairs = [(f, (f + half_size) % frame_count) for f in places]
     sizes = (block_count, block_cols, tile_tok)
-    index = frame_index.astype(jnp.int32).reshape(1)
     single = jnp.float32
-    packed_type = query_rows.dtype
-
-    (guest_send,) = kernel_call(
-        functools.partial(guest_pack_kernel, *sizes),
-        (index, query_rows),
-        (((half, width), packed_type),),
+    half_type = query_rows.dtype
+    groups = (range(FIRST_HEADS), range(FIRST_HEADS, HEADS))
+    every = (range(HEADS),)
+    _, late = (len(group) for group in groups)
+
+    weight_t = head_weight.T
+    *guest_sends, edge_bias, weight_t = kernel_call(
+        functools.partial(guest_pack_kernel, *sizes, groups),
+        (query_rows, tile_mask, weight_t),
+        [((half, len(group) * HD), half_type) for group in groups]
+        + [((4, half), single), (weight_t.shape, half_type)],
+        0,
+        (
+            pltpu.SMEM(tile_mask.shape, tile_mask.dtype),
+            pltpu.SemaphoreType.DMA((2 + 2 * len(groups),)),
+        ),
+        far=(0, 1, 2),
+    )
+
+    def sent_over(value, pairs, axes="frame"):
+        return lax.ppermute(value, axes, pairs)
+
+    guests = [sent_over(guest_sends[0], row_pairs)]
+    *far, near = kernel_call(
+        functools.partial(column_pack_kernel, *sizes, groups),
+        (key_rows, value_rows, weight_t, *guest_sends),
+        [((half, packed_width(len(group), channels)), half_type) for group in groups + every],
+        0,
+        (pltpu.SemaphoreType.DMA((2 + 2 * len(groups),)),),
+        far=(0,),
+    )
+    outer = [sent_over(column, side_pairs, ("groups", "frame")) for column in far]
+    guest_bias = sent_over(edge_bias, row_pairs)
+    guests.append(sent_over(guest_sends[1], row_pairs))
+    inner = sent_over(near, mate_pairs)
+    stats = ((HEADS, tok_rows), single)
+    own_out, own_top, own_sum, side_bias = kernel_call(
+        functools.partial(own_kernel, *sizes, groups),
+        (tile_mask, query_rows, near, *far, inner),
+        (((HEADS, channels, tok_rows), single), stats, stats, ((2, half), single)),
         1,
-        (pltpu.SemaphoreType.DMA((2 * PIECES,)),),
-        far=(1,),
-    )
-    guest_send = pltpu.with_memory_space_constraint(guest_send, pltpu.VMEM)
-    guest = lax.ppermute(guest_send, "frame", row_pairs)
-
-    packed = (half, width + (HEADS + 1) // 2 * 2 * channels)
-    near, far = kernel_call(
-        functools.partial(column_pack_kernel, *sizes),
-        (index, key_rows, value_rows, head_weight.T),
-        ((packed, packed_type), (packed, packed_type)),
-        1,
-        (
-            pltpu.VMEM((tok_rows, width), packed_type),
-            pltpu.VMEM((channels, width), packed_type),
-            pltpu.SemaphoreType.DMA((9,)),
-        ),
-        far=(1, 2, 3),
-    )
-    outer = lax.ppermute(far, "frame", side_pairs)
-    inner = lax.ppermute(near, "frame", mate_pairs)
-    edge_row = 1 - frame_index % block_count // block_cols
-    guest_mask = lax.ppermute(
-        lax.dynamic_slice_in_dim(tile_mask, edge_row * 2, 2, 0).astype(single),
-        "frame",
-        row_pairs,
-    )
-    stats = ((HEADS, tok_rows), single)
-    half_stats = ((HEADS, half), single)
-    own_out, own_top, own_sum = kernel_call(
-        functools.partial(own_kernel, *sizes),
-        (index, tile_mask, query_rows, near, far, inner),
-        (((HEADS, channels, tok_rows), single), stats, stats),
-        2,
         (
             pltpu.VMEM((HEADS, tok_rows, tok_rows), single),
             pltpu.VMEM((HEADS, half, half), single),
-            pltpu.VMEM((HEADS, tok_rows, tok_rows), packed_type),
-            pltpu.VMEM((HEADS, half, half), packed_type),
+            pltpu.VMEM((HEADS, tok_rows, tok_rows), half_type),
+            pltpu.VMEM((HEADS, half, half), half_type),
         ),
     )
-    half_out = ((HEADS, channels, half), single)
-    side_out, guest_out, side_top, top, total, sent = kernel_call(
-        functools.partial(edge_kernel, *sizes),
+
+    def edge(number, guest_type):
+        group = groups[number]
+        heads = len(group)
+        return kernel_call(
+            functools.partial(edge_kernel, *sizes, group),
+            (
+                side_bias, guest_bias, query_rows, near, far[number], inner,
+                outer[number], guests[number], own_top, own_sum,
+            ),
+            (
+                ((heads, channels, half), single),
+                ((heads, channels, half), guest_type),
+                ((heads, half), single),
+                ((heads, tok_rows), single),
+                ((heads, tok_rows), single),
+                ((4, heads, half), single),
+            ),
+            0,
+            (
+                pltpu.VMEM((heads, half, half), single),
+                pltpu.VMEM((heads, tok_rows, half), single),
+                pltpu.VMEM((heads, half, half), half_type),
+                pltpu.VMEM((heads, tok_rows, half), half_type),
+            ),
+        )
+
+    side_out, guest_out, side_top, top, total, sent = edge(0, single)
+    got = sent_over(sent, row_pairs)
+    late_side, late_guest, late_side_top, late_top, late_total, late_sent = edge(1, half_type)
+    (guest_velocity,) = kernel_call(
+        guest_blend_kernel,
+        (guest_out, sent, got, late_sent),
+        (((channels + 2 * late, half), single),),
+    )
+    back = sent_over(guest_velocity, row_pairs)
+    back_out = sent_over(late_guest, row_pairs)
+    velocity_type = ((channels, tok_rows), single)
+    (velocity,) = kernel_call(
+        functools.partial(own_blend_kernel, tile_tok, groups[0]),
+        (own_out, side_out, own_top, side_top, top, total, got),
+        (velocity_type,),
+    )
+    (velocity,) = kernel_call(
+        functools.partial(join_kernel, tile_tok, groups[1]),
         (
-            index, tile_mask, guest_mask, query_rows, near, far, inner, outer, guest,
-            own_top, own_sum,
+            own_out, late_side, own_top, late_side_top, late_top, late_total, velocity,
+            back, back_out,
         ),
-        (half_out, half_out, half_stats, stats, stats, ((4, HEADS, half), single)),
-        3,
-        (
-            pltpu.VMEM((HEADS, half, half), single),
-            pltpu.VMEM((HEADS, tok_rows, half), single),
-            pltpu.VMEM((HEADS, half, half), packed_type),
-            pltpu.VMEM((HEADS, tok_rows, half), packed_type),
-        ),
-    )
-    got = lax.ppermute(sent, "frame", row_pairs)
-    velocity, guest_velocity = kernel_call(
-        functools.partial(blend_kernel, tile_tok),
-        (own_out, side_out, guest_out, own_top, side_top, top, total, sent, got),
-        (((channels, tok_rows), single), ((channels, half), single)),
-    )
-    back = lax.ppermute(guest_velocity, "frame", row_pairs)
-    (velocity,) = kernel_call(
-        functools.partial(join_kernel, tile_tok),
-        (velocity, back),
-        (((channels, tok_rows), single),),
-    )
-    partner = lax.ppermute(velocity, "frame", branch_pairs)
+        (velocity_type,),
+    )
+    partner = sent_over(velocity, branch_pairs)
     out = ((channels, tok_rows), single)
     results = kernel_call(
         functools.partial(update_kernel, *sizes, half_size),
-        (index, step_index, velocity, partner, latent.T),
+        (step_index, velocity, partner, latent.T),
         (out, out, out),
-        2,
+        1,
         stay=False,
     )
     return tuple(result.T for result in results)

time: 44 us -> 43.5 us (0.989)
  Pallas kernels: 13 us -> 10.4 us
  waiting for transfers between devices: 16.9 us -> 18.7 us
    pallas_call x7 -> x9, Pallas kernels: 13 us -> 10.4 us  [kernel_call(): pl.pallas_call(body, out_shape=[pltpu.VMEM(shape, dtype) if stay else jax...]
    ppermute x7 -> x10, waiting for transfers between devices: 16.9 us -> 18.7 us  [sent_over(): return lax.ppermute(value, axes, pairs)]
    ppermute x7 -> x10, starting transfers between devices: 12.4 us -> 12.7 us  [sent_over(): return lax.ppermute(value, axes, pairs)]
  transfers between devices with their start and end apart: 7 -> 10, of which waited for: 4 -> 4; matrix products, arithmetic and copies ran while one was open for 0% -> 0% of each run, Pallas kernels for 13% -> 14%
where the time goes in v3:
time: 43.5 us; the launch traced here: 43.3 us
  waiting for transfers between devices  18.7 us (43%)
  starting transfers between devices  12.7 us (29%)
  Pallas kernels  10.4 us (24%)
  between operations  1.35 us (3%)
    ppermute x10, waiting for transfers between devices, sent_over(): return lax.ppermute(value, axes, pairs)  18.7 us
    ppermute x10, starting transfers between devices, sent_over(): return lax.ppermute(value, axes, pairs)  12.7 us
    pallas_call x9, Pallas kernels, kernel_call(): pl.pallas_call(body, out_shape=[pltpu.VMEM(shape, dtype) if stay else jax...  10.4 us
  transfers between devices with their start and end apart: 10, of which 4 were waited for; matrix products, arithmetic and copies ran while one was open for 0% of the time, Pallas kernels for 14%

profile of v3, /device:TPU:0, one launch (start us, length us, event | category | flops | bytes accessed | tf_op | source)
XLA Modules:
  0.0 43.3 jit_solution(6366790786510564923)
XLA Ops:
  0.6 1.4 %shard_map.94 = (bf16[128,1792]{1,0:T(8,128)(2,1)S(1)}, bf16[128,768]{1,0:T(8,128)(2,1)S(1)}, f32[4,128]{1,0:T(4,128)S(1)}, bf16[64,2560]{1,0:T(8,128)(2,1)S(1)}) custom-call(bf16[256,2560]{1,0:T(8,128)(2,1)} %query_ref.7, s32[4,27]{1,0:T(4,128)} %mask_ref.3, bf16[64,2560]{1,0:T(8,128)(2,1)} %bitcast.6), custom_call_target="tpu_custom_call" | custom-call | tf_op jit(solution)/shard_map/pallas_call | solution.py:645
  2.0 0.3 copy-done.1
  2.3 1.9 %shard_map.95 = (bf16[128,2688]{1,0:T(8,128)(2,1)S(1)}, bf16[128,1152]{1,0:T(8,128)(2,1)S(1)}, bf16[128,3840]{1,0:T(8,128)(2,1)S(1)}) custom-call(bf16[256,2560]{1,0:T(8,128)(2,1)} %key_ref.1, bf16[256,2560]{1,0:T(8,128)(2,1)S(1)} %copy-done.1, bf16[64,2560]{1,0:T(8,128)(2,1)S(1)} %get-tuple-element.29.weight_ref, ...), custom_call_target="tpu_custom_call" | custom-call | tf_op jit(solution)/shard_map/pallas_call | solution.py:645
  4.2 0.6 %collective-permute-start = (bf16[128,3840]{1,0:T(8,128)(2,1)S(1)}, bf16[128,3840]{1,0:T(8,128)(2,1)S(1)}, u32[]{:S(2)}, u32[]{:S(2)}) collective-permute-start(bf16[128,3840]{1,0:T(8,128)(2,1)S(1)} %get-tuple-element.32.refs_0_.near_ref), channel_id=1, source_target_pairs={{0,1},{1,0},{2,3},{3,2},{4,5},{5,4},{6,7},{7,6},{8,9},{9,8},{10,11... | collective-permute-start | bytes 2949128 | tf_op jit(solution)/shard_map/ppermute | solution.py:711
  4.7 2.6 %collective-permute-start.4 = (bf16[128,2688]{1,0:T(8,128)(2,1)S(1)}, bf16[128,2688]{1,0:T(8,128)(2,1)S(1)}, u32[]{:S(2)}, u32[]{:S(2)}) collective-permute-start(bf16[128,2688]{1,0:T(8,128)(2,1)S(1)} %get-tuple-element.33.refs_1_.far_ref), channel_id=1, source_target_pairs={{0,16},{16,0},{1,2},{17,18},{2,1},{18,17},{3,19},{19,3},{4,20},{20... | collective-permute-start | bytes 2064392 | tf_op jit(solution)/shard_map/ppermute | solution.py:711
  7.3 1.6 %collective-permute-start.5 = (bf16[128,1792]{1,0:T(8,128)(2,1)S(1)}, bf16[128,1792]{1,0:T(8,128)(2,1)S(1)}, u32[]{:S(2)}, u32[]{:S(2)}) collective-permute-start(bf16[128,1792]{1,0:T(8,128)(2,1)S(1)} %get-tuple-element.30.refs_0_), channel_id=1, source_target_pairs={{0,4},{1,5},{2,6},{3,7},{4,0},{5,1},{6,2},{7,3},{8,12},{9,13},{10,... | collective-permute-start | bytes 1376264 | tf_op jit(solution)/shard_map/ppermute | solution.py:711
  8.9 0.5 %collective-permute-start.2 = (bf16[128,1152]{1,0:T(8,128)(2,1)S(1)}, bf16[128,1152]{1,0:T(8,128)(2,1)S(1)}, u32[]{:S(2)}, u32[]{:S(2)}) collective-permute-start(bf16[128,1152]{1,0:T(8,128)(2,1)S(1)} %get-tuple-element.34.refs_2_.far_ref), channel_id=1, source_target_pairs={{0,16},{16,0},{1,2},{17,18},{2,1},{18,17},{3,19},{19,3},{4,20},{20... | collective-permute-start | bytes 884744 | tf_op jit(solution)/shard_map/ppermute | solution.py:711
  9.4 0.0 collective-permute-start.3
  9.4 0.0 collective-permute-done.refs_3_.inner_ref
  9.4 2.0 %collective-permute-start.1 = (f32[4,128]{1,0:T(4,128)S(1)}, f32[4,128]{1,0:T(4,128)S(1)}, u32[]{:S(2)}, u32[]{:S(2)}) collective-permute-start(f32[4,128]{1,0:T(4,128)S(1)} %get-tuple-element.37), channel_id=1, source_target_pairs={{0,4},{1,5},{2,6},{3,7},{4,0},{5,1},{6,2},{7,3},{8,12},{9,13},{10,... | collective-permute-start | bytes 6152 | tf_op jit(solution)/shard_map/ppermute | solution.py:711
  11.4 0.0 copy-done.3
  11.4 3.1 %shard_map.96 = (f32[20,64,256]{2,1,0:T(8,128)S(1)}, f32[20,256]{1,0:T(8,128)S(1)}, f32[20,256]{1,0:T(8,128)S(1)}, f32[2,128]{1,0:T(2,128)S(1)}) custom-call(s32[4,27]{1,0:T(4,128)S(1)} %copy-done.3, bf16[256,2560]{1,0:T(8,128)(2,1)S(1)} %copy-done, bf16[128,3840]{1,0:T(8,128)(2,1)S(1)} %get-tuple-element.32.refs_0_.near_ref, ...), custom_call_target="tpu_custom_call" | custom-call | tf_op jit(solution)/shard_map/pallas_call | solution.py:645
  14.6 9.5 %collective-permute-done.1.guest_bias_ref = f32[4,128]{1,0:T(4,128)S(1)} collective-permute-done((f32[4,128]{1,0:T(4,128)S(1)}, f32[4,128]{1,0:T(4,128)S(1)}, u32[]{:S(2)}, u32[]{:S(2)}) %collective-permute-start.1) | collective-permute-done | bytes 2080 | tf_op jit(solution)/shard_map/ppermute | solution.py:711
  24.1 0.0 collective-permute-done.3.guest_ref
  24.1 0.0 collective-permute-done.2.outer_ref
  24.1 0.9 %shard_map.97 = (f32[6,64,128]{2,1,0:T(8,128)S(1)}, bf16[6,64,128]{2,1,0:T(8,128)(2,1)S(1)}, f32[6,128]{1,0:T(8,128)S(1)}, f32[6,256]{1,0:T(8,128)S(1)}, f32[6,256]{1,0:T(8,128)S(1)}, /*index=5*/f32[4,6,128]{2,1,0:T(8,128)S(1)}) custom-call(f32[2,128]{1,0:T(2,128)S(1)} %get-tuple-element.36.side_bias_ref, ...), custom_call_target="tpu_custom_call" | custom-call | tf_op jit(solution)/shard_map/pallas_call | solution.py:645
  25.0 1.6 %collective-permute-start.8 = (bf16[6,64,128]{2,1,0:T(8,128)(2,1)S(1)}, bf16[6,64,128]{2,1,0:T(8,128)(2,1)S(1)}, u32[]{:S(2)}, u32[]{:S(2)}) collective-permute-start(bf16[6,64,128]{2,1,0:T(8,128)(2,1)S(1)} %get-tuple-element.51), channel_id=1, source_target_pairs={{0,4},{1,5},{2,6},{3,7},{4,0},{5,1},{6,2},{7,3},{8,12},{9,13},{10,... | collective-permute-start | bytes 294920 | tf_op jit(solution)/shard_map/ppermute | solution.py:711
  26.6 0.0 collective-permute-done.5.guest_ref
  26.6 0.0 collective-permute-done.4.outer_ref
  26.6 1.6 %shard_map.98 = (f32[14,64,128]{2,1,0:T(8,128)S(1)}, f32[14,64,128]{2,1,0:T(8,128)S(1)}, f32[14,128]{1,0:T(8,128)S(1)}, f32[14,256]{1,0:T(8,128)S(1)}, f32[14,256]{1,0:T(8,128)S(1)}, /*index=5*/f32[4,14,128]{2,1,0:T(8,128)S(1)}) custom-call(f32[2,128]{1,0:T(2,128)S(1)} %get-tuple-element.36.side_bias_ref, ...), custom_call_target="tpu_custom_call" | custom-call | tf_op jit(solution)/shard_map/pallas_call | solution.py:645
  28.2 0.5 %collective-permute-start.6 = (f32[4,14,128]{2,1,0:T(8,128)S(1)}, f32[4,14,128]{2,1,0:T(8,128)S(1)}, u32[]{:S(2)}, u32[]{:S(2)}) collective-permute-start(f32[4,14,128]{2,1,0:T(8,128)S(1)} %get-tuple-element.48.sent_ref), channel_id=1, source_target_pairs={{0,4},{1,5},{2,6},{3,7},{4,0},{5,1},{6,2},{7,3},{8,12},{9,13},{10,... | collective-permute-start | bytes 86024 | tf_op jit(solution)/shard_map/ppermute | solution.py:711
  28.7 3.5 %collective-permute-done.6.got_ref = f32[4,14,128]{2,1,0:T(8,128)S(1)} collective-permute-done((f32[4,14,128]{2,1,0:T(8,128)S(1)}, f32[4,14,128]{2,1,0:T(8,128)S(1)}, u32[]{:S(2)}, u32[]{:S(2)}) %collective-permute-start.6) | collective-permute-done | bytes 28704 | tf_op jit(solution)/shard_map/ppermute | solution.py:711
  32.2 0.1 shard_map.100
  32.2 0.5 %collective-permute-start.7 = (f32[76,128]{1,0:T(8,128)S(1)}, f32[76,128]{1,0:T(8,128)S(1)}, u32[]{:S(2)}, u32[]{:S(2)}) collective-permute-start(f32[76,128]{1,0:T(8,128)S(1)} %shard_map.100), channel_id=1, source_target_pairs={{0,4},{1,5},{2,6},{3,7},{4,0},{5,1},{6,2},{7,3},{8,12},{9,13},{10,... | collective-permute-start | bytes 116744 | tf_op jit(solution)/shard_map/ppermute | solution.py:711
  32.7 0.2 shard_map.99.velocity_ref
  32.9 0.0 copy-start.2
  32.9 3.3 %collective-permute-done.7.back_ref = f32[76,128]{1,0:T(8,128)S(1)} collective-permute-done((f32[76,128]{1,0:T(8,128)S(1)}, f32[76,128]{1,0:T(8,128)S(1)}, u32[]{:S(2)}, u32[]{:S(2)}) %collective-permute-start.7) | collective-permute-done | bytes 38944 | tf_op jit(solution)/shard_map/ppermute | solution.py:711
  36.3 0.0 collective-permute-done.8.back_out_ref
  36.3 0.2 shard_map.101.velocity_ref
  36.5 2.8 %collective-permute-start.9 = (f32[64,256]{1,0:T(8,128)S(1)}, f32[64,256]{1,0:T(8,128)S(1)}, u32[]{:S(2)}, u32[]{:S(2)}) collective-permute-start(f32[64,256]{1,0:T(8,128)S(1)} %shard_map.101.velocity_ref), channel_id=1, source_target_pairs={{0,8},{1,9},{2,10},{3,11},{4,12},{5,13},{6,14},{7,15},{8,0},{9,1},... | collective-permute-start | bytes 196616 | tf_op jit(solution)/shard_map/ppermute | solution.py:711
  40.0 2.4 %collective-permute-done.9.partner_ref = f32[64,256]{1,0:T(8,128)S(1)} collective-permute-done((f32[64,256]{1,0:T(8,128)S(1)}, f32[64,256]{1,0:T(8,128)S(1)}, u32[]{:S(2)}, u32[]{:S(2)}) %collective-permute-start.9) | collective-permute-done | bytes 65568 | tf_op jit(solution)/shard_map/ppermute | solution.py:711
  42.4 1.0 %shard_map.102 = (f32[64,256]{1,0:T(8,128)}, f32[64,256]{1,0:T(8,128)}, f32[64,256]{1,0:T(8,128)}) custom-call(s32[1]{0:T(128)S(6)} %copy.10.step_ref, f32[64,256]{1,0:T(8,128)S(1)} %shard_map.101.velocity_ref, f32[64,256]{1,0:T(8,128)S(1)} %collective-permute-done.9.partner_ref, f32[64,256]{1,0:T(8,128)S(1)} %bitcast.5), custom_call_target="tpu_custom_call" | custom-call | tf_op jit(solution)/shard_map/pallas_call | solution.py:645
  (5 shorter events, 0.0 us)
Async XLA Ops:
  0.6 1.7 %copy-start.1 = (bf16[256,2560]{1,0:T(8,128)(2,1)S(1)}, bf16[256,2560]{1,0:T(8,128)(2,1)}, u32[]{:S(2)}) copy-start(bf16[256,2560]{1,0:T(8,128)(2,1)} %value_ref.1) | copy-start | bytes 3932164
  2.3 9.1 %copy-start = (bf16[256,2560]{1,0:T(8,128)(2,1)S(1)}, bf16[256,2560]{1,0:T(8,128)(2,1)}, u32[]{:S(2)}) copy-start(bf16[256,2560]{1,0:T(8,128)(2,1)} %query_ref.7) | copy-start | bytes 3932164
  2.3 9.1 %copy-start.3 = (s32[4,27]{1,0:T(4,128)S(1)}, s32[4,27]{1,0:T(4,128)}, u32[]{:S(2)}) copy-start(s32[4,27]{1,0:T(4,128)} %mask_ref.3) | copy-start | bytes 1300
  4.2 5.2 %collective-permute-start = (bf16[128,3840]{1,0:T(8,128)(2,1)S(1)}, bf16[128,3840]{1,0:T(8,128)(2,1)S(1)}, u32[]{:S(2)}, u32[]{:S(2)}) collective-permute-start(bf16[128,3840]{1,0:T(8,128)(2,1)S(1)} %get-tuple-element.32.refs_0_.near_ref), channel_id=1, source_target_pairs={{0,1},{1,0},{2,3},{3,2},{4,5},{5,4},{6,7},{7,6},{8,9},{9,8},{10,11... | collective-permute-start | bytes 2949128 | tf_op jit(solution)/shard_map/ppermute | solution.py:711
  4.7 21.9 %collective-permute-start.4 = (bf16[128,2688]{1,0:T(8,128)(2,1)S(1)}, bf16[128,2688]{1,0:T(8,128)(2,1)S(1)}, u32[]{:S(2)}, u32[]{:S(2)}) collective-permute-start(bf16[128,2688]{1,0:T(8,128)(2,1)S(1)} %get-tuple-element.33.refs_1_.far_ref), channel_id=1, source_target_pairs={{0,16},{16,0},{1,2},{17,18},{2,1},{18,17},{3,19},{19,3},{4,20},{20... | collective-permute-start | bytes 2064392 | tf_op jit(solution)/shard_map/ppermute | solution.py:711
  7.3 19.3 %collective-permute-start.5 = (bf16[128,1792]{1,0:T(8,128)(2,1)S(1)}, bf16[128,1792]{1,0:T(8,128)(2,1)S(1)}, u32[]{:S(2)}, u32[]{:S(2)}) collective-permute-start(bf16[128,1792]{1,0:T(8,128)(2,1)S(1)} %get-tuple-element.30.refs_0_), channel_id=1, source_target_pairs={{0,4},{1,5},{2,6},{3,7},{4,0},{5,1},{6,2},{7,3},{8,12},{9,13},{10,... | collective-permute-start | bytes 1376264 | tf_op jit(solution)/shard_map/ppermute | solution.py:711
  8.9 15.3 %collective-permute-start.2 = (bf16[128,1152]{1,0:T(8,128)(2,1)S(1)}, bf16[128,1152]{1,0:T(8,128)(2,1)S(1)}, u32[]{:S(2)}, u32[]{:S(2)}) collective-permute-start(bf16[128,1152]{1,0:T(8,128)(2,1)S(1)} %get-tuple-element.34.refs_2_.far_ref), channel_id=1, source_target_pairs={{0,16},{16,0},{1,2},{17,18},{2,1},{18,17},{3,19},{19,3},{4,20},{20... | collective-permute-start | bytes 884744 | tf_op jit(solution)/shard_map/ppermute | solution.py:711
  9.4 14.7 %collective-permute-start.3 = (bf16[128,768]{1,0:T(8,128)(2,1)S(1)}, bf16[128,768]{1,0:T(8,128)(2,1)S(1)}, u32[]{:S(2)}, u32[]{:S(2)}) collective-permute-start(bf16[128,768]{1,0:T(8,128)(2,1)S(1)} %get-tuple-element.31.refs_1_), channel_id=1, source_target_pairs={{0,4},{1,5},{2,6},{3,7},{4,0},{5,1},{6,2},{7,3},{8,12},{9,13},{10,... | collective-permute-start | bytes 589832 | tf_op jit(solution)/shard_map/ppermute | solution.py:711
  9.4 14.7 %collective-permute-start.1 = (f32[4,128]{1,0:T(4,128)S(1)}, f32[4,128]{1,0:T(4,128)S(1)}, u32[]{:S(2)}, u32[]{:S(2)}) collective-permute-start(f32[4,128]{1,0:T(4,128)S(1)} %get-tuple-element.37), channel_id=1, source_target_pairs={{0,4},{1,5},{2,6},{3,7},{4,0},{5,1},{6,2},{7,3},{8,12},{9,13},{10,... | collective-permute-start | bytes 6152 | tf_op jit(solution)/shard_map/ppermute | solution.py:711
  25.0 11.3 %collective-permute-start.8 = (bf16[6,64,128]{2,1,0:T(8,128)(2,1)S(1)}, bf16[6,64,128]{2,1,0:T(8,128)(2,1)S(1)}, u32[]{:S(2)}, u32[]{:S(2)}) collective-permute-start(bf16[6,64,128]{2,1,0:T(8,128)(2,1)S(1)} %get-tuple-element.51), channel_id=1, source_target_pairs={{0,4},{1,5},{2,6},{3,7},{4,0},{5,1},{6,2},{7,3},{8,12},{9,13},{10,... | collective-permute-start | bytes 294920 | tf_op jit(solution)/shard_map/ppermute | solution.py:711
  28.2 4.0 %collective-permute-start.6 = (f32[4,14,128]{2,1,0:T(8,128)S(1)}, f32[4,14,128]{2,1,0:T(8,128)S(1)}, u32[]{:S(2)}, u32[]{:S(2)}) collective-permute-start(f32[4,14,128]{2,1,0:T(8,128)S(1)} %get-tuple-element.48.sent_ref), channel_id=1, source_target_pairs={{0,4},{1,5},{2,6},{3,7},{4,0},{5,1},{6,2},{7,3},{8,12},{9,13},{10,... | collective-permute-start | bytes 86024 | tf_op jit(solution)/shard_map/ppermute | solution.py:711
  32.2 4.1 %collective-permute-start.7 = (f32[76,128]{1,0:T(8,128)S(1)}, f32[76,128]{1,0:T(8,128)S(1)}, u32[]{:S(2)}, u32[]{:S(2)}) collective-permute-start(f32[76,128]{1,0:T(8,128)S(1)} %shard_map.100), channel_id=1, source_target_pairs={{0,4},{1,5},{2,6},{3,7},{4,0},{5,1},{6,2},{7,3},{8,12},{9,13},{10,... | collective-permute-start | bytes 116744 | tf_op jit(solution)/shard_map/ppermute | solution.py:711
  32.9 9.4 %copy-start.2 = (f32[256,64]{0,1:T(8,128)S(1)}, f32[256,64]{0,1:T(8,128)}, u32[]{:S(2)}) copy-start(f32[256,64]{0,1:T(8,128)} %param.12) | copy-start | bytes 196612
  36.5 5.8 %collective-permute-start.9 = (f32[64,256]{1,0:T(8,128)S(1)}, f32[64,256]{1,0:T(8,128)S(1)}, u32[]{:S(2)}, u32[]{:S(2)}) collective-permute-start(f32[64,256]{1,0:T(8,128)S(1)} %shard_map.101.velocity_ref), channel_id=1, source_target_pairs={{0,8},{1,9},{2,10},{3,11},{4,12},{5,13},{6,14},{7,15},{8,0},{9,1},... | collective-permute-start | bytes 196616 | tf_op jit(solution)/shard_map/ppermute | solution.py:711

commit v4 on v3

--- a/solution.py
+++ b/solution.py
@@ -320,20 +320,23 @@
 
 
 def guest_pack_kernel(
-    block_count, block_cols, tile_tok, groups,
-    query_ref, mask_ref, weight_ref, *refs
+    block_count, block_cols, tile_tok,
+    query_ref, key_ref, mask_ref, weight_ref,
+    guest_ref, bias_ref, far_key_ref, near_weight_ref, mask, sems,
 ):
     spot = Spot(block_count, block_cols)
-    *out_refs, bias_ref, near_weight_ref, mask, sems = refs
-    pairs = [(mask_ref, mask), (weight_ref, near_weight_ref)]
-    for out_ref, group in zip(out_refs, groups):
-        lanes = pl.ds(group.start * HD, len(group) * HD)
-        for number, col in enumerate((spot.near, spot.far)):
-            rows = tile_rows((spot.edge, col), tile_tok)
-            target = out_ref.at[pl.ds(number * tile_tok, tile_tok)]
-            pairs.append((query_ref.at[rows, lanes], target))
-    for copy in copied(pairs, sems):
-        copy.wait()
+    pairs = [(mask_ref, mask)]
+    lanes = pl.ds(0, guest_ref.shape[1])
+    for number, col in enumerate((spot.near, spot.far)):
+        target = pl.ds(number * tile_tok, tile_tok)
+        rows = tile_rows((spot.edge, col), tile_tok)
+        pairs.append((query_ref.at[rows, lanes], guest_ref.at[target]))
+    pairs.append((weight_ref, near_weight_ref))
+    for number, tile in enumerate(spot.key_tiles[2:]):
+        target = pl.ds(number * tile_tok, tile_tok)
+        pairs.append((key_ref.at[tile_rows(tile, tile_tok)], far_key_ref.at[target]))
+    copies = copied(pairs, sems)
+    copies[0].wait()
     steps = -spot.guest_step
 
     def flag(col, col_step):
@@ -347,38 +350,43 @@
     ]
     for number, row in enumerate(key_bias(rows, tile_tok)):
         bias_ref[number : number + 1] = row
-
-
-def column_pack_kernel(
-    block_count, block_cols, tile_tok, groups, key_ref, value_ref, weight_ref, *refs
+    for copy in copies[1:]:
+        copy.wait()
+
+
+def fold_into(column, value_ref, weight_ref, places):
+    for head in range(HEADS):
+        lanes = head_lanes(head)
+        values = above(*[value_ref[place, lanes] for place in places])
+        folded = contract_last(weight_ref[:, lanes], values)
+        ref, where = column.folded_at(head)
+        ref[where] = folded.astype(jnp.bfloat16)
+
+
+def far_pack_kernel(
+    block_count, block_cols, tile_tok, groups, key_ref, value_ref, weight_ref, guest_ref, *refs
 ):
     spot = Spot(block_count, block_cols)
-    channels = weight_ref.shape[0]
-    *far_refs, near_ref, sems = refs[-2 - len(groups) :]
-    sides = (
-        (spot.key_tiles[2:], far_refs, groups),
-        (spot.key_tiles[:2], [near_ref], (range(HEADS),)),
-    )
-    pairs = []
-    for tiles, out_refs, out_groups in sides:
-        for out_ref, group in zip(out_refs, out_groups):
-            width = len(group) * HD
-            for number, tile in enumerate(tiles):
-                source = key_ref.at[tile_rows(tile, tile_tok), pl.ds(group.start * HD, width)]
-                target = out_ref.at[pl.ds(number * tile_tok, tile_tok), pl.ds(0, width)]
-                pairs.append((source, target))
-    copies = copied(pairs, sems)
-    for tiles, out_refs, out_groups in sides:
-        column = Column(out_refs, out_groups, channels)
-        places = [tile_rows(tile, tile_tok) for tile in tiles]
-        for head in range(HEADS):
-            lanes = head_lanes(head)
-            values = above(*[value_ref[place, lanes] for place in places])
-            folded = contract_last(weight_ref[:, lanes], values)
-            ref, where = column.folded_at(head)
-            ref[where] = folded.astype(jnp.bfloat16)
-    for copy in copies:
-        copy.wait()
+    for out_ref, group in zip(refs, groups):
+        out_ref[:, : len(group) * HD] = key_ref[:, group.start * HD : group.stop * HD]
+    places = [tile_rows(tile, tile_tok) for tile in spot.key_tiles[2:]]
+    fold_into(Column(refs, groups, weight_ref.shape[0]), value_ref, weight_ref, places)
+
+
+def near_pack_kernel(
+    block_count, block_cols, tile_tok, group,
+    query_ref, key_ref, value_ref, weight_ref, near_ref, guest_ref,
+):
+    spot = Spot(block_count, block_cols)
+    places = [tile_rows(tile, tile_tok) for tile in spot.key_tiles[:2]]
+    for number, col in enumerate((spot.near, spot.far)):
+        rows = slice(number * tile_tok, (number + 1) * tile_tok)
+        near_ref[rows, : HEADS * HD] = key_ref[places[number], :]
+        guest_ref[rows] = query_ref[
+            tile_rows((spot.edge, col), tile_tok), group.start * HD : group.stop * HD
+        ]
+    column = Column([near_ref], (range(HEADS),), weight_ref.shape[0])
+    fold_into(column, value_ref, weight_ref, places)
 
 
 def own_kernel(
@@ -664,7 +672,7 @@
     half_size = frame_count // 2
     block_cols = SW // 2
     block_count = SH // 2 * block_cols
-    tok_rows, _ = query_rows.shape
+    tok_rows, width = query_rows.shape
     tile_tok = tok_rows // 4
     half = 2 * tile_tok
     channels = head_weight.shape[1]
@@ -691,38 +699,44 @@
     half_type = query_rows.dtype
     groups = (range(FIRST_HEADS), range(FIRST_HEADS, HEADS))
     every = (range(HEADS),)
-    _, late = (len(group) for group in groups)
+    early, late = (len(group) for group in groups)
 
     weight_t = head_weight.T
-    *guest_sends, edge_bias, weight_t = kernel_call(
-        functools.partial(guest_pack_kernel, *sizes, groups),
-        (query_rows, tile_mask, weight_t),
-        [((half, len(group) * HD), half_type) for group in groups]
-        + [((4, half), single), (weight_t.shape, half_type)],
+    guest_send, edge_bias, far_keys, weight_t = kernel_call(
+        functools.partial(guest_pack_kernel, *sizes),
+        (query_rows, key_rows, tile_mask, weight_t),
+        (
+            ((half, early * HD), half_type),
+            ((4, half), single),
+            ((half, width), half_type),
+            (weight_t.shape, half_type),
+        ),
         0,
-        (
-            pltpu.SMEM(tile_mask.shape, tile_mask.dtype),
-            pltpu.SemaphoreType.DMA((2 + 2 * len(groups),)),
-        ),
-        far=(0, 1, 2),
+        (pltpu.SMEM(tile_mask.shape, tile_mask.dtype), pltpu.SemaphoreType.DMA((6,))),
+        far=(0, 1, 2, 3),
     )
 
     def sent_over(value, pairs, axes="frame"):
         return lax.ppermute(value, axes, pairs)
 
-    guests = [sent_over(guest_sends[0], row_pairs)]
-    *far, near = kernel_call(
-        functools.partial(column_pack_kernel, *sizes, groups),
-        (key_rows, value_rows, weight_t, *guest_sends),
-        [((half, packed_width(len(group), channels)), half_type) for group in groups + every],
-        0,
-        (pltpu.SemaphoreType.DMA((2 + 2 * len(groups),)),),
-        far=(0,),
+    def column_type(group):
+        return ((half, packed_width(len(group), channels)), half_type)
+
+    guests = [sent_over(guest_send, row_pairs)]
+    far = kernel_call(
+        functools.partial(far_pack_kernel, *sizes, groups),
+        (far_keys, value_rows, weight_t, guest_send),
+        [column_type(group) for group in groups],
     )
     outer = [sent_over(column, side_pairs, ("groups", "frame")) for column in far]
+    near, guest_send = kernel_call(
+        functools.partial(near_pack_kernel, *sizes, groups[1]),
+        (query_rows, key_rows, value_rows, weight_t),
+        (column_type(every[0]), ((half, late * HD), half_type)),
+    )
+    inner = sent_over(near, mate_pairs)
     guest_bias = sent_over(edge_bias, row_pairs)
-    guests.append(sent_over(guest_sends[1], row_pairs))
-    inner = sent_over(near, mate_pairs)
+    guests.append(sent_over(guest_send, row_pairs))
     stats = ((HEADS, tok_rows), single)
     own_out, own_top, own_sum, side_bias = kernel_call(
         functools.partial(own_kernel, *sizes, groups),

time: 43.5 us -> 45.4 us (1.044)
  local copies, waits for them, and re-layouts: 0.28 us -> 2.11 us
  Pallas kernels: 10.4 us -> 9.85 us
    unnamed x8 -> x12, local copies, waits for them, and re-layouts: 0.28 us -> 2.11 us
    pallas_call x9 -> x10, Pallas kernels: 10.4 us -> 9.85 us  [kernel_call(): pl.pallas_call(body, out_shape=[pltpu.VMEM(shape, dtype) if stay else jax...]
    ppermute x10, starting transfers between devices: 12.7 us -> 13.1 us  [sent_over(): return lax.ppermute(value, axes, pairs)]
where the time goes in v4:
time: 45.4 us; the launch traced here: 45.2 us
  waiting for transfers between devices  18.7 us (41%)
  starting transfers between devices  13.1 us (29%)
  Pallas kernels  9.85 us (22%)
  local copies, waits for them, and re-layouts  2.11 us (5%)
  between operations  1.36 us (3%)
    ppermute x10, waiting for transfers between devices, sent_over(): return lax.ppermute(value, axes, pairs)  18.7 us
    ppermute x10, starting transfers between devices, sent_over(): return lax.ppermute(value, axes, pairs)  13.1 us
    pallas_call x10, Pallas kernels, kernel_call(): pl.pallas_call(body, out_shape=[pltpu.VMEM(shape, dtype) if stay else jax...  9.85 us
    unnamed x12, local copies, waits for them, and re-layouts  2.11 us
  transfers between devices with their start and end apart: 10, of which 4 were waited for; matrix products, arithmetic and copies ran while one was open for 0% of the time, Pallas kernels for 14%

profile of v4, /device:TPU:0, one launch (start us, length us, event | category | flops | bytes accessed | tf_op | source)
XLA Modules:
  0.0 45.2 jit_solution(1548510182830319714)
XLA Ops:
  0.7 1.6 %shard_map.94 = (bf16[128,1792]{1,0:T(8,128)(2,1)S(1)}, f32[4,128]{1,0:T(4,128)S(1)}, bf16[128,2560]{1,0:T(8,128)(2,1)S(1)}, bf16[64,2560]{1,0:T(8,128)(2,1)S(1)}) custom-call(bf16[256,2560]{1,0:T(8,128)(2,1)} %query_ref.9, bf16[256,2560]{1,0:T(8,128)(2,1)} %key_ref.3, s32[4,27]{1,0:T(4,128)} %mask_ref.3, bf16[64,2560]{1,0:T(8,128)(2,1)} %bitcast.6), custom_call_target="tpu_custom_call" | custom-call | tf_op jit(solution)/shard_map/pallas_call | solution.py:653
  2.3 0.2 copy-done
  2.5 0.4 copy-done.1
  2.9 1.3 %copy-done.2 = bf16[256,2560]{1,0:T(8,128)(2,1)S(1)} copy-done((bf16[256,2560]{1,0:T(8,128)(2,1)S(1)}, bf16[256,2560]{1,0:T(8,128)(2,1)}, u32[]{:S(2)}) %copy-start.2) | copy-done | bytes 1310744
  4.2 0.6 %shard_map.95 = (bf16[128,3840]{1,0:T(8,128)(2,1)S(1)}, bf16[128,768]{1,0:T(8,128)(2,1)S(1)}) custom-call(bf16[256,2560]{1,0:T(8,128)(2,1)S(1)} %copy-done, bf16[256,2560]{1,0:T(8,128)(2,1)S(1)} %copy-done.1, bf16[256,2560]{1,0:T(8,128)(2,1)S(1)} %copy-done.2, bf16[64,2560]{1,0:T(8,128)(2,1)S(1)} %get-tuple-element.30.weight_ref), custom_call_target="tpu_custom_call" | custom-call | tf_op jit(solution)/shard_map/pallas_call | solution.py:653
  4.8 0.5 %collective-permute-start = (bf16[128,3840]{1,0:T(8,128)(2,1)S(1)}, bf16[128,3840]{1,0:T(8,128)(2,1)S(1)}, u32[]{:S(2)}, u32[]{:S(2)}) collective-permute-start(bf16[128,3840]{1,0:T(8,128)(2,1)S(1)} %get-tuple-element.31.refs_0_.near_ref), channel_id=1, source_target_pairs={{0,1},{1,0},{2,3},{3,2},{4,5},{5,4},{6,7},{7,6},{8,9},{9,8},{10,11... | collective-permute-start | bytes 2949128 | tf_op jit(solution)/shard_map/ppermute | solution.py:720
  5.3 0.2 copy-done.3
  5.5 0.6 %shard_map.96 = (bf16[128,2688]{1,0:T(8,128)(2,1)S(1)}, bf16[128,1152]{1,0:T(8,128)(2,1)S(1)}) custom-call(bf16[128,2560]{1,0:T(8,128)(2,1)S(1)} %get-tuple-element.32.key_ref, bf16[256,2560]{1,0:T(8,128)(2,1)S(1)} %copy-done.3, bf16[64,2560]{1,0:T(8,128)(2,1)S(1)} %get-tuple-element.30.weight_ref, bf16[128,1792]{1,0:T(8,128)(2,1)S(1)} %get-tuple-element.33.guest_ref), custom_call_target="tpu_custom_call" | custom-call | tf_op jit(solution)/shard_map/pallas_call | solution.py:653
  6.1 3.0 %collective-permute-start.4 = (bf16[128,2688]{1,0:T(8,128)(2,1)S(1)}, bf16[128,2688]{1,0:T(8,128)(2,1)S(1)}, u32[]{:S(2)}, u32[]{:S(2)}) collective-permute-start(bf16[128,2688]{1,0:T(8,128)(2,1)S(1)} %get-tuple-element.34.refs_1_.far_ref), channel_id=1, source_target_pairs={{0,16},{16,0},{1,2},{17,18},{2,1},{18,17},{3,19},{19,3},{4,20},{20... | collective-permute-start | bytes 2064392 | tf_op jit(solution)/shard_map/ppermute | solution.py:720
  9.1 1.6 %collective-permute-start.5 = (bf16[128,1792]{1,0:T(8,128)(2,1)S(1)}, bf16[128,1792]{1,0:T(8,128)(2,1)S(1)}, u32[]{:S(2)}, u32[]{:S(2)}) collective-permute-start(bf16[128,1792]{1,0:T(8,128)(2,1)S(1)} %get-tuple-element.33.guest_ref), channel_id=1, source_target_pairs={{0,4},{1,5},{2,6},{3,7},{4,0},{5,1},{6,2},{7,3},{8,12},{9,13},{10,... | collective-permute-start | bytes 1376264 | tf_op jit(solution)/shard_map/ppermute | solution.py:720
  10.7 0.5 %collective-permute-start.2 = (bf16[128,1152]{1,0:T(8,128)(2,1)S(1)}, bf16[128,1152]{1,0:T(8,128)(2,1)S(1)}, u32[]{:S(2)}, u32[]{:S(2)}) collective-permute-start(bf16[128,1152]{1,0:T(8,128)(2,1)S(1)} %get-tuple-element.35.refs_2_.far_ref), channel_id=1, source_target_pairs={{0,16},{16,0},{1,2},{17,18},{2,1},{18,17},{3,19},{19,3},{4,20},{20... | collective-permute-start | bytes 884744 | tf_op jit(solution)/shard_map/ppermute | solution.py:720
  11.2 0.0 collective-permute-start.3
  11.2 0.0 collective-permute-done.refs_3_.inner_ref
  11.2 2.0 %collective-permute-start.1 = (f32[4,128]{1,0:T(4,128)S(1)}, f32[4,128]{1,0:T(4,128)S(1)}, u32[]{:S(2)}, u32[]{:S(2)}) collective-permute-start(f32[4,128]{1,0:T(4,128)S(1)} %get-tuple-element.38), channel_id=1, source_target_pairs={{0,4},{1,5},{2,6},{3,7},{4,0},{5,1},{6,2},{7,3},{8,12},{9,13},{10,... | collective-permute-start | bytes 6152 | tf_op jit(solution)/shard_map/ppermute | solution.py:720
  13.2 3.1 %shard_map.97 = (f32[20,64,256]{2,1,0:T(8,128)S(1)}, f32[20,256]{1,0:T(8,128)S(1)}, f32[20,256]{1,0:T(8,128)S(1)}, f32[2,128]{1,0:T(2,128)S(1)}) custom-call(s32[4,27]{1,0:T(4,128)S(1)} %copy-done.5, bf16[256,2560]{1,0:T(8,128)(2,1)S(1)} %copy-done, bf16[128,3840]{1,0:T(8,128)(2,1)S(1)} %get-tuple-element.31.refs_0_.near_ref, ...), custom_call_target="tpu_custom_call" | custom-call | tf_op jit(solution)/shard_map/pallas_call | solution.py:653
  16.4 9.5 %collective-permute-done.1.guest_bias_ref = f32[4,128]{1,0:T(4,128)S(1)} collective-permute-done((f32[4,128]{1,0:T(4,128)S(1)}, f32[4,128]{1,0:T(4,128)S(1)}, u32[]{:S(2)}, u32[]{:S(2)}) %collective-permute-start.1) | collective-permute-done | bytes 2080 | tf_op jit(solution)/shard_map/ppermute | solution.py:720
  25.9 0.9 %shard_map.98 = (f32[6,64,128]{2,1,0:T(8,128)S(1)}, bf16[6,64,128]{2,1,0:T(8,128)(2,1)S(1)}, f32[6,128]{1,0:T(8,128)S(1)}, f32[6,256]{1,0:T(8,128)S(1)}, f32[6,256]{1,0:T(8,128)S(1)}, /*index=5*/f32[4,6,128]{2,1,0:T(8,128)S(1)}) custom-call(f32[2,128]{1,0:T(2,128)S(1)} %get-tuple-element.37.side_bias_ref, ...), custom_call_target="tpu_custom_call" | custom-call | tf_op jit(solution)/shard_map/pallas_call | solution.py:653
  26.8 1.6 %collective-permute-start.8 = (bf16[6,64,128]{2,1,0:T(8,128)(2,1)S(1)}, bf16[6,64,128]{2,1,0:T(8,128)(2,1)S(1)}, u32[]{:S(2)}, u32[]{:S(2)}) collective-permute-start(bf16[6,64,128]{2,1,0:T(8,128)(2,1)S(1)} %get-tuple-element.53), channel_id=1, source_target_pairs={{0,4},{1,5},{2,6},{3,7},{4,0},{5,1},{6,2},{7,3},{8,12},{9,13},{10,... | collective-permute-start | bytes 294920 | tf_op jit(solution)/shard_map/ppermute | solution.py:720
  28.4 0.0 collective-permute-done.5.guest_ref
  28.4 0.0 collective-permute-done.4.outer_ref
  28.4 1.6 %shard_map.99 = (f32[14,64,128]{2,1,0:T(8,128)S(1)}, f32[14,64,128]{2,1,0:T(8,128)S(1)}, f32[14,128]{1,0:T(8,128)S(1)}, f32[14,256]{1,0:T(8,128)S(1)}, f32[14,256]{1,0:T(8,128)S(1)}, /*index=5*/f32[4,14,128]{2,1,0:T(8,128)S(1)}) custom-call(f32[2,128]{1,0:T(2,128)S(1)} %get-tuple-element.37.side_bias_ref, ...), custom_call_target="tpu_custom_call" | custom-call | tf_op jit(solution)/shard_map/pallas_call | solution.py:653
  30.0 0.5 %collective-permute-start.6 = (f32[4,14,128]{2,1,0:T(8,128)S(1)}, f32[4,14,128]{2,1,0:T(8,128)S(1)}, u32[]{:S(2)}, u32[]{:S(2)}) collective-permute-start(f32[4,14,128]{2,1,0:T(8,128)S(1)} %get-tuple-element.50.sent_ref), channel_id=1, source_target_pairs={{0,4},{1,5},{2,6},{3,7},{4,0},{5,1},{6,2},{7,3},{8,12},{9,13},{10,... | collective-permute-start | bytes 86024 | tf_op jit(solution)/shard_map/ppermute | solution.py:720
  30.5 3.5 %collective-permute-done.6.got_ref = f32[4,14,128]{2,1,0:T(8,128)S(1)} collective-permute-done((f32[4,14,128]{2,1,0:T(8,128)S(1)}, f32[4,14,128]{2,1,0:T(8,128)S(1)}, u32[]{:S(2)}, u32[]{:S(2)}) %collective-permute-start.6) | collective-permute-done | bytes 28704 | tf_op jit(solution)/shard_map/ppermute | solution.py:720
  34.0 0.1 shard_map.101
  34.0 0.5 %collective-permute-start.7 = (f32[76,128]{1,0:T(8,128)S(1)}, f32[76,128]{1,0:T(8,128)S(1)}, u32[]{:S(2)}, u32[]{:S(2)}) collective-permute-start(f32[76,128]{1,0:T(8,128)S(1)} %shard_map.101), channel_id=1, source_target_pairs={{0,4},{1,5},{2,6},{3,7},{4,0},{5,1},{6,2},{7,3},{8,12},{9,13},{10,... | collective-permute-start | bytes 116744 | tf_op jit(solution)/shard_map/ppermute | solution.py:720
  34.5 0.2 shard_map.100.velocity_ref
  34.7 0.0 copy-start.4
  34.7 3.4 %collective-permute-done.7.back_ref = f32[76,128]{1,0:T(8,128)S(1)} collective-permute-done((f32[76,128]{1,0:T(8,128)S(1)}, f32[76,128]{1,0:T(8,128)S(1)}, u32[]{:S(2)}, u32[]{:S(2)}) %collective-permute-start.7) | collective-permute-done | bytes 38944 | tf_op jit(solution)/shard_map/ppermute | solution.py:720
  38.1 0.2 shard_map.102.velocity_ref
  38.4 2.8 %collective-permute-start.9 = (f32[64,256]{1,0:T(8,128)S(1)}, f32[64,256]{1,0:T(8,128)S(1)}, u32[]{:S(2)}, u32[]{:S(2)}) collective-permute-start(f32[64,256]{1,0:T(8,128)S(1)} %shard_map.102.velocity_ref), channel_id=1, source_target_pairs={{0,8},{1,9},{2,10},{3,11},{4,12},{5,13},{6,14},{7,15},{8,0},{9,1},... | collective-permute-start | bytes 196616 | tf_op jit(solution)/shard_map/ppermute | solution.py:720
  41.8 2.3 %collective-permute-done.9.partner_ref = f32[64,256]{1,0:T(8,128)S(1)} collective-permute-done((f32[64,256]{1,0:T(8,128)S(1)}, f32[64,256]{1,0:T(8,128)S(1)}, u32[]{:S(2)}, u32[]{:S(2)}) %collective-permute-start.9) | collective-permute-done | bytes 65568 | tf_op jit(solution)/shard_map/ppermute | solution.py:720
  44.2 1.0 %shard_map.103 = (f32[64,256]{1,0:T(8,128)}, f32[64,256]{1,0:T(8,128)}, f32[64,256]{1,0:T(8,128)}) custom-call(s32[1]{0:T(128)S(6)} %copy.10.step_ref, f32[64,256]{1,0:T(8,128)S(1)} %shard_map.102.velocity_ref, f32[64,256]{1,0:T(8,128)S(1)} %collective-permute-done.9.partner_ref, f32[64,256]{1,0:T(8,128)S(1)} %bitcast.5), custom_call_target="tpu_custom_call" | custom-call | tf_op jit(solution)/shard_map/pallas_call | solution.py:653
  (10 shorter events, 0.0 us)
Async XLA Ops:
  0.6 1.8 %copy-start = (bf16[256,2560]{1,0:T(8,128)(2,1)S(1)}, bf16[256,2560]{1,0:T(8,128)(2,1)}, u32[]{:S(2)}) copy-start(bf16[256,2560]{1,0:T(8,128)(2,1)} %query_ref.9) | copy-start | bytes 3932164
  0.6 2.2 %copy-start.1 = (bf16[256,2560]{1,0:T(8,128)(2,1)S(1)}, bf16[256,2560]{1,0:T(8,128)(2,1)}, u32[]{:S(2)}) copy-start(bf16[256,2560]{1,0:T(8,128)(2,1)} %key_ref.3) | copy-start | bytes 3932164
  2.9 1.3 %copy-start.2 = (bf16[256,2560]{1,0:T(8,128)(2,1)S(1)}, bf16[256,2560]{1,0:T(8,128)(2,1)}, u32[]{:S(2)}) copy-start(bf16[256,2560]{1,0:T(8,128)(2,1)} %value_ref.3) | copy-start | bytes 3932164
  4.2 1.3 %copy-start.3 = (bf16[256,2560]{1,0:T(8,128)(2,1)S(1)}, bf16[256,2560]{1,0:T(8,128)(2,1)}, u32[]{:S(2)}) copy-start(bf16[256,2560]{1,0:T(8,128)(2,1)} %value_ref.3) | copy-start | bytes 3932164
  4.8 6.5 %collective-permute-start = (bf16[128,3840]{1,0:T(8,128)(2,1)S(1)}, bf16[128,3840]{1,0:T(8,128)(2,1)S(1)}, u32[]{:S(2)}, u32[]{:S(2)}) collective-permute-start(bf16[128,3840]{1,0:T(8,128)(2,1)S(1)} %get-tuple-element.31.refs_0_.near_ref), channel_id=1, source_target_pairs={{0,1},{1,0},{2,3},{3,2},{4,5},{5,4},{6,7},{7,6},{8,9},{9,8},{10,11... | collective-permute-start | bytes 2949128 | tf_op jit(solution)/shard_map/ppermute | solution.py:720
  5.5 7.7 %copy-start.5 = (s32[4,27]{1,0:T(4,128)S(1)}, s32[4,27]{1,0:T(4,128)}, u32[]{:S(2)}) copy-start(s32[4,27]{1,0:T(4,128)} %mask_ref.3) | copy-start | bytes 1300
  6.1 22.3 %collective-permute-start.4 = (bf16[128,2688]{1,0:T(8,128)(2,1)S(1)}, bf16[128,2688]{1,0:T(8,128)(2,1)S(1)}, u32[]{:S(2)}, u32[]{:S(2)}) collective-permute-start(bf16[128,2688]{1,0:T(8,128)(2,1)S(1)} %get-tuple-element.34.refs_1_.far_ref), channel_id=1, source_target_pairs={{0,16},{16,0},{1,2},{17,18},{2,1},{18,17},{3,19},{19,3},{4,20},{20... | collective-permute-start | bytes 2064392 | tf_op jit(solution)/shard_map/ppermute | solution.py:720
  9.1 19.3 %collective-permute-start.5 = (bf16[128,1792]{1,0:T(8,128)(2,1)S(1)}, bf16[128,1792]{1,0:T(8,128)(2,1)S(1)}, u32[]{:S(2)}, u32[]{:S(2)}) collective-permute-start(bf16[128,1792]{1,0:T(8,128)(2,1)S(1)} %get-tuple-element.33.guest_ref), channel_id=1, source_target_pairs={{0,4},{1,5},{2,6},{3,7},{4,0},{5,1},{6,2},{7,3},{8,12},{9,13},{10,... | collective-permute-start | bytes 1376264 | tf_op jit(solution)/shard_map/ppermute | solution.py:720
  10.7 15.3 %collective-permute-start.2 = (bf16[128,1152]{1,0:T(8,128)(2,1)S(1)}, bf16[128,1152]{1,0:T(8,128)(2,1)S(1)}, u32[]{:S(2)}, u32[]{:S(2)}) collective-permute-start(bf16[128,1152]{1,0:T(8,128)(2,1)S(1)} %get-tuple-element.35.refs_2_.far_ref), channel_id=1, source_target_pairs={{0,16},{16,0},{1,2},{17,18},{2,1},{18,17},{3,19},{19,3},{4,20},{20... | collective-permute-start | bytes 884744 | tf_op jit(solution)/shard_map/ppermute | solution.py:720
  11.2 14.7 %collective-permute-start.3 = (bf16[128,768]{1,0:T(8,128)(2,1)S(1)}, bf16[128,768]{1,0:T(8,128)(2,1)S(1)}, u32[]{:S(2)}, u32[]{:S(2)}) collective-permute-start(bf16[128,768]{1,0:T(8,128)(2,1)S(1)} %get-tuple-element.39), channel_id=1, source_target_pairs={{0,4},{1,5},{2,6},{3,7},{4,0},{5,1},{6,2},{7,3},{8,12},{9,13},{10,... | collective-permute-start | bytes 589832 | tf_op jit(solution)/shard_map/ppermute | solution.py:720
  11.2 14.7 %collective-permute-start.1 = (f32[4,128]{1,0:T(4,128)S(1)}, f32[4,128]{1,0:T(4,128)S(1)}, u32[]{:S(2)}, u32[]{:S(2)}) collective-permute-start(f32[4,128]{1,0:T(4,128)S(1)} %get-tuple-element.38), channel_id=1, source_target_pairs={{0,4},{1,5},{2,6},{3,7},{4,0},{5,1},{6,2},{7,3},{8,12},{9,13},{10,... | collective-permute-start | bytes 6152 | tf_op jit(solution)/shard_map/ppermute | solution.py:720
  26.8 11.3 %collective-permute-start.8 = (bf16[6,64,128]{2,1,0:T(8,128)(2,1)S(1)}, bf16[6,64,128]{2,1,0:T(8,128)(2,1)S(1)}, u32[]{:S(2)}, u32[]{:S(2)}) collective-permute-start(bf16[6,64,128]{2,1,0:T(8,128)(2,1)S(1)} %get-tuple-element.53), channel_id=1, source_target_pairs={{0,4},{1,5},{2,6},{3,7},{4,0},{5,1},{6,2},{7,3},{8,12},{9,13},{10,... | collective-permute-start | bytes 294920 | tf_op jit(solution)/shard_map/ppermute | solution.py:720
  30.0 4.0 %collective-permute-start.6 = (f32[4,14,128]{2,1,0:T(8,128)S(1)}, f32[4,14,128]{2,1,0:T(8,128)S(1)}, u32[]{:S(2)}, u32[]{:S(2)}) collective-permute-start(f32[4,14,128]{2,1,0:T(8,128)S(1)} %get-tuple-element.50.sent_ref), channel_id=1, source_target_pairs={{0,4},{1,5},{2,6},{3,7},{4,0},{5,1},{6,2},{7,3},{8,12},{9,13},{10,... | collective-permute-start | bytes 86024 | tf_op jit(solution)/shard_map/ppermute | solution.py:720
  34.0 4.1 %collective-permute-start.7 = (f32[76,128]{1,0:T(8,128)S(1)}, f32[76,128]{1,0:T(8,128)S(1)}, u32[]{:S(2)}, u32[]{:S(2)}) collective-permute-start(f32[76,128]{1,0:T(8,128)S(1)} %shard_map.101), channel_id=1, source_target_pairs={{0,4},{1,5},{2,6},{3,7},{4,0},{5,1},{6,2},{7,3},{8,12},{9,13},{10,... | collective-permute-start | bytes 116744 | tf_op jit(solution)/shard_map/ppermute | solution.py:720
  34.7 9.4 %copy-start.4 = (f32[256,64]{0,1:T(8,128)S(1)}, f32[256,64]{0,1:T(8,128)}, u32[]{:S(2)}) copy-start(f32[256,64]{0,1:T(8,128)} %param.12) | copy-start | bytes 196612
  38.4 5.8 %collective-permute-start.9 = (f32[64,256]{1,0:T(8,128)S(1)}, f32[64,256]{1,0:T(8,128)S(1)}, u32[]{:S(2)}, u32[]{:S(2)}) collective-permute-start(f32[64,256]{1,0:T(8,128)S(1)} %shard_map.102.velocity_ref), channel_id=1, source_target_pairs={{0,8},{1,9},{2,10},{3,11},{4,12},{5,13},{6,14},{7,15},{8,0},{9,1},... | collective-permute-start | bytes 196616 | tf_op jit(solution)/shard_map/ppermute | solution.py:720

commit v5 on v4

--- a/solution.py
+++ b/solution.py
@@ -465,8 +465,8 @@
     block_count, block_cols, tile_tok, group,
     side_bias_ref, guest_bias_ref,
     query_ref, near_ref, far_ref, inner_ref, outer_ref, guest_ref, own_top_ref, own_sum_ref,
-    out_ref, guest_out_ref, side_top_ref, top_ref, sum_ref, send_ref,
-    side_scores, guest_scores, side_weights, guest_weights,
+    out_ref, guest_out_ref, side_top_ref, guest_top_ref, log_ref, send_ref,
+    side_scores, guest_scores, side_weights, guest_weights, side_sum_ref, guest_sum_ref,
 ):
     spot = Spot(block_count, block_cols)
     channels = out_ref.shape[1]
@@ -496,49 +496,51 @@
         scores = contract_last(keys, guest_ref[:, head_lanes(row)])
         scores = biased(scores, guest_bias, tile_tok)
         guest_scores[row] = scores
-        send_ref[2, row : row + 1] = largest(scores)
+        guest_top_ref[row : row + 1] = largest(scores)
 
     def soften(head):
         row = head - group.start
         side_weights[row] = softened(side_scores[row], side_top_ref[row : row + 1])
-        guest_weights[row] = softened(guest_scores[row], send_ref[2, row : row + 1])
+        guest_weights[row] = softened(guest_scores[row], guest_top_ref[row : row + 1])
 
     def weigh(head):
         row = head - group.start
         side = contract(with_ones(outer_column.folded(head)), side_weights[row])
         out_ref[row] = side[:channels]
-        sum_ref[row : row + 1, half:] = side[channels : channels + 1]
+        side_sum_ref[row : row + 1] = side[channels : channels + 1]
         folded = beside(
             jnp.where(left, near_column.folded(head), far_column.folded(head)),
             jnp.where(left, inner_column.folded(head), outer_column.folded(head)),
         )
         guest = contract(with_ones(folded), guest_weights[row])
         guest_out_ref[row] = guest[:channels].astype(guest_out_ref.dtype)
-        send_ref[3, row : row + 1] = guest[channels : channels + 1]
+        guest_sum_ref[row : row + 1] = guest[channels : channels + 1]
 
     pipelined(group, score, soften, weigh)
 
     mine = slice(group.start, group.stop)
-    near_top = own_top_ref[mine, :half]
-    near_sum = own_sum_ref[mine, :half]
-    old_top = own_top_ref[mine, half:]
-    side_top = side_top_ref[...]
-    far_top, far_sum = shares(
-        old_top, own_sum_ref[mine, half:], side_top, sum_ref[:, half:]
-    )
-    top_ref[:, :half] = near_top
-    top_ref[:, half:] = far_top
-    sum_ref[:, :half] = near_sum
-    sum_ref[:, half:] = far_sum
-    send_ref[0] = beside(near_top[:, tile_tok:], far_top[:, :tile_tok])
-    send_ref[1] = beside(near_sum[:, tile_tok:], far_sum[:, :tile_tok])
-
-
-def shares(near_top, near_sum, away_top, away_sum):
-    top = jnp.maximum(near_top, away_top)
-    near = jnp.exp2((near_top - top) * EXP_SCALE) * near_sum
-    away = jnp.exp2((away_top - top) * EXP_SCALE) * away_sum
-    return top, near + away
+    near_log = log_sum(own_top_ref[mine, :half], own_sum_ref[mine, :half])
+    far_log = joint(
+        log_sum(own_top_ref[mine, half:], own_sum_ref[mine, half:]),
+        log_sum(side_top_ref[...], side_sum_ref[...]),
+    )
+    log_ref[:, :half] = near_log
+    log_ref[:, half:] = far_log
+    send_ref[0] = beside(near_log[:, tile_tok:], far_log[:, :tile_tok])
+    send_ref[1] = log_sum(guest_top_ref[...], guest_sum_ref[...])
+
+
+def log_sum(top, total):
+    return top * EXP_SCALE + jnp.log2(total)
+
+
+def joint(left, right):
+    top = jnp.maximum(left, right)
+    return top + jnp.log2(jnp.exp2(left - top) + jnp.exp2(right - top))
+
+
+def share_of(top, whole):
+    return jnp.exp2(top * EXP_SCALE - whole)
 
 
 def centred(values, fill, tile_tok):
@@ -546,28 +548,24 @@
     return jnp.concatenate([side, values, side], axis=1)
 
 
-def guest_blend_kernel(guest_out_ref, sent_ref, got_ref, late_ref, back_ref):
+def guest_blend_kernel(
+    guest_out_ref, guest_top_ref, sent_ref, got_ref, late_top_ref, late_sent_ref, back_ref
+):
     heads, channels, _ = guest_out_ref.shape
-    top, total = shares(sent_ref[2], sent_ref[3], got_ref[0], got_ref[1])
-    share = jnp.exp2((sent_ref[2] - top) * EXP_SCALE) / total
+    share = share_of(guest_top_ref[...], joint(sent_ref[1], got_ref[0]))
     velocity = jnp.zeros(guest_out_ref.shape[1:], jnp.float32)
     for row in range(heads):
         velocity = velocity + share[row : row + 1] * guest_out_ref[row]
+    late = late_top_ref.shape[0]
     back_ref[:channels] = velocity
-    late = late_ref.shape[1]
-    back_ref[channels : channels + late] = late_ref[2]
-    back_ref[channels + late : channels + 2 * late] = late_ref[3]
-
-
-def own_part(tile_tok, group, own_out_ref, side_out_ref, own_top_ref, side_top_ref,
-             top, total, far_top, far_total):
+    back_ref[channels : channels + late] = late_sent_ref[1]
+    back_ref[channels + late : channels + 2 * late] = late_top_ref[...]
+
+
+def own_part(tile_tok, group, own_out_ref, side_out_ref, own_top_ref, side_top_ref, whole):
     half = 2 * tile_tok
-    top, total = shares(
-        top, total, centred(far_top, NEG, tile_tok), centred(far_total, 0.0, tile_tok)
-    )
-    own_top = own_top_ref[group.start : group.stop]
-    own_share = jnp.exp2((own_top - top) * EXP_SCALE) / total
-    side_share = jnp.exp2((side_top_ref[...] - top[:, half:]) * EXP_SCALE) / total[:, half:]
+    own_share = share_of(own_top_ref[group.start : group.stop], whole)
+    side_share = share_of(side_top_ref[...], whole[:, half:])
     near = jnp.zeros((own_out_ref.shape[1], half), jnp.float32)
     far = jnp.zeros((own_out_ref.shape[1], half), jnp.float32)
     for row, head in enumerate(group):
@@ -575,32 +573,33 @@
         near = near + own_share[one, :half] * own_out_ref[head, :, :half]
         far = far + own_share[one, half:] * own_out_ref[head, :, half:]
         far = far + side_share[one] * side_out_ref[row]
-    guest_top = beside(top[:, tile_tok:half], top[:, half : half + tile_tok])
-    guest_total = beside(total[:, tile_tok:half], total[:, half : half + tile_tok])
-    return beside(near, far), jnp.exp2((far_top - guest_top) * EXP_SCALE) / guest_total
+    return beside(near, far)
 
 
 def own_blend_kernel(
     tile_tok, group, own_out_ref, side_out_ref, own_top_ref, side_top_ref,
-    top_ref, sum_ref, got_ref, velocity_ref,
+    log_ref, got_ref, velocity_ref,
 ):
-    velocity_ref[...], _ = own_part(
-        tile_tok, group, own_out_ref, side_out_ref, own_top_ref, side_top_ref,
-        top_ref[...], sum_ref[...], got_ref[2], got_ref[3],
+    whole = joint(log_ref[...], centred(got_ref[1], NEG, tile_tok))
+    velocity_ref[...] = own_part(
+        tile_tok, group, own_out_ref, side_out_ref, own_top_ref, side_top_ref, whole
     )
 
 
 def join_kernel(
     tile_tok, group, own_out_ref, side_out_ref, own_top_ref, side_top_ref,
-    top_ref, sum_ref, velocity_ref, back_ref, back_out_ref, out_ref,
+    log_ref, velocity_ref, back_ref, back_out_ref, out_ref,
 ):
     channels = own_out_ref.shape[1]
+    half = 2 * tile_tok
     late = len(group)
-    velocity, share = own_part(
-        tile_tok, group, own_out_ref, side_out_ref, own_top_ref, side_top_ref,
-        top_ref[...], sum_ref[...],
-        back_ref[channels : channels + late], back_ref[channels + late : channels + 2 * late],
-    )
+    guest_log = back_ref[channels : channels + late]
+    whole = joint(log_ref[...], centred(guest_log, NEG, tile_tok))
+    velocity = own_part(
+        tile_tok, group, own_out_ref, side_out_ref, own_top_ref, side_top_ref, whole
+    )
+    edge = beside(whole[:, tile_tok:half], whole[:, half : half + tile_tok])
+    share = share_of(back_ref[channels + late : channels + 2 * late], edge)
     guest = back_ref[:channels]
     for row in range(late):
         guest = guest + share[row : row + 1] * back_out_ref[row].astype(jnp.float32)
@@ -764,9 +763,9 @@
                 ((heads, channels, half), single),
                 ((heads, channels, half), guest_type),
                 ((heads, half), single),
+                ((heads, half), single),
                 ((heads, tok_rows), single),
-                ((heads, tok_rows), single),
-                ((4, heads, half), single),
+                ((2, heads, half), single),
             ),
             0,
             (
@@ -774,15 +773,17 @@
                 pltpu.VMEM((heads, tok_rows, half), single),
                 pltpu.VMEM((heads, half, half), half_type),
                 pltpu.VMEM((heads, tok_rows, half), half_type),
+                pltpu.VMEM((heads, half), single),
+                pltpu.VMEM((heads, half), single),
             ),
         )
 
-    side_out, guest_out, side_top, top, total, sent = edge(0, single)
+    side_out, guest_out, side_top, guest_top, log, sent = edge(0, single)
     got = sent_over(sent, row_pairs)
-    late_side, late_guest, late_side_top, late_top, late_total, late_sent = edge(1, half_type)
+    late_side, late_guest, late_side_top, late_guest_top, late_log, late_sent = edge(1, half_type)
     (guest_velocity,) = kernel_call(
         guest_blend_kernel,
-        (guest_out, sent, got, late_sent),
+        (guest_out, guest_top, sent, got, late_guest_top, late_sent),
         (((channels + 2 * late, half), single),),
     )
     back = sent_over(guest_velocity, row_pairs)
@@ -790,13 +791,13 @@
     velocity_type = ((channels, tok_rows), single)
     (velocity,) = kernel_call(
         functools.partial(own_blend_kernel, tile_tok, groups[0]),
-        (own_out, side_out, own_top, side_top, top, total, got),
+        (own_out, side_out, own_top, side_top, log, got),
         (velocity_type,),
     )
     (velocity,) = kernel_call(
         functools.partial(join_kernel, tile_tok, groups[1]),
         (
-            own_out, late_side, own_top, late_side_top, late_top, late_total, velocity,
+            own_out, late_side, own_top, late_side_top, late_log, velocity,
             back, back_out,
         ),
         (velocity_type,),

time: 45.4 us -> 45.2 us (level)
  transfers between devices with their start and end apart: 10 -> 10, of which waited for: 4 -> 4; matrix products, arithmetic and copies ran while one was open for 0% -> 0% of each run, Pallas kernels for 14% -> 15%
where the time goes in v5:
time: 45.2 us; the launch traced here: 45 us
  waiting for transfers between devices  18.6 us (41%)
  starting transfers between devices  13 us (29%)
  Pallas kernels  9.96 us (22%)
  local copies, waits for them, and re-layouts  2.11 us (5%)
  between operations  1.36 us (3%)
    ppermute x10, waiting for transfers between devices, sent_over(): return lax.ppermute(value, axes, pairs)  18.6 us
    ppermute x10, starting transfers between devices, sent_over(): return lax.ppermute(value, axes, pairs)  13 us
    pallas_call x10, Pallas kernels, kernel_call(): pl.pallas_call(body, out_shape=[pltpu.VMEM(shape, dtype) if stay else jax...  9.96 us
    unnamed x12, local copies, waits for them, and re-layouts  2.11 us
  transfers between devices with their start and end apart: 10, of which 4 were waited for; matrix products, arithmetic and copies ran while one was open for 0% of the time, Pallas kernels for 15%

profile of v5, /device:TPU:0, one launch (start us, length us, event | category | flops | bytes accessed | tf_op | source)
XLA Modules:
  0.0 45.0 jit_solution(14476898721088155178)
XLA Ops:
  0.7 1.6 %shard_map.94 = (bf16[128,1792]{1,0:T(8,128)(2,1)S(1)}, f32[4,128]{1,0:T(4,128)S(1)}, bf16[128,2560]{1,0:T(8,128)(2,1)S(1)}, bf16[64,2560]{1,0:T(8,128)(2,1)S(1)}) custom-call(bf16[256,2560]{1,0:T(8,128)(2,1)} %query_ref.9, bf16[256,2560]{1,0:T(8,128)(2,1)} %key_ref.3, s32[4,27]{1,0:T(4,128)} %mask_ref.3, bf16[64,2560]{1,0:T(8,128)(2,1)} %bitcast.6), custom_call_target="tpu_custom_call" | custom-call | tf_op jit(solution)/shard_map/pallas_call | solution.py:652
  2.3 0.2 copy-done
  2.5 0.4 copy-done.1
  2.9 1.3 %copy-done.2 = bf16[256,2560]{1,0:T(8,128)(2,1)S(1)} copy-done((bf16[256,2560]{1,0:T(8,128)(2,1)S(1)}, bf16[256,2560]{1,0:T(8,128)(2,1)}, u32[]{:S(2)}) %copy-start.2) | copy-done | bytes 1310744
  4.2 0.6 %shard_map.95 = (bf16[128,3840]{1,0:T(8,128)(2,1)S(1)}, bf16[128,768]{1,0:T(8,128)(2,1)S(1)}) custom-call(bf16[256,2560]{1,0:T(8,128)(2,1)S(1)} %copy-done, bf16[256,2560]{1,0:T(8,128)(2,1)S(1)} %copy-done.1, bf16[256,2560]{1,0:T(8,128)(2,1)S(1)} %copy-done.2, bf16[64,2560]{1,0:T(8,128)(2,1)S(1)} %get-tuple-element.30.weight_ref), custom_call_target="tpu_custom_call" | custom-call | tf_op jit(solution)/shard_map/pallas_call | solution.py:652
  4.8 0.5 %collective-permute-start = (bf16[128,3840]{1,0:T(8,128)(2,1)S(1)}, bf16[128,3840]{1,0:T(8,128)(2,1)S(1)}, u32[]{:S(2)}, u32[]{:S(2)}) collective-permute-start(bf16[128,3840]{1,0:T(8,128)(2,1)S(1)} %get-tuple-element.31.refs_0_.near_ref), channel_id=1, source_target_pairs={{0,1},{1,0},{2,3},{3,2},{4,5},{5,4},{6,7},{7,6},{8,9},{9,8},{10,11... | collective-permute-start | bytes 2949128 | tf_op jit(solution)/shard_map/ppermute | solution.py:719
  5.3 0.2 copy-done.3
  5.5 0.6 %shard_map.96 = (bf16[128,2688]{1,0:T(8,128)(2,1)S(1)}, bf16[128,1152]{1,0:T(8,128)(2,1)S(1)}) custom-call(bf16[128,2560]{1,0:T(8,128)(2,1)S(1)} %get-tuple-element.32.key_ref, bf16[256,2560]{1,0:T(8,128)(2,1)S(1)} %copy-done.3, bf16[64,2560]{1,0:T(8,128)(2,1)S(1)} %get-tuple-element.30.weight_ref, bf16[128,1792]{1,0:T(8,128)(2,1)S(1)} %get-tuple-element.33.guest_ref), custom_call_target="tpu_custom_call" | custom-call | tf_op jit(solution)/shard_map/pallas_call | solution.py:652
  6.1 3.0 %collective-permute-start.4 = (bf16[128,2688]{1,0:T(8,128)(2,1)S(1)}, bf16[128,2688]{1,0:T(8,128)(2,1)S(1)}, u32[]{:S(2)}, u32[]{:S(2)}) collective-permute-start(bf16[128,2688]{1,0:T(8,128)(2,1)S(1)} %get-tuple-element.34.refs_1_.far_ref), channel_id=1, source_target_pairs={{0,16},{16,0},{1,2},{17,18},{2,1},{18,17},{3,19},{19,3},{4,20},{20... | collective-permute-start | bytes 2064392 | tf_op jit(solution)/shard_map/ppermute | solution.py:719
  9.1 1.6 %collective-permute-start.5 = (bf16[128,1792]{1,0:T(8,128)(2,1)S(1)}, bf16[128,1792]{1,0:T(8,128)(2,1)S(1)}, u32[]{:S(2)}, u32[]{:S(2)}) collective-permute-start(bf16[128,1792]{1,0:T(8,128)(2,1)S(1)} %get-tuple-element.33.guest_ref), channel_id=1, source_target_pairs={{0,4},{1,5},{2,6},{3,7},{4,0},{5,1},{6,2},{7,3},{8,12},{9,13},{10,... | collective-permute-start | bytes 1376264 | tf_op jit(solution)/shard_map/ppermute | solution.py:719
  10.7 0.5 %collective-permute-start.2 = (bf16[128,1152]{1,0:T(8,128)(2,1)S(1)}, bf16[128,1152]{1,0:T(8,128)(2,1)S(1)}, u32[]{:S(2)}, u32[]{:S(2)}) collective-permute-start(bf16[128,1152]{1,0:T(8,128)(2,1)S(1)} %get-tuple-element.35.refs_2_.far_ref), channel_id=1, source_target_pairs={{0,16},{16,0},{1,2},{17,18},{2,1},{18,17},{3,19},{19,3},{4,20},{20... | collective-permute-start | bytes 884744 | tf_op jit(solution)/shard_map/ppermute | solution.py:719
  11.2 0.0 collective-permute-start.3
  11.2 2.0 %collective-permute-start.1 = (f32[4,128]{1,0:T(4,128)S(1)}, f32[4,128]{1,0:T(4,128)S(1)}, u32[]{:S(2)}, u32[]{:S(2)}) collective-permute-start(f32[4,128]{1,0:T(4,128)S(1)} %get-tuple-element.38), channel_id=1, source_target_pairs={{0,4},{1,5},{2,6},{3,7},{4,0},{5,1},{6,2},{7,3},{8,12},{9,13},{10,... | collective-permute-start | bytes 6152 | tf_op jit(solution)/shard_map/ppermute | solution.py:719
  13.2 3.2 %shard_map.97 = (f32[20,64,256]{2,1,0:T(8,128)S(1)}, f32[20,256]{1,0:T(8,128)S(1)}, f32[20,256]{1,0:T(8,128)S(1)}, f32[2,128]{1,0:T(2,128)S(1)}) custom-call(s32[4,27]{1,0:T(4,128)S(1)} %copy-done.5, bf16[256,2560]{1,0:T(8,128)(2,1)S(1)} %copy-done, bf16[128,3840]{1,0:T(8,128)(2,1)S(1)} %get-tuple-element.31.refs_0_.near_ref, ...), custom_call_target="tpu_custom_call" | custom-call | tf_op jit(solution)/shard_map/pallas_call | solution.py:652
  16.4 9.5 %collective-permute-done.1.guest_bias_ref = f32[4,128]{1,0:T(4,128)S(1)} collective-permute-done((f32[4,128]{1,0:T(4,128)S(1)}, f32[4,128]{1,0:T(4,128)S(1)}, u32[]{:S(2)}, u32[]{:S(2)}) %collective-permute-start.1) | collective-permute-done | bytes 2080 | tf_op jit(solution)/shard_map/ppermute | solution.py:719
  25.9 0.9 %shard_map.98 = (f32[6,64,128]{2,1,0:T(8,128)S(1)}, bf16[6,64,128]{2,1,0:T(8,128)(2,1)S(1)}, f32[6,128]{1,0:T(8,128)S(1)}, f32[6,128]{1,0:T(8,128)S(1)}, f32[6,256]{1,0:T(8,128)S(1)}, /*index=5*/f32[2,6,128]{2,1,0:T(8,128)S(1)}) custom-call(f32[2,128]{1,0:T(2,128)S(1)} %get-tuple-element.37.side_bias_ref, ...), custom_call_target="tpu_custom_call" | custom-call | tf_op jit(solution)/shard_map/pallas_call | solution.py:652
  26.8 1.6 %collective-permute-start.8 = (bf16[6,64,128]{2,1,0:T(8,128)(2,1)S(1)}, bf16[6,64,128]{2,1,0:T(8,128)(2,1)S(1)}, u32[]{:S(2)}, u32[]{:S(2)}) collective-permute-start(bf16[6,64,128]{2,1,0:T(8,128)(2,1)S(1)} %get-tuple-element.53), channel_id=1, source_target_pairs={{0,4},{1,5},{2,6},{3,7},{4,0},{5,1},{6,2},{7,3},{8,12},{9,13},{10,... | collective-permute-start | bytes 294920 | tf_op jit(solution)/shard_map/ppermute | solution.py:719
  28.4 0.0 collective-permute-done.5.guest_ref
  28.4 0.0 collective-permute-done.4.outer_ref
  28.4 1.6 %shard_map.99 = (f32[14,64,128]{2,1,0:T(8,128)S(1)}, f32[14,64,128]{2,1,0:T(8,128)S(1)}, f32[14,128]{1,0:T(8,128)S(1)}, f32[14,128]{1,0:T(8,128)S(1)}, f32[14,256]{1,0:T(8,128)S(1)}, /*index=5*/f32[2,14,128]{2,1,0:T(8,128)S(1)}) custom-call(f32[2,128]{1,0:T(2,128)S(1)} %get-tuple-element.37.side_bias_ref, ...), custom_call_target="tpu_custom_call" | custom-call | tf_op jit(solution)/shard_map/pallas_call | solution.py:652
  30.1 0.5 %collective-permute-start.6 = (f32[2,14,128]{2,1,0:T(8,128)S(1)}, f32[2,14,128]{2,1,0:T(8,128)S(1)}, u32[]{:S(2)}, u32[]{:S(2)}) collective-permute-start(f32[2,14,128]{2,1,0:T(8,128)S(1)} %get-tuple-element.48.sent_ref), channel_id=1, source_target_pairs={{0,4},{1,5},{2,6},{3,7},{4,0},{5,1},{6,2},{7,3},{8,12},{9,13},{10,... | collective-permute-start | bytes 43016 | tf_op jit(solution)/shard_map/ppermute | solution.py:719
  30.5 3.3 %collective-permute-done.6.got_ref = f32[2,14,128]{2,1,0:T(8,128)S(1)} collective-permute-done((f32[2,14,128]{2,1,0:T(8,128)S(1)}, f32[2,14,128]{2,1,0:T(8,128)S(1)}, u32[]{:S(2)}, u32[]{:S(2)}) %collective-permute-start.6) | collective-permute-done | bytes 14368 | tf_op jit(solution)/shard_map/ppermute | solution.py:719
  33.8 0.1 shard_map.101
  33.9 0.5 %collective-permute-start.7 = (f32[76,128]{1,0:T(8,128)S(1)}, f32[76,128]{1,0:T(8,128)S(1)}, u32[]{:S(2)}, u32[]{:S(2)}) collective-permute-start(f32[76,128]{1,0:T(8,128)S(1)} %shard_map.101), channel_id=1, source_target_pairs={{0,4},{1,5},{2,6},{3,7},{4,0},{5,1},{6,2},{7,3},{8,12},{9,13},{10,... | collective-permute-start | bytes 116744 | tf_op jit(solution)/shard_map/ppermute | solution.py:719
  34.4 0.2 shard_map.100.velocity_ref
  34.6 0.0 copy-start.4
  34.6 3.3 %collective-permute-done.7.back_ref = f32[76,128]{1,0:T(8,128)S(1)} collective-permute-done((f32[76,128]{1,0:T(8,128)S(1)}, f32[76,128]{1,0:T(8,128)S(1)}, u32[]{:S(2)}, u32[]{:S(2)}) %collective-permute-start.7) | collective-permute-done | bytes 38944 | tf_op jit(solution)/shard_map/ppermute | solution.py:719
  38.0 0.0 collective-permute-done.8.back_out_ref
  38.0 0.2 shard_map.102.velocity_ref
  38.2 2.7 %collective-permute-start.9 = (f32[64,256]{1,0:T(8,128)S(1)}, f32[64,256]{1,0:T(8,128)S(1)}, u32[]{:S(2)}, u32[]{:S(2)}) collective-permute-start(f32[64,256]{1,0:T(8,128)S(1)} %shard_map.102.velocity_ref), channel_id=1, source_target_pairs={{0,8},{1,9},{2,10},{3,11},{4,12},{5,13},{6,14},{7,15},{8,0},{9,1},... | collective-permute-start | bytes 196616 | tf_op jit(solution)/shard_map/ppermute | solution.py:719
  41.5 2.5 %collective-permute-done.9.partner_ref = f32[64,256]{1,0:T(8,128)S(1)} collective-permute-done((f32[64,256]{1,0:T(8,128)S(1)}, f32[64,256]{1,0:T(8,128)S(1)}, u32[]{:S(2)}, u32[]{:S(2)}) %collective-permute-start.9) | collective-permute-done | bytes 65568 | tf_op jit(solution)/shard_map/ppermute | solution.py:719
  44.0 1.0 %shard_map.103 = (f32[64,256]{1,0:T(8,128)}, f32[64,256]{1,0:T(8,128)}, f32[64,256]{1,0:T(8,128)}) custom-call(s32[1]{0:T(128)S(6)} %copy.10.step_ref, f32[64,256]{1,0:T(8,128)S(1)} %shard_map.102.velocity_ref, f32[64,256]{1,0:T(8,128)S(1)} %collective-permute-done.9.partner_ref, f32[64,256]{1,0:T(8,128)S(1)} %bitcast.5), custom_call_target="tpu_custom_call" | custom-call | tf_op jit(solution)/shard_map/pallas_call | solution.py:652
  (10 shorter events, 0.0 us)
Async XLA Ops:
  0.6 1.8 %copy-start = (bf16[256,2560]{1,0:T(8,128)(2,1)S(1)}, bf16[256,2560]{1,0:T(8,128)(2,1)}, u32[]{:S(2)}) copy-start(bf16[256,2560]{1,0:T(8,128)(2,1)} %query_ref.9) | copy-start | bytes 3932164
  0.6 2.2 %copy-start.1 = (bf16[256,2560]{1,0:T(8,128)(2,1)S(1)}, bf16[256,2560]{1,0:T(8,128)(2,1)}, u32[]{:S(2)}) copy-start(bf16[256,2560]{1,0:T(8,128)(2,1)} %key_ref.3) | copy-start | bytes 3932164
  2.9 1.3 %copy-start.2 = (bf16[256,2560]{1,0:T(8,128)(2,1)S(1)}, bf16[256,2560]{1,0:T(8,128)(2,1)}, u32[]{:S(2)}) copy-start(bf16[256,2560]{1,0:T(8,128)(2,1)} %value_ref.3) | copy-start | bytes 3932164
  4.2 1.3 %copy-start.3 = (bf16[256,2560]{1,0:T(8,128)(2,1)S(1)}, bf16[256,2560]{1,0:T(8,128)(2,1)}, u32[]{:S(2)}) copy-start(bf16[256,2560]{1,0:T(8,128)(2,1)} %value_ref.3) | copy-start | bytes 3932164
  4.8 6.5 %collective-permute-start = (bf16[128,3840]{1,0:T(8,128)(2,1)S(1)}, bf16[128,3840]{1,0:T(8,128)(2,1)S(1)}, u32[]{:S(2)}, u32[]{:S(2)}) collective-permute-start(bf16[128,3840]{1,0:T(8,128)(2,1)S(1)} %get-tuple-element.31.refs_0_.near_ref), channel_id=1, source_target_pairs={{0,1},{1,0},{2,3},{3,2},{4,5},{5,4},{6,7},{7,6},{8,9},{9,8},{10,11... | collective-permute-start | bytes 2949128 | tf_op jit(solution)/shard_map/ppermute | solution.py:719
  5.5 7.7 %copy-start.5 = (s32[4,27]{1,0:T(4,128)S(1)}, s32[4,27]{1,0:T(4,128)}, u32[]{:S(2)}) copy-start(s32[4,27]{1,0:T(4,128)} %mask_ref.3) | copy-start | bytes 1300
  6.1 22.4 %collective-permute-start.4 = (bf16[128,2688]{1,0:T(8,128)(2,1)S(1)}, bf16[128,2688]{1,0:T(8,128)(2,1)S(1)}, u32[]{:S(2)}, u32[]{:S(2)}) collective-permute-start(bf16[128,2688]{1,0:T(8,128)(2,1)S(1)} %get-tuple-element.34.refs_1_.far_ref), channel_id=1, source_target_pairs={{0,16},{16,0},{1,2},{17,18},{2,1},{18,17},{3,19},{19,3},{4,20},{20... | collective-permute-start | bytes 2064392 | tf_op jit(solution)/shard_map/ppermute | solution.py:719
  9.1 19.3 %collective-permute-start.5 = (bf16[128,1792]{1,0:T(8,128)(2,1)S(1)}, bf16[128,1792]{1,0:T(8,128)(2,1)S(1)}, u32[]{:S(2)}, u32[]{:S(2)}) collective-permute-start(bf16[128,1792]{1,0:T(8,128)(2,1)S(1)} %get-tuple-element.33.guest_ref), channel_id=1, source_target_pairs={{0,4},{1,5},{2,6},{3,7},{4,0},{5,1},{6,2},{7,3},{8,12},{9,13},{10,... | collective-permute-start | bytes 1376264 | tf_op jit(solution)/shard_map/ppermute | solution.py:719
  10.7 15.3 %collective-permute-start.2 = (bf16[128,1152]{1,0:T(8,128)(2,1)S(1)}, bf16[128,1152]{1,0:T(8,128)(2,1)S(1)}, u32[]{:S(2)}, u32[]{:S(2)}) collective-permute-start(bf16[128,1152]{1,0:T(8,128)(2,1)S(1)} %get-tuple-element.35.refs_2_.far_ref), channel_id=1, source_target_pairs={{0,16},{16,0},{1,2},{17,18},{2,1},{18,17},{3,19},{19,3},{4,20},{20... | collective-permute-start | bytes 884744 | tf_op jit(solution)/shard_map/ppermute | solution.py:719
  11.2 14.7 %collective-permute-start.3 = (bf16[128,768]{1,0:T(8,128)(2,1)S(1)}, bf16[128,768]{1,0:T(8,128)(2,1)S(1)}, u32[]{:S(2)}, u32[]{:S(2)}) collective-permute-start(bf16[128,768]{1,0:T(8,128)(2,1)S(1)} %get-tuple-element.39), channel_id=1, source_target_pairs={{0,4},{1,5},{2,6},{3,7},{4,0},{5,1},{6,2},{7,3},{8,12},{9,13},{10,... | collective-permute-start | bytes 589832 | tf_op jit(solution)/shard_map/ppermute | solution.py:719
  11.2 14.7 %collective-permute-start.1 = (f32[4,128]{1,0:T(4,128)S(1)}, f32[4,128]{1,0:T(4,128)S(1)}, u32[]{:S(2)}, u32[]{:S(2)}) collective-permute-start(f32[4,128]{1,0:T(4,128)S(1)} %get-tuple-element.38), channel_id=1, source_target_pairs={{0,4},{1,5},{2,6},{3,7},{4,0},{5,1},{6,2},{7,3},{8,12},{9,13},{10,... | collective-permute-start | bytes 6152 | tf_op jit(solution)/shard_map/ppermute | solution.py:719
  26.8 11.1 %collective-permute-start.8 = (bf16[6,64,128]{2,1,0:T(8,128)(2,1)S(1)}, bf16[6,64,128]{2,1,0:T(8,128)(2,1)S(1)}, u32[]{:S(2)}, u32[]{:S(2)}) collective-permute-start(bf16[6,64,128]{2,1,0:T(8,128)(2,1)S(1)} %get-tuple-element.53), channel_id=1, source_target_pairs={{0,4},{1,5},{2,6},{3,7},{4,0},{5,1},{6,2},{7,3},{8,12},{9,13},{10,... | collective-permute-start | bytes 294920 | tf_op jit(solution)/shard_map/ppermute | solution.py:719
  30.1 3.8 %collective-permute-start.6 = (f32[2,14,128]{2,1,0:T(8,128)S(1)}, f32[2,14,128]{2,1,0:T(8,128)S(1)}, u32[]{:S(2)}, u32[]{:S(2)}) collective-permute-start(f32[2,14,128]{2,1,0:T(8,128)S(1)} %get-tuple-element.48.sent_ref), channel_id=1, source_target_pairs={{0,4},{1,5},{2,6},{3,7},{4,0},{5,1},{6,2},{7,3},{8,12},{9,13},{10,... | collective-permute-start | bytes 43016 | tf_op jit(solution)/shard_map/ppermute | solution.py:719
  33.9 4.1 %collective-permute-start.7 = (f32[76,128]{1,0:T(8,128)S(1)}, f32[76,128]{1,0:T(8,128)S(1)}, u32[]{:S(2)}, u32[]{:S(2)}) collective-permute-start(f32[76,128]{1,0:T(8,128)S(1)} %shard_map.101), channel_id=1, source_target_pairs={{0,4},{1,5},{2,6},{3,7},{4,0},{5,1},{6,2},{7,3},{8,12},{9,13},{10,... | collective-permute-start | bytes 116744 | tf_op jit(solution)/shard_map/ppermute | solution.py:719
  34.6 9.4 %copy-start.4 = (f32[256,64]{0,1:T(8,128)S(1)}, f32[256,64]{0,1:T(8,128)}, u32[]{:S(2)}) copy-start(f32[256,64]{0,1:T(8,128)} %param.12) | copy-start | bytes 196612
  38.2 5.8 %collective-permute-start.9 = (f32[64,256]{1,0:T(8,128)S(1)}, f32[64,256]{1,0:T(8,128)S(1)}, u32[]{:S(2)}, u32[]{:S(2)}) collective-permute-start(f32[64,256]{1,0:T(8,128)S(1)} %shard_map.102.velocity_ref), channel_id=1, source_target_pairs={{0,8},{1,9},{2,10},{3,11},{4,12},{5,13},{6,14},{7,15},{8,0},{9,1},... | collective-permute-start | bytes 196616 | tf_op jit(solution)/shard_map/ppermute | solution.py:719

commit v6 on v5

--- a/solution.py
+++ b/solution.py
@@ -355,7 +355,7 @@
 
 
 def fold_into(column, value_ref, weight_ref, places):
-    for head in range(HEADS):
+    for head in (head for group in column.groups for head in group):
         lanes = head_lanes(head)
         values = above(*[value_ref[place, lanes] for place in places])
         folded = contract_last(weight_ref[:, lanes], values)
@@ -364,20 +364,24 @@
 
 
 def far_pack_kernel(
-    block_count, block_cols, tile_tok, groups, key_ref, value_ref, weight_ref, guest_ref, *refs
+    block_count, block_cols, tile_tok, group,
+    key_ref, value_ref, weight_ref, guest_ref, far_ref,
 ):
     spot = Spot(block_count, block_cols)
-    for out_ref, group in zip(refs, groups):
-        out_ref[:, : len(group) * HD] = key_ref[:, group.start * HD : group.stop * HD]
+    far_ref[:, : len(group) * HD] = key_ref[:, group.start * HD : group.stop * HD]
     places = [tile_rows(tile, tile_tok) for tile in spot.key_tiles[2:]]
-    fold_into(Column(refs, groups, weight_ref.shape[0]), value_ref, weight_ref, places)
+    fold_into(Column([far_ref], (group,), weight_ref.shape[0]), value_ref, weight_ref, places)
 
 
 def near_pack_kernel(
     block_count, block_cols, tile_tok, group,
-    query_ref, key_ref, value_ref, weight_ref, near_ref, guest_ref,
+    query_ref, key_ref, value_ref, weight_ref, far_key_ref, near_ref, guest_ref, far_ref,
 ):
     spot = Spot(block_count, block_cols)
+    far_pack_kernel(
+        block_count, block_cols, tile_tok, group,
+        far_key_ref, value_ref, weight_ref, None, far_ref,
+    )
     places = [tile_rows(tile, tile_tok) for tile in spot.key_tiles[:2]]
     for number, col in enumerate((spot.near, spot.far)):
         rows = slice(number * tile_tok, (number + 1) * tile_tok)
@@ -619,15 +623,14 @@
     cond = jnp.where(is_cond, own, other)
     uncond = jnp.where(is_cond, other, own)
     blended = uncond + GUIDANCE * (cond - uncond)
-    edge = blended[:, tile_tok : tile_tok + half]
-    rest = jnp.concatenate([blended[:, :tile_tok], blended[:, tile_tok + half :]], axis=1)
-
-    def natural(pair):
-        swapped = jnp.concatenate([pair[:, tile_tok:], pair[:, :tile_tok]], axis=1)
-        return jnp.where(spot.near == 0, pair, swapped)
-
-    edge = natural(edge)
-    rest = natural(rest)
+    left, right = blended[:, :half], blended[:, half:]
+    first = lax.broadcasted_iota(jnp.int32, left.shape, 1) < tile_tok
+    outside = jnp.where(first, left, right)
+    inside = jnp.where(first, right, left)
+    straight = spot.near == 0
+    rolled = pltpu.roll(jnp.where(straight, inside, outside), tile_tok, 1)
+    edge = jnp.where(straight, rolled, inside)
+    rest = jnp.where(straight, outside, rolled)
     moment = jnp.full((1, half), step_ref[0].astype(jnp.float32))
     sigma_now = flow_sigma(moment)
     step_size = flow_sigma(moment + 1.0) - sigma_now
@@ -723,16 +726,19 @@
 
     guests = [sent_over(guest_send, row_pairs)]
     far = kernel_call(
-        functools.partial(far_pack_kernel, *sizes, groups),
+        functools.partial(far_pack_kernel, *sizes, groups[0]),
         (far_keys, value_rows, weight_t, guest_send),
-        [column_type(group) for group in groups],
-    )
-    outer = [sent_over(column, side_pairs, ("groups", "frame")) for column in far]
-    near, guest_send = kernel_call(
+        (column_type(groups[0]),),
+    )
+    side_axes = ("groups", "frame")
+    outer = [sent_over(far[0], side_pairs, side_axes)]
+    near, guest_send, late_far = kernel_call(
         functools.partial(near_pack_kernel, *sizes, groups[1]),
-        (query_rows, key_rows, value_rows, weight_t),
-        (column_type(every[0]), ((half, late * HD), half_type)),
-    )
+        (query_rows, key_rows, value_rows, weight_t, far_keys),
+        (column_type(every[0]), ((half, late * HD), half_type), column_type(groups[1])),
+    )
+    far = [*far, late_far]
+    outer.append(sent_over(late_far, side_pairs, side_axes))
     inner = sent_over(near, mate_pairs)
     guest_bias = sent_over(edge_bias, row_pairs)
     guests.append(sent_over(guest_send, row_pairs))

time: 45.2 us -> 44.3 us (0.980)
  starting transfers between devices: 13 us -> 12.5 us
    ppermute x10, starting transfers between devices: 13 us -> 12.5 us  [sent_over(): return lax.ppermute(value, axes, pairs)]
    unnamed x12 -> x10, local copies, waits for them, and re-layouts: 2.11 us -> 1.91 us
  transfers between devices with their start and end apart: 10 -> 10, of which waited for: 4 -> 4; matrix products, arithmetic and copies ran while one was open for 0% -> 0% of each run, Pallas kernels for 15% -> 14%
where the time goes in v6:
time: 44.3 us; the launch traced here: 44.1 us
  waiting for transfers between devices  18.7 us (42%)
  starting transfers between devices  12.5 us (28%)
  Pallas kernels  9.68 us (22%)
  local copies, waits for them, and re-layouts  1.91 us (4%)
  between operations  1.36 us (3%)
    ppermute x10, waiting for transfers between devices, sent_over(): return lax.ppermute(value, axes, pairs)  18.7 us
    ppermute x10, starting transfers between devices, sent_over(): return lax.ppermute(value, axes, pairs)  12.5 us
    pallas_call x10, Pallas kernels, kernel_call(): pl.pallas_call(body, out_shape=[pltpu.VMEM(shape, dtype) if stay else jax...  9.68 us
    unnamed x10, local copies, waits for them, and re-layouts  1.91 us
  transfers between devices with their start and end apart: 10, of which 4 were waited for; matrix products, arithmetic and copies ran while one was open for 0% of the time, Pallas kernels for 14%

profile of v6, /device:TPU:0, one launch (start us, length us, event | category | flops | bytes accessed | tf_op | source)
XLA Modules:
  0.0 44.1 jit_solution(13195101893320471873)
XLA Ops:
  0.7 1.6 %shard_map.94 = (bf16[128,1792]{1,0:T(8,128)(2,1)S(1)}, f32[4,128]{1,0:T(4,128)S(1)}, bf16[128,2560]{1,0:T(8,128)(2,1)S(1)}, bf16[64,2560]{1,0:T(8,128)(2,1)S(1)}) custom-call(bf16[256,2560]{1,0:T(8,128)(2,1)} %query_ref.9, bf16[256,2560]{1,0:T(8,128)(2,1)} %key_ref.3, s32[4,27]{1,0:T(4,128)} %mask_ref.3, bf16[64,2560]{1,0:T(8,128)(2,1)} %bitcast.6), custom_call_target="tpu_custom_call" | custom-call | tf_op jit(solution)/shard_map/pallas_call | solution.py:655
  2.3 0.2 copy-done
  2.5 0.4 copy-done.1
  2.9 1.3 %copy-done.2 = bf16[256,2560]{1,0:T(8,128)(2,1)S(1)} copy-done((bf16[256,2560]{1,0:T(8,128)(2,1)S(1)}, bf16[256,2560]{1,0:T(8,128)(2,1)}, u32[]{:S(2)}) %copy-start.2) | copy-done | bytes 1310744
  4.2 0.7 %shard_map.95 = (bf16[128,3840]{1,0:T(8,128)(2,1)S(1)}, bf16[128,768]{1,0:T(8,128)(2,1)S(1)}, bf16[128,1152]{1,0:T(8,128)(2,1)S(1)}) custom-call(bf16[256,2560]{1,0:T(8,128)(2,1)S(1)} %copy-done, bf16[256,2560]{1,0:T(8,128)(2,1)S(1)} %copy-done.1, bf16[256,2560]{1,0:T(8,128)(2,1)S(1)} %copy-done.2, bf16[64,2560]{1,0:T(8,128)(2,1)S(1)} %get-tuple-element.29.weight_ref, ...), custom_call_target="tpu_custom_call" | custom-call | tf_op jit(solution)/shard_map/pallas_call | solution.py:655
  4.9 0.6 %collective-permute-start = (bf16[128,3840]{1,0:T(8,128)(2,1)S(1)}, bf16[128,3840]{1,0:T(8,128)(2,1)S(1)}, u32[]{:S(2)}, u32[]{:S(2)}) collective-permute-start(bf16[128,3840]{1,0:T(8,128)(2,1)S(1)} %get-tuple-element.31.refs_0_.near_ref), channel_id=1, source_target_pairs={{0,1},{1,0},{2,3},{3,2},{4,5},{5,4},{6,7},{7,6},{8,9},{9,8},{10,11... | collective-permute-start | bytes 2949128 | tf_op jit(solution)/shard_map/ppermute | solution.py:722
  5.4 0.4 shard_map.96.refs_1_.far_ref
  5.9 2.6 %collective-permute-start.4 = (bf16[128,2688]{1,0:T(8,128)(2,1)S(1)}, bf16[128,2688]{1,0:T(8,128)(2,1)S(1)}, u32[]{:S(2)}, u32[]{:S(2)}) collective-permute-start(bf16[128,2688]{1,0:T(8,128)(2,1)S(1)} %shard_map.96.refs_1_.far_ref), channel_id=1, source_target_pairs={{0,16},{16,0},{1,2},{17,18},{2,1},{18,17},{3,19},{19,3},{4,20},{20... | collective-permute-start | bytes 2064392 | tf_op jit(solution)/shard_map/ppermute | solution.py:722
  8.4 1.6 %collective-permute-start.5 = (bf16[128,1792]{1,0:T(8,128)(2,1)S(1)}, bf16[128,1792]{1,0:T(8,128)(2,1)S(1)}, u32[]{:S(2)}, u32[]{:S(2)}) collective-permute-start(bf16[128,1792]{1,0:T(8,128)(2,1)S(1)} %get-tuple-element.32.guest_ref), channel_id=1, source_target_pairs={{0,4},{1,5},{2,6},{3,7},{4,0},{5,1},{6,2},{7,3},{8,12},{9,13},{10,... | collective-permute-start | bytes 1376264 | tf_op jit(solution)/shard_map/ppermute | solution.py:722
  10.0 0.5 %collective-permute-start.2 = (bf16[128,1152]{1,0:T(8,128)(2,1)S(1)}, bf16[128,1152]{1,0:T(8,128)(2,1)S(1)}, u32[]{:S(2)}, u32[]{:S(2)}) collective-permute-start(bf16[128,1152]{1,0:T(8,128)(2,1)S(1)} %get-tuple-element.33.refs_2_.far_ref), channel_id=1, source_target_pairs={{0,16},{16,0},{1,2},{17,18},{2,1},{18,17},{3,19},{19,3},{4,20},{20... | collective-permute-start | bytes 884744 | tf_op jit(solution)/shard_map/ppermute | solution.py:722
  10.5 0.0 collective-permute-start.3
  10.5 0.0 collective-permute-done.refs_3_.inner_ref
  10.5 2.0 %collective-permute-start.1 = (f32[4,128]{1,0:T(4,128)S(1)}, f32[4,128]{1,0:T(4,128)S(1)}, u32[]{:S(2)}, u32[]{:S(2)}) collective-permute-start(f32[4,128]{1,0:T(4,128)S(1)} %get-tuple-element.36), channel_id=1, source_target_pairs={{0,4},{1,5},{2,6},{3,7},{4,0},{5,1},{6,2},{7,3},{8,12},{9,13},{10,... | collective-permute-start | bytes 6152 | tf_op jit(solution)/shard_map/ppermute | solution.py:722
  12.5 3.1 %shard_map.97 = (f32[20,64,256]{2,1,0:T(8,128)S(1)}, f32[20,256]{1,0:T(8,128)S(1)}, f32[20,256]{1,0:T(8,128)S(1)}, f32[2,128]{1,0:T(2,128)S(1)}) custom-call(s32[4,27]{1,0:T(4,128)S(1)} %copy-done.4, bf16[256,2560]{1,0:T(8,128)(2,1)S(1)} %copy-done, bf16[128,3840]{1,0:T(8,128)(2,1)S(1)} %get-tuple-element.31.refs_0_.near_ref, ...), custom_call_target="tpu_custom_call" | custom-call | tf_op jit(solution)/shard_map/pallas_call | solution.py:655
  15.7 9.5 %collective-permute-done.1.guest_bias_ref = f32[4,128]{1,0:T(4,128)S(1)} collective-permute-done((f32[4,128]{1,0:T(4,128)S(1)}, f32[4,128]{1,0:T(4,128)S(1)}, u32[]{:S(2)}, u32[]{:S(2)}) %collective-permute-start.1) | collective-permute-done | bytes 2080 | tf_op jit(solution)/shard_map/ppermute | solution.py:722
  25.2 0.0 collective-permute-done.3.guest_ref
  25.2 0.0 collective-permute-done.2.outer_ref
  25.2 0.9 %shard_map.98 = (f32[6,64,128]{2,1,0:T(8,128)S(1)}, bf16[6,64,128]{2,1,0:T(8,128)(2,1)S(1)}, f32[6,128]{1,0:T(8,128)S(1)}, f32[6,128]{1,0:T(8,128)S(1)}, f32[6,256]{1,0:T(8,128)S(1)}, /*index=5*/f32[2,6,128]{2,1,0:T(8,128)S(1)}) custom-call(f32[2,128]{1,0:T(2,128)S(1)} %get-tuple-element.35.side_bias_ref, ...), custom_call_target="tpu_custom_call" | custom-call | tf_op jit(solution)/shard_map/pallas_call | solution.py:655
  26.2 1.6 %collective-permute-start.8 = (bf16[6,64,128]{2,1,0:T(8,128)(2,1)S(1)}, bf16[6,64,128]{2,1,0:T(8,128)(2,1)S(1)}, u32[]{:S(2)}, u32[]{:S(2)}) collective-permute-start(bf16[6,64,128]{2,1,0:T(8,128)(2,1)S(1)} %get-tuple-element.51), channel_id=1, source_target_pairs={{0,4},{1,5},{2,6},{3,7},{4,0},{5,1},{6,2},{7,3},{8,12},{9,13},{10,... | collective-permute-start | bytes 294920 | tf_op jit(solution)/shard_map/ppermute | solution.py:722
  27.7 0.0 collective-permute-done.5.guest_ref
  27.7 1.6 %shard_map.99 = (f32[14,64,128]{2,1,0:T(8,128)S(1)}, f32[14,64,128]{2,1,0:T(8,128)S(1)}, f32[14,128]{1,0:T(8,128)S(1)}, f32[14,128]{1,0:T(8,128)S(1)}, f32[14,256]{1,0:T(8,128)S(1)}, /*index=5*/f32[2,14,128]{2,1,0:T(8,128)S(1)}) custom-call(f32[2,128]{1,0:T(2,128)S(1)} %get-tuple-element.35.side_bias_ref, ...), custom_call_target="tpu_custom_call" | custom-call | tf_op jit(solution)/shard_map/pallas_call | solution.py:655
  29.4 0.5 %collective-permute-start.6 = (f32[2,14,128]{2,1,0:T(8,128)S(1)}, f32[2,14,128]{2,1,0:T(8,128)S(1)}, u32[]{:S(2)}, u32[]{:S(2)}) collective-permute-start(f32[2,14,128]{2,1,0:T(8,128)S(1)} %get-tuple-element.46.sent_ref), channel_id=1, source_target_pairs={{0,4},{1,5},{2,6},{3,7},{4,0},{5,1},{6,2},{7,3},{8,12},{9,13},{10,... | collective-permute-start | bytes 43016 | tf_op jit(solution)/shard_map/ppermute | solution.py:722
  29.8 3.3 %collective-permute-done.6.got_ref = f32[2,14,128]{2,1,0:T(8,128)S(1)} collective-permute-done((f32[2,14,128]{2,1,0:T(8,128)S(1)}, f32[2,14,128]{2,1,0:T(8,128)S(1)}, u32[]{:S(2)}, u32[]{:S(2)}) %collective-permute-start.6) | collective-permute-done | bytes 14368 | tf_op jit(solution)/shard_map/ppermute | solution.py:722
  33.1 0.1 shard_map.101
  33.2 0.5 %collective-permute-start.7 = (f32[76,128]{1,0:T(8,128)S(1)}, f32[76,128]{1,0:T(8,128)S(1)}, u32[]{:S(2)}, u32[]{:S(2)}) collective-permute-start(f32[76,128]{1,0:T(8,128)S(1)} %shard_map.101), channel_id=1, source_target_pairs={{0,4},{1,5},{2,6},{3,7},{4,0},{5,1},{6,2},{7,3},{8,12},{9,13},{10,... | collective-permute-start | bytes 116744 | tf_op jit(solution)/shard_map/ppermute | solution.py:722
  33.7 0.2 shard_map.100.velocity_ref
  33.9 0.0 copy-start.3
  33.9 3.3 %collective-permute-done.7.back_ref = f32[76,128]{1,0:T(8,128)S(1)} collective-permute-done((f32[76,128]{1,0:T(8,128)S(1)}, f32[76,128]{1,0:T(8,128)S(1)}, u32[]{:S(2)}, u32[]{:S(2)}) %collective-permute-start.7) | collective-permute-done | bytes 38944 | tf_op jit(solution)/shard_map/ppermute | solution.py:722
  37.3 0.2 shard_map.102.velocity_ref
  37.5 2.7 %collective-permute-start.9 = (f32[64,256]{1,0:T(8,128)S(1)}, f32[64,256]{1,0:T(8,128)S(1)}, u32[]{:S(2)}, u32[]{:S(2)}) collective-permute-start(f32[64,256]{1,0:T(8,128)S(1)} %shard_map.102.velocity_ref), channel_id=1, source_target_pairs={{0,8},{1,9},{2,10},{3,11},{4,12},{5,13},{6,14},{7,15},{8,0},{9,1},... | collective-permute-start | bytes 196616 | tf_op jit(solution)/shard_map/ppermute | solution.py:722
  40.8 2.5 %collective-permute-done.9.partner_ref = f32[64,256]{1,0:T(8,128)S(1)} collective-permute-done((f32[64,256]{1,0:T(8,128)S(1)}, f32[64,256]{1,0:T(8,128)S(1)}, u32[]{:S(2)}, u32[]{:S(2)}) %collective-permute-start.9) | collective-permute-done | bytes 65568 | tf_op jit(solution)/shard_map/ppermute | solution.py:722
  43.3 0.8 %shard_map.103 = (f32[64,256]{1,0:T(8,128)}, f32[64,256]{1,0:T(8,128)}, f32[64,256]{1,0:T(8,128)}) custom-call(s32[1]{0:T(128)S(6)} %copy.10.step_ref, f32[64,256]{1,0:T(8,128)S(1)} %shard_map.102.velocity_ref, f32[64,256]{1,0:T(8,128)S(1)} %collective-permute-done.9.partner_ref, f32[64,256]{1,0:T(8,128)S(1)} %bitcast.5), custom_call_target="tpu_custom_call" | custom-call | tf_op jit(solution)/shard_map/pallas_call | solution.py:655
  (8 shorter events, 0.0 us)
Async XLA Ops:
  0.6 1.8 %copy-start = (bf16[256,2560]{1,0:T(8,128)(2,1)S(1)}, bf16[256,2560]{1,0:T(8,128)(2,1)}, u32[]{:S(2)}) copy-start(bf16[256,2560]{1,0:T(8,128)(2,1)} %query_ref.9) | copy-start | bytes 3932164
  0.6 2.2 %copy-start.1 = (bf16[256,2560]{1,0:T(8,128)(2,1)S(1)}, bf16[256,2560]{1,0:T(8,128)(2,1)}, u32[]{:S(2)}) copy-start(bf16[256,2560]{1,0:T(8,128)(2,1)} %key_ref.3) | copy-start | bytes 3932164
  2.9 1.3 %copy-start.2 = (bf16[256,2560]{1,0:T(8,128)(2,1)S(1)}, bf16[256,2560]{1,0:T(8,128)(2,1)}, u32[]{:S(2)}) copy-start(bf16[256,2560]{1,0:T(8,128)(2,1)} %value_ref.3) | copy-start | bytes 3932164
  4.9 5.7 %collective-permute-start = (bf16[128,3840]{1,0:T(8,128)(2,1)S(1)}, bf16[128,3840]{1,0:T(8,128)(2,1)S(1)}, u32[]{:S(2)}, u32[]{:S(2)}) collective-permute-start(bf16[128,3840]{1,0:T(8,128)(2,1)S(1)} %get-tuple-element.31.refs_0_.near_ref), channel_id=1, source_target_pairs={{0,1},{1,0},{2,3},{3,2},{4,5},{5,4},{6,7},{7,6},{8,9},{9,8},{10,11... | collective-permute-start | bytes 2949128 | tf_op jit(solution)/shard_map/ppermute | solution.py:722
  5.4 7.1 %copy-start.4 = (s32[4,27]{1,0:T(4,128)S(1)}, s32[4,27]{1,0:T(4,128)}, u32[]{:S(2)}) copy-start(s32[4,27]{1,0:T(4,128)} %mask_ref.3) | copy-start | bytes 1300
  5.9 21.9 %collective-permute-start.4 = (bf16[128,2688]{1,0:T(8,128)(2,1)S(1)}, bf16[128,2688]{1,0:T(8,128)(2,1)S(1)}, u32[]{:S(2)}, u32[]{:S(2)}) collective-permute-start(bf16[128,2688]{1,0:T(8,128)(2,1)S(1)} %shard_map.96.refs_1_.far_ref), channel_id=1, source_target_pairs={{0,16},{16,0},{1,2},{17,18},{2,1},{18,17},{3,19},{19,3},{4,20},{20... | collective-permute-start | bytes 2064392 | tf_op jit(solution)/shard_map/ppermute | solution.py:722
  8.4 19.3 %collective-permute-start.5 = (bf16[128,1792]{1,0:T(8,128)(2,1)S(1)}, bf16[128,1792]{1,0:T(8,128)(2,1)S(1)}, u32[]{:S(2)}, u32[]{:S(2)}) collective-permute-start(bf16[128,1792]{1,0:T(8,128)(2,1)S(1)} %get-tuple-element.32.guest_ref), channel_id=1, source_target_pairs={{0,4},{1,5},{2,6},{3,7},{4,0},{5,1},{6,2},{7,3},{8,12},{9,13},{10,... | collective-permute-start | bytes 1376264 | tf_op jit(solution)/shard_map/ppermute | solution.py:722
  10.0 15.3 %collective-permute-start.2 = (bf16[128,1152]{1,0:T(8,128)(2,1)S(1)}, bf16[128,1152]{1,0:T(8,128)(2,1)S(1)}, u32[]{:S(2)}, u32[]{:S(2)}) collective-permute-start(bf16[128,1152]{1,0:T(8,128)(2,1)S(1)} %get-tuple-element.33.refs_2_.far_ref), channel_id=1, source_target_pairs={{0,16},{16,0},{1,2},{17,18},{2,1},{18,17},{3,19},{19,3},{4,20},{20... | collective-permute-start | bytes 884744 | tf_op jit(solution)/shard_map/ppermute | solution.py:722
  10.5 14.7 %collective-permute-start.3 = (bf16[128,768]{1,0:T(8,128)(2,1)S(1)}, bf16[128,768]{1,0:T(8,128)(2,1)S(1)}, u32[]{:S(2)}, u32[]{:S(2)}) collective-permute-start(bf16[128,768]{1,0:T(8,128)(2,1)S(1)} %get-tuple-element.37), channel_id=1, source_target_pairs={{0,4},{1,5},{2,6},{3,7},{4,0},{5,1},{6,2},{7,3},{8,12},{9,13},{10,... | collective-permute-start | bytes 589832 | tf_op jit(solution)/shard_map/ppermute | solution.py:722
  10.5 14.7 %collective-permute-start.1 = (f32[4,128]{1,0:T(4,128)S(1)}, f32[4,128]{1,0:T(4,128)S(1)}, u32[]{:S(2)}, u32[]{:S(2)}) collective-permute-start(f32[4,128]{1,0:T(4,128)S(1)} %get-tuple-element.36), channel_id=1, source_target_pairs={{0,4},{1,5},{2,6},{3,7},{4,0},{5,1},{6,2},{7,3},{8,12},{9,13},{10,... | collective-permute-start | bytes 6152 | tf_op jit(solution)/shard_map/ppermute | solution.py:722
  26.2 11.1 %collective-permute-start.8 = (bf16[6,64,128]{2,1,0:T(8,128)(2,1)S(1)}, bf16[6,64,128]{2,1,0:T(8,128)(2,1)S(1)}, u32[]{:S(2)}, u32[]{:S(2)}) collective-permute-start(bf16[6,64,128]{2,1,0:T(8,128)(2,1)S(1)} %get-tuple-element.51), channel_id=1, source_target_pairs={{0,4},{1,5},{2,6},{3,7},{4,0},{5,1},{6,2},{7,3},{8,12},{9,13},{10,... | collective-permute-start | bytes 294920 | tf_op jit(solution)/shard_map/ppermute | solution.py:722
  29.4 3.8 %collective-permute-start.6 = (f32[2,14,128]{2,1,0:T(8,128)S(1)}, f32[2,14,128]{2,1,0:T(8,128)S(1)}, u32[]{:S(2)}, u32[]{:S(2)}) collective-permute-start(f32[2,14,128]{2,1,0:T(8,128)S(1)} %get-tuple-element.46.sent_ref), channel_id=1, source_target_pairs={{0,4},{1,5},{2,6},{3,7},{4,0},{5,1},{6,2},{7,3},{8,12},{9,13},{10,... | collective-permute-start | bytes 43016 | tf_op jit(solution)/shard_map/ppermute | solution.py:722
  33.2 4.1 %collective-permute-start.7 = (f32[76,128]{1,0:T(8,128)S(1)}, f32[76,128]{1,0:T(8,128)S(1)}, u32[]{:S(2)}, u32[]{:S(2)}) collective-permute-start(f32[76,128]{1,0:T(8,128)S(1)} %shard_map.101), channel_id=1, source_target_pairs={{0,4},{1,5},{2,6},{3,7},{4,0},{5,1},{6,2},{7,3},{8,12},{9,13},{10,... | collective-permute-start | bytes 116744 | tf_op jit(solution)/shard_map/ppermute | solution.py:722
  33.9 9.4 %copy-start.3 = (f32[256,64]{0,1:T(8,128)S(1)}, f32[256,64]{0,1:T(8,128)}, u32[]{:S(2)}) copy-start(f32[256,64]{0,1:T(8,128)} %param.12) | copy-start | bytes 196612
  37.5 5.8 %collective-permute-start.9 = (f32[64,256]{1,0:T(8,128)S(1)}, f32[64,256]{1,0:T(8,128)S(1)}, u32[]{:S(2)}, u32[]{:S(2)}) collective-permute-start(f32[64,256]{1,0:T(8,128)S(1)} %shard_map.102.velocity_ref), channel_id=1, source_target_pairs={{0,8},{1,9},{2,10},{3,11},{4,12},{5,13},{6,14},{7,15},{8,0},{9,1},... | collective-permute-start | bytes 196616 | tf_op jit(solution)/shard_map/ppermute | solution.py:722

commit v7 on v6

--- a/solution.py
+++ b/solution.py
@@ -466,7 +466,7 @@
 
 
 def edge_kernel(
-    block_count, block_cols, tile_tok, group,
+    block_count, block_cols, tile_tok, group, late,
     side_bias_ref, guest_bias_ref,
     query_ref, near_ref, far_ref, inner_ref, outer_ref, guest_ref, own_top_ref, own_sum_ref,
     out_ref, guest_out_ref, side_top_ref, guest_top_ref, log_ref, send_ref,
@@ -517,7 +517,12 @@
             jnp.where(left, inner_column.folded(head), outer_column.folded(head)),
         )
         guest = contract(with_ones(folded), guest_weights[row])
-        guest_out_ref[row] = guest[:channels].astype(guest_out_ref.dtype)
+        if late:
+            share = guest[:channels] / guest[channels : channels + 1]
+            place = slice(row * channels, (row + 1) * channels)
+            guest_out_ref[place] = share.astype(guest_out_ref.dtype)
+        else:
+            guest_out_ref[row] = guest[:channels]
         guest_sum_ref[row : row + 1] = guest[channels : channels + 1]
 
     pipelined(group, score, soften, weigh)
@@ -531,7 +536,16 @@
     log_ref[:, :half] = near_log
     log_ref[:, half:] = far_log
     send_ref[0] = beside(near_log[:, tile_tok:], far_log[:, :tile_tok])
-    send_ref[1] = log_sum(guest_top_ref[...], guest_sum_ref[...])
+    guest_log = log_sum(guest_top_ref[...], guest_sum_ref[...])
+    send_ref[1] = guest_log
+    if late:
+        first = len(group) * channels
+        guest_out_ref[first:] = jnp.zeros_like(guest_out_ref[first:])
+        for number in range(3):
+            part = guest_log.astype(guest_out_ref.dtype)
+            start = first + 16 * number
+            guest_out_ref[start : start + len(group)] = part
+            guest_log = guest_log - part.astype(jnp.float32)
 
 
 def log_sum(top, total):
@@ -553,17 +567,14 @@
 
 
 def guest_blend_kernel(
-    guest_out_ref, guest_top_ref, sent_ref, got_ref, late_top_ref, late_sent_ref, back_ref
+    guest_out_ref, guest_top_ref, sent_ref, got_ref, late_ref, back_ref
 ):
-    heads, channels, _ = guest_out_ref.shape
+    heads, _, _ = guest_out_ref.shape
     share = share_of(guest_top_ref[...], joint(sent_ref[1], got_ref[0]))
     velocity = jnp.zeros(guest_out_ref.shape[1:], jnp.float32)
     for row in range(heads):
         velocity = velocity + share[row : row + 1] * guest_out_ref[row]
-    late = late_top_ref.shape[0]
-    back_ref[:channels] = velocity
-    back_ref[channels : channels + late] = late_sent_ref[1]
-    back_ref[channels + late : channels + 2 * late] = late_top_ref[...]
+    back_ref[...] = velocity.astype(back_ref.dtype)
 
 
 def own_part(tile_tok, group, own_out_ref, side_out_ref, own_top_ref, side_top_ref, whole):
@@ -597,16 +608,22 @@
     channels = own_out_ref.shape[1]
     half = 2 * tile_tok
     late = len(group)
-    guest_log = back_ref[channels : channels + late]
+    first = late * channels
+    guest_log = jnp.zeros((late, half), jnp.float32)
+    for number in range(3):
+        start = first + 16 * number
+        guest_log = guest_log + back_out_ref[start : start + late].astype(jnp.float32)
     whole = joint(log_ref[...], centred(guest_log, NEG, tile_tok))
     velocity = own_part(
         tile_tok, group, own_out_ref, side_out_ref, own_top_ref, side_top_ref, whole
     )
     edge = beside(whole[:, tile_tok:half], whole[:, half : half + tile_tok])
-    share = share_of(back_ref[channels + late : channels + 2 * late], edge)
-    guest = back_ref[:channels]
+    share = jnp.exp2(guest_log - edge)
+    guest = back_ref[...].astype(jnp.float32)
     for row in range(late):
-        guest = guest + share[row : row + 1] * back_out_ref[row].astype(jnp.float32)
+        guest = guest + share[row : row + 1] * back_out_ref[
+            row * channels : (row + 1) * channels
+        ].astype(jnp.float32)
     out_ref[...] = velocity_ref[...] + velocity + centred(guest, 0.0, tile_tok)
 
 
@@ -760,14 +777,17 @@
         group = groups[number]
         heads = len(group)
         return kernel_call(
-            functools.partial(edge_kernel, *sizes, group),
+            functools.partial(edge_kernel, *sizes, group, number > 0),
             (
                 side_bias, guest_bias, query_rows, near, far[number], inner,
                 outer[number], guests[number], own_top, own_sum,
             ),
             (
                 ((heads, channels, half), single),
-                ((heads, channels, half), guest_type),
+                (
+                    (heads * channels + 48, half) if number else (heads, channels, half),
+                    guest_type,
+                ),
                 ((heads, half), single),
                 ((heads, half), single),
                 ((heads, tok_rows), single),
@@ -786,11 +806,11 @@
 
     side_out, guest_out, side_top, guest_top, log, sent = edge(0, single)
     got = sent_over(sent, row_pairs)
-    late_side, late_guest, late_side_top, late_guest_top, late_log, late_sent = edge(1, half_type)
+    late_side, late_guest, late_side_top, _, late_log, late_sent = edge(1, half_type)
     (guest_velocity,) = kernel_call(
         guest_blend_kernel,
-        (guest_out, guest_top, sent, got, late_guest_top, late_sent),
-        (((channels + 2 * late, half), single),),
+        (guest_out, guest_top, sent, got, late_sent),
+        (((channels, half), half_type),),
     )
     back = sent_over(guest_velocity, row_pairs)
     back_out = sent_over(late_guest, row_pairs)

time: 44.3 us -> 44.5 us (level)
  Pallas kernels: 9.68 us -> 10.2 us
    pallas_call x10, Pallas kernels: 9.68 us -> 10.2 us  [kernel_call(): pl.pallas_call(body, out_shape=[pltpu.VMEM(shape, dtype) if stay else jax...]
  transfers between devices with their start and end apart: 10 -> 10, of which waited for: 4 -> 4; matrix products, arithmetic and copies ran while one was open for 0% -> 0% of each run, Pallas kernels for 14% -> 15%
where the time goes in v7:
time: 44.5 us; the launch traced here: 44.4 us
  waiting for transfers between devices  18.4 us (41%)
  starting transfers between devices  12.5 us (28%)
  Pallas kernels  10.2 us (23%)
  local copies, waits for them, and re-layouts  1.91 us (4%)
  between operations  1.36 us (3%)
    ppermute x10, waiting for transfers between devices, sent_over(): return lax.ppermute(value, axes, pairs)  18.4 us
    ppermute x10, starting transfers between devices, sent_over(): return lax.ppermute(value, axes, pairs)  12.5 us
    pallas_call x10, Pallas kernels, kernel_call(): pl.pallas_call(body, out_shape=[pltpu.VMEM(shape, dtype) if stay else jax...  10.2 us
    unnamed x10, local copies, waits for them, and re-layouts  1.91 us
  transfers between devices with their start and end apart: 10, of which 4 were waited for; matrix products, arithmetic and copies ran while one was open for 0% of the time, Pallas kernels for 15%

profile of v7, /device:TPU:0, one launch (start us, length us, event | category | flops | bytes accessed | tf_op | source)
XLA Modules:
  0.0 44.4 jit_solution(18348467371750234920)
XLA Ops:
  0.7 1.6 %shard_map.94 = (bf16[128,1792]{1,0:T(8,128)(2,1)S(1)}, f32[4,128]{1,0:T(4,128)S(1)}, bf16[128,2560]{1,0:T(8,128)(2,1)S(1)}, bf16[64,2560]{1,0:T(8,128)(2,1)S(1)}) custom-call(bf16[256,2560]{1,0:T(8,128)(2,1)} %query_ref.9, bf16[256,2560]{1,0:T(8,128)(2,1)} %key_ref.3, s32[4,27]{1,0:T(4,128)} %mask_ref.3, bf16[64,2560]{1,0:T(8,128)(2,1)} %bitcast.6), custom_call_target="tpu_custom_call" | custom-call | tf_op jit(solution)/shard_map/pallas_call | solution.py:672
  2.3 0.2 copy-done
  2.5 0.4 copy-done.1
  2.9 1.3 %copy-done.2 = bf16[256,2560]{1,0:T(8,128)(2,1)S(1)} copy-done((bf16[256,2560]{1,0:T(8,128)(2,1)S(1)}, bf16[256,2560]{1,0:T(8,128)(2,1)}, u32[]{:S(2)}) %copy-start.2) | copy-done | bytes 1310744
  4.2 0.7 %shard_map.95 = (bf16[128,3840]{1,0:T(8,128)(2,1)S(1)}, bf16[128,768]{1,0:T(8,128)(2,1)S(1)}, bf16[128,1152]{1,0:T(8,128)(2,1)S(1)}) custom-call(bf16[256,2560]{1,0:T(8,128)(2,1)S(1)} %copy-done, bf16[256,2560]{1,0:T(8,128)(2,1)S(1)} %copy-done.1, bf16[256,2560]{1,0:T(8,128)(2,1)S(1)} %copy-done.2, bf16[64,2560]{1,0:T(8,128)(2,1)S(1)} %get-tuple-element.28.weight_ref, ...), custom_call_target="tpu_custom_call" | custom-call | tf_op jit(solution)/shard_map/pallas_call | solution.py:672
  4.9 0.6 %collective-permute-start = (bf16[128,3840]{1,0:T(8,128)(2,1)S(1)}, bf16[128,3840]{1,0:T(8,128)(2,1)S(1)}, u32[]{:S(2)}, u32[]{:S(2)}) collective-permute-start(bf16[128,3840]{1,0:T(8,128)(2,1)S(1)} %get-tuple-element.30.refs_0_.near_ref), channel_id=1, source_target_pairs={{0,1},{1,0},{2,3},{3,2},{4,5},{5,4},{6,7},{7,6},{8,9},{9,8},{10,11... | collective-permute-start | bytes 2949128 | tf_op jit(solution)/shard_map/ppermute | solution.py:739
  5.4 0.4 shard_map.96.refs_1_.far_ref
  5.9 2.6 %collective-permute-start.4 = (bf16[128,2688]{1,0:T(8,128)(2,1)S(1)}, bf16[128,2688]{1,0:T(8,128)(2,1)S(1)}, u32[]{:S(2)}, u32[]{:S(2)}) collective-permute-start(bf16[128,2688]{1,0:T(8,128)(2,1)S(1)} %shard_map.96.refs_1_.far_ref), channel_id=1, source_target_pairs={{0,16},{16,0},{1,2},{17,18},{2,1},{18,17},{3,19},{19,3},{4,20},{20... | collective-permute-start | bytes 2064392 | tf_op jit(solution)/shard_map/ppermute | solution.py:739
  8.4 1.6 %collective-permute-start.5 = (bf16[128,1792]{1,0:T(8,128)(2,1)S(1)}, bf16[128,1792]{1,0:T(8,128)(2,1)S(1)}, u32[]{:S(2)}, u32[]{:S(2)}) collective-permute-start(bf16[128,1792]{1,0:T(8,128)(2,1)S(1)} %get-tuple-element.31.guest_ref), channel_id=1, source_target_pairs={{0,4},{1,5},{2,6},{3,7},{4,0},{5,1},{6,2},{7,3},{8,12},{9,13},{10,... | collective-permute-start | bytes 1376264 | tf_op jit(solution)/shard_map/ppermute | solution.py:739
  10.0 0.5 %collective-permute-start.2 = (bf16[128,1152]{1,0:T(8,128)(2,1)S(1)}, bf16[128,1152]{1,0:T(8,128)(2,1)S(1)}, u32[]{:S(2)}, u32[]{:S(2)}) collective-permute-start(bf16[128,1152]{1,0:T(8,128)(2,1)S(1)} %get-tuple-element.32.refs_2_.far_ref), channel_id=1, source_target_pairs={{0,16},{16,0},{1,2},{17,18},{2,1},{18,17},{3,19},{19,3},{4,20},{20... | collective-permute-start | bytes 884744 | tf_op jit(solution)/shard_map/ppermute | solution.py:739
  10.5 0.0 collective-permute-start.3
  10.5 0.0 collective-permute-done.refs_3_.inner_ref
  10.5 2.0 %collective-permute-start.1 = (f32[4,128]{1,0:T(4,128)S(1)}, f32[4,128]{1,0:T(4,128)S(1)}, u32[]{:S(2)}, u32[]{:S(2)}) collective-permute-start(f32[4,128]{1,0:T(4,128)S(1)} %get-tuple-element.35), channel_id=1, source_target_pairs={{0,4},{1,5},{2,6},{3,7},{4,0},{5,1},{6,2},{7,3},{8,12},{9,13},{10,... | collective-permute-start | bytes 6152 | tf_op jit(solution)/shard_map/ppermute | solution.py:739
  12.5 3.1 %shard_map.97 = (f32[20,64,256]{2,1,0:T(8,128)S(1)}, f32[20,256]{1,0:T(8,128)S(1)}, f32[20,256]{1,0:T(8,128)S(1)}, f32[2,128]{1,0:T(2,128)S(1)}) custom-call(s32[4,27]{1,0:T(4,128)S(1)} %copy-done.4, bf16[256,2560]{1,0:T(8,128)(2,1)S(1)} %copy-done, bf16[128,3840]{1,0:T(8,128)(2,1)S(1)} %get-tuple-element.30.refs_0_.near_ref, ...), custom_call_target="tpu_custom_call" | custom-call | tf_op jit(solution)/shard_map/pallas_call | solution.py:672
  15.7 9.5 %collective-permute-done.1.guest_bias_ref = f32[4,128]{1,0:T(4,128)S(1)} collective-permute-done((f32[4,128]{1,0:T(4,128)S(1)}, f32[4,128]{1,0:T(4,128)S(1)}, u32[]{:S(2)}, u32[]{:S(2)}) %collective-permute-start.1) | collective-permute-done | bytes 2080 | tf_op jit(solution)/shard_map/ppermute | solution.py:739
  25.2 0.0 collective-permute-done.3.guest_ref
  25.2 0.0 collective-permute-done.2.outer_ref
  25.2 1.4 %shard_map.98 = (f32[6,64,128]{2,1,0:T(8,128)S(1)}, bf16[432,128]{1,0:T(8,128)(2,1)S(1)}, f32[6,128]{1,0:T(8,128)S(1)}, f32[6,128]{1,0:T(8,128)}, f32[6,256]{1,0:T(8,128)S(1)}, /*index=5*/f32[2,6,128]{2,1,0:T(8,128)S(1)}) custom-call(f32[2,128]{1,0:T(2,128)S(1)} %get-tuple-element.34.side_bias_ref, f32[4,128]{1,0:T(4,128)S(1)} %collective-permute-done.1.guest_bias_ref, ...), custom_call_target="tpu_custom_call" | custom-call | tf_op jit(solution)/shard_map/pallas_call | solution.py:672
  26.7 1.6 %collective-permute-start.8 = (bf16[432,128]{1,0:T(8,128)(2,1)S(1)}, bf16[432,128]{1,0:T(8,128)(2,1)S(1)}, u32[]{:S(2)}, u32[]{:S(2)}) collective-permute-start(bf16[432,128]{1,0:T(8,128)(2,1)S(1)} %get-tuple-element.49), channel_id=1, source_target_pairs={{0,4},{1,5},{2,6},{3,7},{4,0},{5,1},{6,2},{7,3},{8,12},{9,13},{10,... | collective-permute-start | bytes 331784 | tf_op jit(solution)/shard_map/ppermute | solution.py:739
  28.2 0.0 collective-permute-done.5.guest_ref
  28.2 1.6 %shard_map.99 = (f32[14,64,128]{2,1,0:T(8,128)S(1)}, f32[14,64,128]{2,1,0:T(8,128)S(1)}, f32[14,128]{1,0:T(8,128)S(1)}, f32[14,128]{1,0:T(8,128)S(1)}, f32[14,256]{1,0:T(8,128)S(1)}, /*index=5*/f32[2,14,128]{2,1,0:T(8,128)S(1)}) custom-call(f32[2,128]{1,0:T(2,128)S(1)} %get-tuple-element.34.side_bias_ref, ...), custom_call_target="tpu_custom_call" | custom-call | tf_op jit(solution)/shard_map/pallas_call | solution.py:672
  29.8 0.5 %collective-permute-start.6 = (f32[2,14,128]{2,1,0:T(8,128)S(1)}, f32[2,14,128]{2,1,0:T(8,128)S(1)}, u32[]{:S(2)}, u32[]{:S(2)}) collective-permute-start(f32[2,14,128]{2,1,0:T(8,128)S(1)} %get-tuple-element.45.sent_ref), channel_id=1, source_target_pairs={{0,4},{1,5},{2,6},{3,7},{4,0},{5,1},{6,2},{7,3},{8,12},{9,13},{10,... | collective-permute-start | bytes 43016 | tf_op jit(solution)/shard_map/ppermute | solution.py:739
  30.3 3.3 %collective-permute-done.6.got_ref = f32[2,14,128]{2,1,0:T(8,128)S(1)} collective-permute-done((f32[2,14,128]{2,1,0:T(8,128)S(1)}, f32[2,14,128]{2,1,0:T(8,128)S(1)}, u32[]{:S(2)}, u32[]{:S(2)}) %collective-permute-start.6) | collective-permute-done | bytes 14368 | tf_op jit(solution)/shard_map/ppermute | solution.py:739
  33.6 0.1 shard_map.101
  33.7 0.5 %collective-permute-start.7 = (bf16[64,128]{1,0:T(8,128)(2,1)S(1)}, bf16[64,128]{1,0:T(8,128)(2,1)S(1)}, u32[]{:S(2)}, u32[]{:S(2)}) collective-permute-start(bf16[64,128]{1,0:T(8,128)(2,1)S(1)} %shard_map.101), channel_id=1, source_target_pairs={{0,4},{1,5},{2,6},{3,7},{4,0},{5,1},{6,2},{7,3},{8,12},{9,13},{10,... | collective-permute-start | bytes 49160 | tf_op jit(solution)/shard_map/ppermute | solution.py:739
  34.2 0.2 shard_map.100.velocity_ref
  34.4 0.0 copy-start.3
  34.4 3.1 %collective-permute-done.7.back_ref = bf16[64,128]{1,0:T(8,128)(2,1)S(1)} collective-permute-done((bf16[64,128]{1,0:T(8,128)(2,1)S(1)}, bf16[64,128]{1,0:T(8,128)(2,1)S(1)}, u32[]{:S(2)}, u32[]{:S(2)}) %collective-permute-start.7) | collective-permute-done | bytes 16416 | tf_op jit(solution)/shard_map/ppermute | solution.py:739
  37.5 0.3 shard_map.102.velocity_ref
  37.8 2.7 %collective-permute-start.9 = (f32[64,256]{1,0:T(8,128)S(1)}, f32[64,256]{1,0:T(8,128)S(1)}, u32[]{:S(2)}, u32[]{:S(2)}) collective-permute-start(f32[64,256]{1,0:T(8,128)S(1)} %shard_map.102.velocity_ref), channel_id=1, source_target_pairs={{0,8},{1,9},{2,10},{3,11},{4,12},{5,13},{6,14},{7,15},{8,0},{9,1},... | collective-permute-start | bytes 196616 | tf_op jit(solution)/shard_map/ppermute | solution.py:739
  41.1 2.5 %collective-permute-done.9.partner_ref = f32[64,256]{1,0:T(8,128)S(1)} collective-permute-done((f32[64,256]{1,0:T(8,128)S(1)}, f32[64,256]{1,0:T(8,128)S(1)}, u32[]{:S(2)}, u32[]{:S(2)}) %collective-permute-start.9) | collective-permute-done | bytes 65568 | tf_op jit(solution)/shard_map/ppermute | solution.py:739
  43.6 0.8 %shard_map.103 = (f32[64,256]{1,0:T(8,128)}, f32[64,256]{1,0:T(8,128)}, f32[64,256]{1,0:T(8,128)}) custom-call(s32[1]{0:T(128)S(6)} %copy.10.step_ref, f32[64,256]{1,0:T(8,128)S(1)} %shard_map.102.velocity_ref, f32[64,256]{1,0:T(8,128)S(1)} %collective-permute-done.9.partner_ref, f32[64,256]{1,0:T(8,128)S(1)} %bitcast.5), custom_call_target="tpu_custom_call" | custom-call | tf_op jit(solution)/shard_map/pallas_call | solution.py:672
  (8 shorter events, 0.0 us)
Async XLA Ops:
  0.6 1.8 %copy-start = (bf16[256,2560]{1,0:T(8,128)(2,1)S(1)}, bf16[256,2560]{1,0:T(8,128)(2,1)}, u32[]{:S(2)}) copy-start(bf16[256,2560]{1,0:T(8,128)(2,1)} %query_ref.9) | copy-start | bytes 3932164
  0.6 2.2 %copy-start.1 = (bf16[256,2560]{1,0:T(8,128)(2,1)S(1)}, bf16[256,2560]{1,0:T(8,128)(2,1)}, u32[]{:S(2)}) copy-start(bf16[256,2560]{1,0:T(8,128)(2,1)} %key_ref.3) | copy-start | bytes 3932164
  2.9 1.3 %copy-start.2 = (bf16[256,2560]{1,0:T(8,128)(2,1)S(1)}, bf16[256,2560]{1,0:T(8,128)(2,1)}, u32[]{:S(2)}) copy-start(bf16[256,2560]{1,0:T(8,128)(2,1)} %value_ref.3) | copy-start | bytes 3932164
  4.9 5.7 %collective-permute-start = (bf16[128,3840]{1,0:T(8,128)(2,1)S(1)}, bf16[128,3840]{1,0:T(8,128)(2,1)S(1)}, u32[]{:S(2)}, u32[]{:S(2)}) collective-permute-start(bf16[128,3840]{1,0:T(8,128)(2,1)S(1)} %get-tuple-element.30.refs_0_.near_ref), channel_id=1, source_target_pairs={{0,1},{1,0},{2,3},{3,2},{4,5},{5,4},{6,7},{7,6},{8,9},{9,8},{10,11... | collective-permute-start | bytes 2949128 | tf_op jit(solution)/shard_map/ppermute | solution.py:739
  5.4 7.1 %copy-start.4 = (s32[4,27]{1,0:T(4,128)S(1)}, s32[4,27]{1,0:T(4,128)}, u32[]{:S(2)}) copy-start(s32[4,27]{1,0:T(4,128)} %mask_ref.3) | copy-start | bytes 1300
  5.9 22.4 %collective-permute-start.4 = (bf16[128,2688]{1,0:T(8,128)(2,1)S(1)}, bf16[128,2688]{1,0:T(8,128)(2,1)S(1)}, u32[]{:S(2)}, u32[]{:S(2)}) collective-permute-start(bf16[128,2688]{1,0:T(8,128)(2,1)S(1)} %shard_map.96.refs_1_.far_ref), channel_id=1, source_target_pairs={{0,16},{16,0},{1,2},{17,18},{2,1},{18,17},{3,19},{19,3},{4,20},{20... | collective-permute-start | bytes 2064392 | tf_op jit(solution)/shard_map/ppermute | solution.py:739
  8.4 19.8 %collective-permute-start.5 = (bf16[128,1792]{1,0:T(8,128)(2,1)S(1)}, bf16[128,1792]{1,0:T(8,128)(2,1)S(1)}, u32[]{:S(2)}, u32[]{:S(2)}) collective-permute-start(bf16[128,1792]{1,0:T(8,128)(2,1)S(1)} %get-tuple-element.31.guest_ref), channel_id=1, source_target_pairs={{0,4},{1,5},{2,6},{3,7},{4,0},{5,1},{6,2},{7,3},{8,12},{9,13},{10,... | collective-permute-start | bytes 1376264 | tf_op jit(solution)/shard_map/ppermute | solution.py:739
  10.0 15.3 %collective-permute-start.2 = (bf16[128,1152]{1,0:T(8,128)(2,1)S(1)}, bf16[128,1152]{1,0:T(8,128)(2,1)S(1)}, u32[]{:S(2)}, u32[]{:S(2)}) collective-permute-start(bf16[128,1152]{1,0:T(8,128)(2,1)S(1)} %get-tuple-element.32.refs_2_.far_ref), channel_id=1, source_target_pairs={{0,16},{16,0},{1,2},{17,18},{2,1},{18,17},{3,19},{19,3},{4,20},{20... | collective-permute-start | bytes 884744 | tf_op jit(solution)/shard_map/ppermute | solution.py:739
  10.5 14.7 %collective-permute-start.3 = (bf16[128,768]{1,0:T(8,128)(2,1)S(1)}, bf16[128,768]{1,0:T(8,128)(2,1)S(1)}, u32[]{:S(2)}, u32[]{:S(2)}) collective-permute-start(bf16[128,768]{1,0:T(8,128)(2,1)S(1)} %get-tuple-element.36), channel_id=1, source_target_pairs={{0,4},{1,5},{2,6},{3,7},{4,0},{5,1},{6,2},{7,3},{8,12},{9,13},{10,... | collective-permute-start | bytes 589832 | tf_op jit(solution)/shard_map/ppermute | solution.py:739
  10.5 14.7 %collective-permute-start.1 = (f32[4,128]{1,0:T(4,128)S(1)}, f32[4,128]{1,0:T(4,128)S(1)}, u32[]{:S(2)}, u32[]{:S(2)}) collective-permute-start(f32[4,128]{1,0:T(4,128)S(1)} %get-tuple-element.35), channel_id=1, source_target_pairs={{0,4},{1,5},{2,6},{3,7},{4,0},{5,1},{6,2},{7,3},{8,12},{9,13},{10,... | collective-permute-start | bytes 6152 | tf_op jit(solution)/shard_map/ppermute | solution.py:739
  26.7 10.8 %collective-permute-start.8 = (bf16[432,128]{1,0:T(8,128)(2,1)S(1)}, bf16[432,128]{1,0:T(8,128)(2,1)S(1)}, u32[]{:S(2)}, u32[]{:S(2)}) collective-permute-start(bf16[432,128]{1,0:T(8,128)(2,1)S(1)} %get-tuple-element.49), channel_id=1, source_target_pairs={{0,4},{1,5},{2,6},{3,7},{4,0},{5,1},{6,2},{7,3},{8,12},{9,13},{10,... | collective-permute-start | bytes 331784 | tf_op jit(solution)/shard_map/ppermute | solution.py:739
  29.8 3.8 %collective-permute-start.6 = (f32[2,14,128]{2,1,0:T(8,128)S(1)}, f32[2,14,128]{2,1,0:T(8,128)S(1)}, u32[]{:S(2)}, u32[]{:S(2)}) collective-permute-start(f32[2,14,128]{2,1,0:T(8,128)S(1)} %get-tuple-element.45.sent_ref), channel_id=1, source_target_pairs={{0,4},{1,5},{2,6},{3,7},{4,0},{5,1},{6,2},{7,3},{8,12},{9,13},{10,... | collective-permute-start | bytes 43016 | tf_op jit(solution)/shard_map/ppermute | solution.py:739
  33.7 3.8 %collective-permute-start.7 = (bf16[64,128]{1,0:T(8,128)(2,1)S(1)}, bf16[64,128]{1,0:T(8,128)(2,1)S(1)}, u32[]{:S(2)}, u32[]{:S(2)}) collective-permute-start(bf16[64,128]{1,0:T(8,128)(2,1)S(1)} %shard_map.101), channel_id=1, source_target_pairs={{0,4},{1,5},{2,6},{3,7},{4,0},{5,1},{6,2},{7,3},{8,12},{9,13},{10,... | collective-permute-start | bytes 49160 | tf_op jit(solution)/shard_map/ppermute | solution.py:739
  34.4 9.2 %copy-start.3 = (f32[256,64]{0,1:T(8,128)S(1)}, f32[256,64]{0,1:T(8,128)}, u32[]{:S(2)}) copy-start(f32[256,64]{0,1:T(8,128)} %param.12) | copy-start | bytes 196612
  37.8 5.8 %collective-permute-start.9 = (f32[64,256]{1,0:T(8,128)S(1)}, f32[64,256]{1,0:T(8,128)S(1)}, u32[]{:S(2)}, u32[]{:S(2)}) collective-permute-start(f32[64,256]{1,0:T(8,128)S(1)} %shard_map.102.velocity_ref), channel_id=1, source_target_pairs={{0,8},{1,9},{2,10},{3,11},{4,12},{5,13},{6,14},{7,15},{8,0},{9,1},... | collective-permute-start | bytes 196616 | tf_op jit(solution)/shard_map/ppermute | solution.py:739

commit v8 on v6

--- a/solution.py
+++ b/solution.py
@@ -607,7 +607,14 @@
     guest = back_ref[:channels]
     for row in range(late):
         guest = guest + share[row : row + 1] * back_out_ref[row].astype(jnp.float32)
-    out_ref[...] = velocity_ref[...] + velocity + centred(guest, 0.0, tile_tok)
+    first = lax.broadcasted_iota(jnp.int32, guest.shape, 1) < tile_tok
+    rolled = pltpu.roll(guest, tile_tok, 1)
+    out_ref[:, :half] = (
+        velocity_ref[:, :half] + velocity[:, :half] + jnp.where(first, 0.0, rolled)
+    )
+    out_ref[:, half:] = (
+        velocity_ref[:, half:] + velocity[:, half:] + jnp.where(first, rolled, 0.0)
+    )
 
 
 def update_kernel(

time: 44.3 us -> 44.3 us (level)
  no operation moved by 1% of the time
where the time goes in v8:
time: 44.3 us; the launch traced here: 44.1 us
  waiting for transfers between devices  18.7 us (42%)
  starting transfers between devices  12.5 us (28%)
  Pallas kernels  9.68 us (22%)
  local copies, waits for them, and re-layouts  1.91 us (4%)
  between operations  1.36 us (3%)
    ppermute x10, waiting for transfers between devices, sent_over(): return lax.ppermute(value, axes, pairs)  18.7 us
    ppermute x10, starting transfers between devices, sent_over(): return lax.ppermute(value, axes, pairs)  12.5 us
    pallas_call x10, Pallas kernels, kernel_call(): pl.pallas_call(body, out_shape=[pltpu.VMEM(shape, dtype) if stay else jax...  9.68 us
    unnamed x10, local copies, waits for them, and re-layouts  1.91 us
  transfers between devices with their start and end apart: 10, of which 4 were waited for; matrix products, arithmetic and copies ran while one was open for 0% of the time, Pallas kernels for 14%

profile of v8, /device:TPU:0, one launch (start us, length us, event | category | flops | bytes accessed | tf_op | source)
XLA Modules:
  0.0 44.1 jit_solution(8662470972909977980)
XLA Ops:
  0.7 1.6 %shard_map.94 = (bf16[128,1792]{1,0:T(8,128)(2,1)S(1)}, f32[4,128]{1,0:T(4,128)S(1)}, bf16[128,2560]{1,0:T(8,128)(2,1)S(1)}, bf16[64,2560]{1,0:T(8,128)(2,1)S(1)}) custom-call(bf16[256,2560]{1,0:T(8,128)(2,1)} %query_ref.9, bf16[256,2560]{1,0:T(8,128)(2,1)} %key_ref.3, s32[4,27]{1,0:T(4,128)} %mask_ref.3, bf16[64,2560]{1,0:T(8,128)(2,1)} %bitcast.6), custom_call_target="tpu_custom_call" | custom-call | tf_op jit(solution)/shard_map/pallas_call | solution.py:662
  2.3 0.2 copy-done
  2.5 0.4 copy-done.1
  2.9 1.3 %copy-done.2 = bf16[256,2560]{1,0:T(8,128)(2,1)S(1)} copy-done((bf16[256,2560]{1,0:T(8,128)(2,1)S(1)}, bf16[256,2560]{1,0:T(8,128)(2,1)}, u32[]{:S(2)}) %copy-start.2) | copy-done | bytes 1310744
  4.2 0.7 %shard_map.95 = (bf16[128,3840]{1,0:T(8,128)(2,1)S(1)}, bf16[128,768]{1,0:T(8,128)(2,1)S(1)}, bf16[128,1152]{1,0:T(8,128)(2,1)S(1)}) custom-call(bf16[256,2560]{1,0:T(8,128)(2,1)S(1)} %copy-done, bf16[256,2560]{1,0:T(8,128)(2,1)S(1)} %copy-done.1, bf16[256,2560]{1,0:T(8,128)(2,1)S(1)} %copy-done.2, bf16[64,2560]{1,0:T(8,128)(2,1)S(1)} %get-tuple-element.29.weight_ref, ...), custom_call_target="tpu_custom_call" | custom-call | tf_op jit(solution)/shard_map/pallas_call | solution.py:662
  4.9 0.6 %collective-permute-start = (bf16[128,3840]{1,0:T(8,128)(2,1)S(1)}, bf16[128,3840]{1,0:T(8,128)(2,1)S(1)}, u32[]{:S(2)}, u32[]{:S(2)}) collective-permute-start(bf16[128,3840]{1,0:T(8,128)(2,1)S(1)} %get-tuple-element.31.refs_0_.near_ref), channel_id=1, source_target_pairs={{0,1},{1,0},{2,3},{3,2},{4,5},{5,4},{6,7},{7,6},{8,9},{9,8},{10,11... | collective-permute-start | bytes 2949128 | tf_op jit(solution)/shard_map/ppermute | solution.py:729
  5.4 0.4 shard_map.96.refs_1_.far_ref
  5.9 2.6 %collective-permute-start.4 = (bf16[128,2688]{1,0:T(8,128)(2,1)S(1)}, bf16[128,2688]{1,0:T(8,128)(2,1)S(1)}, u32[]{:S(2)}, u32[]{:S(2)}) collective-permute-start(bf16[128,2688]{1,0:T(8,128)(2,1)S(1)} %shard_map.96.refs_1_.far_ref), channel_id=1, source_target_pairs={{0,16},{16,0},{1,2},{17,18},{2,1},{18,17},{3,19},{19,3},{4,20},{20... | collective-permute-start | bytes 2064392 | tf_op jit(solution)/shard_map/ppermute | solution.py:729
  8.4 1.6 %collective-permute-start.5 = (bf16[128,1792]{1,0:T(8,128)(2,1)S(1)}, bf16[128,1792]{1,0:T(8,128)(2,1)S(1)}, u32[]{:S(2)}, u32[]{:S(2)}) collective-permute-start(bf16[128,1792]{1,0:T(8,128)(2,1)S(1)} %get-tuple-element.32.guest_ref), channel_id=1, source_target_pairs={{0,4},{1,5},{2,6},{3,7},{4,0},{5,1},{6,2},{7,3},{8,12},{9,13},{10,... | collective-permute-start | bytes 1376264 | tf_op jit(solution)/shard_map/ppermute | solution.py:729
  10.0 0.5 %collective-permute-start.2 = (bf16[128,1152]{1,0:T(8,128)(2,1)S(1)}, bf16[128,1152]{1,0:T(8,128)(2,1)S(1)}, u32[]{:S(2)}, u32[]{:S(2)}) collective-permute-start(bf16[128,1152]{1,0:T(8,128)(2,1)S(1)} %get-tuple-element.33.refs_2_.far_ref), channel_id=1, source_target_pairs={{0,16},{16,0},{1,2},{17,18},{2,1},{18,17},{3,19},{19,3},{4,20},{20... | collective-permute-start | bytes 884744 | tf_op jit(solution)/shard_map/ppermute | solution.py:729
  10.5 0.0 collective-permute-start.3
  10.5 0.0 collective-permute-done.refs_3_.inner_ref
  10.5 2.0 %collective-permute-start.1 = (f32[4,128]{1,0:T(4,128)S(1)}, f32[4,128]{1,0:T(4,128)S(1)}, u32[]{:S(2)}, u32[]{:S(2)}) collective-permute-start(f32[4,128]{1,0:T(4,128)S(1)} %get-tuple-element.36), channel_id=1, source_target_pairs={{0,4},{1,5},{2,6},{3,7},{4,0},{5,1},{6,2},{7,3},{8,12},{9,13},{10,... | collective-permute-start | bytes 6152 | tf_op jit(solution)/shard_map/ppermute | solution.py:729
  12.5 3.1 %shard_map.97 = (f32[20,64,256]{2,1,0:T(8,128)S(1)}, f32[20,256]{1,0:T(8,128)S(1)}, f32[20,256]{1,0:T(8,128)S(1)}, f32[2,128]{1,0:T(2,128)S(1)}) custom-call(s32[4,27]{1,0:T(4,128)S(1)} %copy-done.4, bf16[256,2560]{1,0:T(8,128)(2,1)S(1)} %copy-done, bf16[128,3840]{1,0:T(8,128)(2,1)S(1)} %get-tuple-element.31.refs_0_.near_ref, ...), custom_call_target="tpu_custom_call" | custom-call | tf_op jit(solution)/shard_map/pallas_call | solution.py:662
  15.7 9.5 %collective-permute-done.1.guest_bias_ref = f32[4,128]{1,0:T(4,128)S(1)} collective-permute-done((f32[4,128]{1,0:T(4,128)S(1)}, f32[4,128]{1,0:T(4,128)S(1)}, u32[]{:S(2)}, u32[]{:S(2)}) %collective-permute-start.1) | collective-permute-done | bytes 2080 | tf_op jit(solution)/shard_map/ppermute | solution.py:729
  25.2 0.0 collective-permute-done.3.guest_ref
  25.2 0.0 collective-permute-done.2.outer_ref
  25.2 0.9 %shard_map.98 = (f32[6,64,128]{2,1,0:T(8,128)S(1)}, bf16[6,64,128]{2,1,0:T(8,128)(2,1)S(1)}, f32[6,128]{1,0:T(8,128)S(1)}, f32[6,128]{1,0:T(8,128)S(1)}, f32[6,256]{1,0:T(8,128)S(1)}, /*index=5*/f32[2,6,128]{2,1,0:T(8,128)S(1)}) custom-call(f32[2,128]{1,0:T(2,128)S(1)} %get-tuple-element.35.side_bias_ref, ...), custom_call_target="tpu_custom_call" | custom-call | tf_op jit(solution)/shard_map/pallas_call | solution.py:662
  26.2 1.6 %collective-permute-start.8 = (bf16[6,64,128]{2,1,0:T(8,128)(2,1)S(1)}, bf16[6,64,128]{2,1,0:T(8,128)(2,1)S(1)}, u32[]{:S(2)}, u32[]{:S(2)}) collective-permute-start(bf16[6,64,128]{2,1,0:T(8,128)(2,1)S(1)} %get-tuple-element.51), channel_id=1, source_target_pairs={{0,4},{1,5},{2,6},{3,7},{4,0},{5,1},{6,2},{7,3},{8,12},{9,13},{10,... | collective-permute-start | bytes 294920 | tf_op jit(solution)/shard_map/ppermute | solution.py:729
  27.7 0.0 collective-permute-done.5.guest_ref
  27.7 1.6 %shard_map.99 = (f32[14,64,128]{2,1,0:T(8,128)S(1)}, f32[14,64,128]{2,1,0:T(8,128)S(1)}, f32[14,128]{1,0:T(8,128)S(1)}, f32[14,128]{1,0:T(8,128)S(1)}, f32[14,256]{1,0:T(8,128)S(1)}, /*index=5*/f32[2,14,128]{2,1,0:T(8,128)S(1)}) custom-call(f32[2,128]{1,0:T(2,128)S(1)} %get-tuple-element.35.side_bias_ref, ...), custom_call_target="tpu_custom_call" | custom-call | tf_op jit(solution)/shard_map/pallas_call | solution.py:662
  29.4 0.5 %collective-permute-start.6 = (f32[2,14,128]{2,1,0:T(8,128)S(1)}, f32[2,14,128]{2,1,0:T(8,128)S(1)}, u32[]{:S(2)}, u32[]{:S(2)}) collective-permute-start(f32[2,14,128]{2,1,0:T(8,128)S(1)} %get-tuple-element.46.sent_ref), channel_id=1, source_target_pairs={{0,4},{1,5},{2,6},{3,7},{4,0},{5,1},{6,2},{7,3},{8,12},{9,13},{10,... | collective-permute-start | bytes 43016 | tf_op jit(solution)/shard_map/ppermute | solution.py:729
  29.8 3.3 %collective-permute-done.6.got_ref = f32[2,14,128]{2,1,0:T(8,128)S(1)} collective-permute-done((f32[2,14,128]{2,1,0:T(8,128)S(1)}, f32[2,14,128]{2,1,0:T(8,128)S(1)}, u32[]{:S(2)}, u32[]{:S(2)}) %collective-permute-start.6) | collective-permute-done | bytes 14368 | tf_op jit(solution)/shard_map/ppermute | solution.py:729
  33.1 0.1 shard_map.101
  33.2 0.5 %collective-permute-start.7 = (f32[76,128]{1,0:T(8,128)S(1)}, f32[76,128]{1,0:T(8,128)S(1)}, u32[]{:S(2)}, u32[]{:S(2)}) collective-permute-start(f32[76,128]{1,0:T(8,128)S(1)} %shard_map.101), channel_id=1, source_target_pairs={{0,4},{1,5},{2,6},{3,7},{4,0},{5,1},{6,2},{7,3},{8,12},{9,13},{10,... | collective-permute-start | bytes 116744 | tf_op jit(solution)/shard_map/ppermute | solution.py:729
  33.7 0.2 shard_map.100.velocity_ref
  33.9 0.0 copy-start.3
  33.9 3.3 %collective-permute-done.7.back_ref = f32[76,128]{1,0:T(8,128)S(1)} collective-permute-done((f32[76,128]{1,0:T(8,128)S(1)}, f32[76,128]{1,0:T(8,128)S(1)}, u32[]{:S(2)}, u32[]{:S(2)}) %collective-permute-start.7) | collective-permute-done | bytes 38944 | tf_op jit(solution)/shard_map/ppermute | solution.py:729
  37.3 0.2 shard_map.102.velocity_ref
  37.5 2.7 %collective-permute-start.9 = (f32[64,256]{1,0:T(8,128)S(1)}, f32[64,256]{1,0:T(8,128)S(1)}, u32[]{:S(2)}, u32[]{:S(2)}) collective-permute-start(f32[64,256]{1,0:T(8,128)S(1)} %shard_map.102.velocity_ref), channel_id=1, source_target_pairs={{0,8},{1,9},{2,10},{3,11},{4,12},{5,13},{6,14},{7,15},{8,0},{9,1},... | collective-permute-start | bytes 196616 | tf_op jit(solution)/shard_map/ppermute | solution.py:729
  40.8 2.5 %collective-permute-done.9.partner_ref = f32[64,256]{1,0:T(8,128)S(1)} collective-permute-done((f32[64,256]{1,0:T(8,128)S(1)}, f32[64,256]{1,0:T(8,128)S(1)}, u32[]{:S(2)}, u32[]{:S(2)}) %collective-permute-start.9) | collective-permute-done | bytes 65568 | tf_op jit(solution)/shard_map/ppermute | solution.py:729
  43.3 0.8 %shard_map.103 = (f32[64,256]{1,0:T(8,128)}, f32[64,256]{1,0:T(8,128)}, f32[64,256]{1,0:T(8,128)}) custom-call(s32[1]{0:T(128)S(6)} %copy.10.step_ref, f32[64,256]{1,0:T(8,128)S(1)} %shard_map.102.velocity_ref, f32[64,256]{1,0:T(8,128)S(1)} %collective-permute-done.9.partner_ref, f32[64,256]{1,0:T(8,128)S(1)} %bitcast.5), custom_call_target="tpu_custom_call" | custom-call | tf_op jit(solution)/shard_map/pallas_call | solution.py:662
  (8 shorter events, 0.0 us)
Async XLA Ops:
  0.6 1.8 %copy-start = (bf16[256,2560]{1,0:T(8,128)(2,1)S(1)}, bf16[256,2560]{1,0:T(8,128)(2,1)}, u32[]{:S(2)}) copy-start(bf16[256,2560]{1,0:T(8,128)(2,1)} %query_ref.9) | copy-start | bytes 3932164
  0.6 2.2 %copy-start.1 = (bf16[256,2560]{1,0:T(8,128)(2,1)S(1)}, bf16[256,2560]{1,0:T(8,128)(2,1)}, u32[]{:S(2)}) copy-start(bf16[256,2560]{1,0:T(8,128)(2,1)} %key_ref.3) | copy-start | bytes 3932164
  2.9 1.3 %copy-start.2 = (bf16[256,2560]{1,0:T(8,128)(2,1)S(1)}, bf16[256,2560]{1,0:T(8,128)(2,1)}, u32[]{:S(2)}) copy-start(bf16[256,2560]{1,0:T(8,128)(2,1)} %value_ref.3) | copy-start | bytes 3932164
  4.9 5.7 %collective-permute-start = (bf16[128,3840]{1,0:T(8,128)(2,1)S(1)}, bf16[128,3840]{1,0:T(8,128)(2,1)S(1)}, u32[]{:S(2)}, u32[]{:S(2)}) collective-permute-start(bf16[128,3840]{1,0:T(8,128)(2,1)S(1)} %get-tuple-element.31.refs_0_.near_ref), channel_id=1, source_target_pairs={{0,1},{1,0},{2,3},{3,2},{4,5},{5,4},{6,7},{7,6},{8,9},{9,8},{10,11... | collective-permute-start | bytes 2949128 | tf_op jit(solution)/shard_map/ppermute | solution.py:729
  5.4 7.1 %copy-start.4 = (s32[4,27]{1,0:T(4,128)S(1)}, s32[4,27]{1,0:T(4,128)}, u32[]{:S(2)}) copy-start(s32[4,27]{1,0:T(4,128)} %mask_ref.3) | copy-start | bytes 1300
  5.9 21.9 %collective-permute-start.4 = (bf16[128,2688]{1,0:T(8,128)(2,1)S(1)}, bf16[128,2688]{1,0:T(8,128)(2,1)S(1)}, u32[]{:S(2)}, u32[]{:S(2)}) collective-permute-start(bf16[128,2688]{1,0:T(8,128)(2,1)S(1)} %shard_map.96.refs_1_.far_ref), channel_id=1, source_target_pairs={{0,16},{16,0},{1,2},{17,18},{2,1},{18,17},{3,19},{19,3},{4,20},{20... | collective-permute-start | bytes 2064392 | tf_op jit(solution)/shard_map/ppermute | solution.py:729
  8.4 19.3 %collective-permute-start.5 = (bf16[128,1792]{1,0:T(8,128)(2,1)S(1)}, bf16[128,1792]{1,0:T(8,128)(2,1)S(1)}, u32[]{:S(2)}, u32[]{:S(2)}) collective-permute-start(bf16[128,1792]{1,0:T(8,128)(2,1)S(1)} %get-tuple-element.32.guest_ref), channel_id=1, source_target_pairs={{0,4},{1,5},{2,6},{3,7},{4,0},{5,1},{6,2},{7,3},{8,12},{9,13},{10,... | collective-permute-start | bytes 1376264 | tf_op jit(solution)/shard_map/ppermute | solution.py:729
  10.0 15.3 %collective-permute-start.2 = (bf16[128,1152]{1,0:T(8,128)(2,1)S(1)}, bf16[128,1152]{1,0:T(8,128)(2,1)S(1)}, u32[]{:S(2)}, u32[]{:S(2)}) collective-permute-start(bf16[128,1152]{1,0:T(8,128)(2,1)S(1)} %get-tuple-element.33.refs_2_.far_ref), channel_id=1, source_target_pairs={{0,16},{16,0},{1,2},{17,18},{2,1},{18,17},{3,19},{19,3},{4,20},{20... | collective-permute-start | bytes 884744 | tf_op jit(solution)/shard_map/ppermute | solution.py:729
  10.5 14.7 %collective-permute-start.3 = (bf16[128,768]{1,0:T(8,128)(2,1)S(1)}, bf16[128,768]{1,0:T(8,128)(2,1)S(1)}, u32[]{:S(2)}, u32[]{:S(2)}) collective-permute-start(bf16[128,768]{1,0:T(8,128)(2,1)S(1)} %get-tuple-element.37), channel_id=1, source_target_pairs={{0,4},{1,5},{2,6},{3,7},{4,0},{5,1},{6,2},{7,3},{8,12},{9,13},{10,... | collective-permute-start | bytes 589832 | tf_op jit(solution)/shard_map/ppermute | solution.py:729
  10.5 14.7 %collective-permute-start.1 = (f32[4,128]{1,0:T(4,128)S(1)}, f32[4,128]{1,0:T(4,128)S(1)}, u32[]{:S(2)}, u32[]{:S(2)}) collective-permute-start(f32[4,128]{1,0:T(4,128)S(1)} %get-tuple-element.36), channel_id=1, source_target_pairs={{0,4},{1,5},{2,6},{3,7},{4,0},{5,1},{6,2},{7,3},{8,12},{9,13},{10,... | collective-permute-start | bytes 6152 | tf_op jit(solution)/shard_map/ppermute | solution.py:729
  26.2 11.1 %collective-permute-start.8 = (bf16[6,64,128]{2,1,0:T(8,128)(2,1)S(1)}, bf16[6,64,128]{2,1,0:T(8,128)(2,1)S(1)}, u32[]{:S(2)}, u32[]{:S(2)}) collective-permute-start(bf16[6,64,128]{2,1,0:T(8,128)(2,1)S(1)} %get-tuple-element.51), channel_id=1, source_target_pairs={{0,4},{1,5},{2,6},{3,7},{4,0},{5,1},{6,2},{7,3},{8,12},{9,13},{10,... | collective-permute-start | bytes 294920 | tf_op jit(solution)/shard_map/ppermute | solution.py:729
  29.4 3.8 %collective-permute-start.6 = (f32[2,14,128]{2,1,0:T(8,128)S(1)}, f32[2,14,128]{2,1,0:T(8,128)S(1)}, u32[]{:S(2)}, u32[]{:S(2)}) collective-permute-start(f32[2,14,128]{2,1,0:T(8,128)S(1)} %get-tuple-element.46.sent_ref), channel_id=1, source_target_pairs={{0,4},{1,5},{2,6},{3,7},{4,0},{5,1},{6,2},{7,3},{8,12},{9,13},{10,... | collective-permute-start | bytes 43016 | tf_op jit(solution)/shard_map/ppermute | solution.py:729
  33.2 4.1 %collective-permute-start.7 = (f32[76,128]{1,0:T(8,128)S(1)}, f32[76,128]{1,0:T(8,128)S(1)}, u32[]{:S(2)}, u32[]{:S(2)}) collective-permute-start(f32[76,128]{1,0:T(8,128)S(1)} %shard_map.101), channel_id=1, source_target_pairs={{0,4},{1,5},{2,6},{3,7},{4,0},{5,1},{6,2},{7,3},{8,12},{9,13},{10,... | collective-permute-start | bytes 116744 | tf_op jit(solution)/shard_map/ppermute | solution.py:729
  33.9 9.4 %copy-start.3 = (f32[256,64]{0,1:T(8,128)S(1)}, f32[256,64]{0,1:T(8,128)}, u32[]{:S(2)}) copy-start(f32[256,64]{0,1:T(8,128)} %param.12) | copy-start | bytes 196612
  37.5 5.8 %collective-permute-start.9 = (f32[64,256]{1,0:T(8,128)S(1)}, f32[64,256]{1,0:T(8,128)S(1)}, u32[]{:S(2)}, u32[]{:S(2)}) collective-permute-start(f32[64,256]{1,0:T(8,128)S(1)} %shard_map.102.velocity_ref), channel_id=1, source_target_pairs={{0,8},{1,9},{2,10},{3,11},{4,12},{5,13},{6,14},{7,15},{8,0},{9,1},... | collective-permute-start | bytes 196616 | tf_op jit(solution)/shard_map/ppermute | solution.py:729
